TPU v7x, 128 devices: a whole 4x4x4 slice. The times are simulated.
128 devices in a mesh: gx: 8 (over x, core), gy: 16 (over z, y).
Axes of the slice: x: 4, y: 4, z: 4, core: 2. Of those that a mesh axis runs over, the one named last changes fastest.
Arguments:
- blade_state: float32 [5, 8, 524288], P(None, 'gx', 'gy'), may hold values from -6 to 6
- back_state: float32 [5, 128, 8192], P(None, 'gx', 'gy'), may hold values from -6 to 6
- blade_cotangent: float32 [5, 8, 524288], P(None, 'gx', 'gy'), may hold values from -6 to 6
- back_cotangent: float32 [5, 128, 8192], P(None, 'gx', 'gy'), may hold values from -6 to 6
- blade_flux: float32 [3, 5, 5], replicated, may hold values from -3 to 3
- back_flux: float32 [3, 5, 5], replicated, may hold values from -3 to 3
- blade_owner: int32 [2, 131072, 1], P(None, ('gx', 'gy')), may hold values from 0 to 127; in each aligned block of 1024 rows (0 to 1023, 1024 to 2047, ..., all dimensions but the last counted through in order) at most 16 rows name the same one
- back_donor_cell: int32 [2, 262144], P(None, ('gx', 'gy')), may hold values from 32 to 7614, as said below
- back_donor_weight: float32 [2, 8, 262144], P(None, None, ('gx', 'gy')), may hold values from 0 to 1, as said below
- hole_cell: int32 [2, 262144], P(None, ('gx', 'gy')), may hold values from 0 to 8159, as said below
- hole_owner: int32 [2, 262144, 1], P(None, ('gx', 'gy')), may hold values from 0 to 127; in each aligned block of 2048 rows (0 to 2047, 2048 to 4095, ..., all dimensions but the last counted through in order) at most 32 rows name the same one
- blade_donor_cell: int32 [2, 524288], P(None, ('gx', 'gy')), may hold values from 0 to 24190, as said below
- blade_donor_weight: float32 [2, 8, 524288], P(None, None, ('gx', 'gy')), may hold values from 0 to 1, as said below
Outputs:
- blade_adjoint: float32 [5, 8, 524288], P(None, 'gx', 'gy')
- back_adjoint: float32 [5, 128, 8192], P(None, 'gx', 'gy')
Inputs may be any that keep to these rules, and one draw needn't show every extreme that they name: `blade_owner`: in each step, at most 16 rim receivers of one device name the same owner. `hole_owner`: in each step, at most 32 hole receivers of one device name the same owner. `back_donor_cell`: local cell number (x * 8 + y) * 64 + z of the owner's block with x < 15, y < 7 and 32 <= z < 63. `blade_donor_cell`: local cell number (j * 64 + k) * 128 + i of the owner's blade block with j < 3, k < 61 and i < 127. `hole_cell`: in each step the 2048 cells of one device are distinct local cell numbers (x * 8 + y) * 64 + z of that device with z < 32. `back_donor_weight`: trilinear weights: products of three fractions, nonnegative, summing to one over the 8 corners of each slot. `blade_donor_weight`: trilinear weights: products of three fractions, nonnegative, summing to one over the 8 corners of each slot.
All inputs are finite; a program needn't handle non-finite values.
Results may differ from a plain program's by a relative error of at most 0.0003.
Values sent between devices are 32-bit elements; how exact they have to be, the bound alone decides.
No kernel may reach another device: no remote copies, remote signals or barrier semaphores. Data moves between devices by JAX's collectives and lax.ppermute only.
A program may use at most 384 MiB of HBM per device.

v0:
```python
import jax
import jax.numpy as jnp
from jax import lax
from jax.sharding import PartitionSpec as P

WRAP_DEV = 4
WALL_CELLS = 64
CHORD_CELLS = 128
EAST_DEV = 16
NORTH_DEV = 8
VERT_CELLS = 64
HOLE_DEV = 2048
REVERSE_STEPS = 2
RIM_DEV = 1024


exact_mode = lax.Precision.HIGHEST
time_step = 0.2
damping = 0.1


def padded_2(block, sides, width, periodic):
    for axis, dim in sides:
        count = lax.axis_size(axis)
        forward = [(i, i + 1) for i in range(count - 1)]
        if periodic:
            forward.append((count - 1, 0))
        backward = [(target, source) for source, target in forward]
        low = lax.ppermute(
            lax.slice_in_dim(block, block.shape[dim] - width, None, axis=dim), axis, forward
        )
        high = lax.ppermute(lax.slice_in_dim(block, 0, width, axis=dim), axis, backward)
        block = jnp.concatenate([low, block, high], axis=dim)
    return block


def face_slice(padded, axis_pos, shift):
    pieces = [slice(None)] * (padded.ndim - 3)
    for position in range(3):
        if position == axis_pos:
            length = padded.shape[padded.ndim - 3 + position] - 2
            pieces.append(slice(shift, shift + length))
        else:
            pieces.append(slice(1, -1))
    return padded[tuple(pieces)]


def flux_apply(matrices, direction, states):
    linear = jnp.einsum("ce,e...->c...", matrices[direction], states, precision=exact_mode)
    return linear + states[1 + direction] * states


def residual_of(padded, matrices):
    center = face_slice(padded, 0, 1)
    summed = jnp.zeros_like(center)
    for direction in range(3):
        upper_side = face_slice(padded, direction, 2)
        lower_side = face_slice(padded, direction, 0)
        summed = summed + 0.5 * (
            flux_apply(matrices, direction, upper_side)
            - flux_apply(matrices, direction, lower_side)
        )
        summed = summed - damping * (upper_side - 2.0 * center + lower_side)
    return summed


def adjoint_of(states, padded, matrices):
    center = face_slice(padded, 0, 1)
    summed = jnp.zeros_like(center)
    for direction in range(3):
        upper_side = face_slice(padded, direction, 2)
        lower_side = face_slice(padded, direction, 0)
        jump_half = 0.5 * (lower_side - upper_side)
        turned = jnp.einsum("ec,e...->c...", matrices[direction], jump_half, precision=exact_mode)
        turned = turned + states[1 + direction] * jump_half
        contracted = jnp.sum(states * jump_half, axis=0)
        turned = turned.at[1 + direction].add(contracted)
        summed = summed + turned - damping * (upper_side - 2.0 * center + lower_side)
    return summed


def blade_padded(flat_field):
    shaped = flat_field.reshape(5, WRAP_DEV, WALL_CELLS, CHORD_CELLS)
    widened = padded_2(shaped, (("gy", 1),), 1, True)
    return jnp.pad(widened, ((0, 0), (0, 0), (1, 1), (1, 1)))


def back_padded(flat_field):
    shaped = flat_field.reshape(5, EAST_DEV, NORTH_DEV, VERT_CELLS)
    widened = padded_2(shaped, (("gx", 1), ("gy", 2)), 1, False)
    return jnp.pad(widened, ((0, 0), (0, 0), (0, 0), (1, 1)))


def slot_address(owners, capacity, devices):
    count = owners.shape[0]
    owner_marks = (owners[:, None] == jnp.arange(devices, dtype=jnp.int32)[None, :]).astype(
        jnp.bfloat16
    )
    positions = jnp.arange(count, dtype=jnp.int32)
    lower_ones = (positions[:, None] > positions[None, :]).astype(jnp.bfloat16)
    before = jnp.dot(lower_ones, owner_marks, preferred_element_type=jnp.float32)
    rank_list = jnp.sum(before * owner_marks.astype(jnp.float32), axis=1).astype(jnp.int32)
    return owners * capacity + rank_list


def corner_offset(corner, strides):
    return corner // 4 * strides[0] + corner // 2 % 2 * strides[1] + corner % 2 * strides[2]


def corner_stack(values, strides):
    cells = values.shape[1]
    reach = strides[0] + strides[1] + strides[2]
    widened = jnp.pad(values, ((0, 0), (0, reach)))
    shifted = [
        widened[:, corner_offset(corner, strides) : corner_offset(corner, strides) + cells]
        for corner in range(8)
    ]
    return jnp.concatenate(shifted, axis=0).T


def interpolate(values, base_rows, weight_rows, strides):
    picked = corner_stack(values, strides)[base_rows].reshape(base_rows.shape[0], 8, 5)
    return jnp.einsum("sce,cs->es", picked, weight_rows, precision=exact_mode)


def spread(values, base_rows, weight_rows, strides, incoming):
    cells = values.shape[1]
    slots = base_rows.shape[0]
    terms = (weight_rows[:, None, :] * incoming[None, :, :]).reshape(40, slots).T
    gathered = jnp.zeros((cells, 40), jnp.float32).at[base_rows].add(terms)
    gathered = gathered.T.reshape(8, 5, cells)
    for corner in range(8):
        offset = corner_offset(corner, strides)
        values = values + jnp.pad(gathered[corner], ((0, 0), (offset, 0)))[:, :cells]
    return values


def forward_move(rim_values, hole_values):
    first_count = lax.axis_size("gx")
    second_count = lax.axis_size("gy")
    rim_parts, hole_parts = (
        lax.all_to_all(
            rim_values.reshape(5, first_count * second_count, -1),
            ("gx", "gy"),
            split_axis=1,
            concat_axis=1,
            tiled=True,
        ),
        lax.all_to_all(
            hole_values.reshape(5, first_count * second_count, -1),
            ("gx", "gy"),
            split_axis=1,
            concat_axis=1,
            tiled=True,
        ),
    )
    return (rim_parts.reshape(5, -1), hole_parts.reshape(5, -1))


def backward_move(rim_values, hole_values):
    first_count = lax.axis_size("gx")
    second_count = lax.axis_size("gy")
    rim_parts, hole_parts = (
        lax.all_to_all(
            rim_values.reshape(5, first_count * second_count, -1),
            ("gx", "gy"),
            split_axis=1,
            concat_axis=1,
            tiled=True,
        ),
        lax.all_to_all(
            hole_values.reshape(5, first_count * second_count, -1),
            ("gx", "gy"),
            split_axis=1,
            concat_axis=1,
            tiled=True,
        ),
    )
    return (rim_parts.reshape(5, -1), hole_parts.reshape(5, -1))


def fill_fringe(blade_flat, back_flat, step_table, strides_pair):
    rim_address, hole_address, hole_list, back_base, back_weight, blade_base, blade_weight = (
        step_table
    )
    rim_values = interpolate(back_flat, back_base, back_weight, strides_pair[1])
    hole_values = interpolate(blade_flat, blade_base, blade_weight, strides_pair[0])
    rim_arrived, hole_arrived = forward_move(rim_values, hole_values)
    rim_fill = rim_arrived.T[rim_address].T
    shaped = blade_flat.reshape(5, WRAP_DEV, WALL_CELLS, CHORD_CELLS)
    shaped = shaped.at[:, :, WALL_CELLS - 2 :, :].set(rim_fill.reshape(5, WRAP_DEV, 2, CHORD_CELLS))
    back_filled = back_flat.T.at[hole_list].set(hole_arrived.T[hole_address]).T
    return (shaped.reshape(5, -1), back_filled)


def transpose_fringe(blade_flat, back_flat, step_table, strides_pair):
    rim_address, hole_address, hole_list, back_base, back_weight, blade_base, blade_weight = (
        step_table
    )
    shaped = blade_flat.reshape(5, WRAP_DEV, WALL_CELLS, CHORD_CELLS)
    rim_cot = shaped[:, :, WALL_CELLS - 2 :, :].reshape(5, -1)
    blade_kept = shaped.at[:, :, WALL_CELLS - 2 :, :].set(0.0).reshape(5, -1)
    rim_sent = jnp.zeros((2 * RIM_DEV, 5), jnp.float32).at[rim_address].set(rim_cot.T).T
    back_rows = back_flat.T
    hole_sent = (
        jnp.zeros((2 * HOLE_DEV, 5), jnp.float32).at[hole_address].set(back_rows[hole_list]).T
    )
    back_kept = back_rows.at[hole_list].set(0.0).T
    rim_arrived, hole_arrived = backward_move(rim_sent, hole_sent)
    back_out = spread(back_kept, back_base, back_weight, strides_pair[1], rim_arrived)
    blade_out = spread(blade_kept, blade_base, blade_weight, strides_pair[0], hole_arrived)
    return (blade_out, back_out)


def body(
    blade_state,
    back_state,
    blade_cotangent,
    back_cotangent,
    blade_flux,
    back_flux,
    blade_owner,
    back_donor_cell,
    back_donor_weight,
    hole_cell,
    hole_owner,
    blade_donor_cell,
    blade_donor_weight,
):
    devices = lax.axis_size("gx") * lax.axis_size("gy")
    rim_capacity = 2 * RIM_DEV // devices
    hole_capacity = 2 * HOLE_DEV // devices
    strides_pair = (
        (WALL_CELLS * CHORD_CELLS, CHORD_CELLS, 1),
        (NORTH_DEV * VERT_CELLS, VERT_CELLS, 1),
    )
    tables = []
    for step_index in range(REVERSE_STEPS):
        tables.append(
            (
                slot_address(blade_owner[step_index, :, 0], rim_capacity, devices),
                slot_address(hole_owner[step_index, :, 0], hole_capacity, devices),
                hole_cell[step_index],
                back_donor_cell[step_index],
                back_donor_weight[step_index],
                blade_donor_cell[step_index],
                blade_donor_weight[step_index],
            )
        )
    blade_shape = (5, WRAP_DEV, WALL_CELLS, CHORD_CELLS)
    back_shape = (5, EAST_DEV, NORTH_DEV, VERT_CELLS)
    blade_first, back_first = fill_fringe(
        blade_state[:, 0], back_state.reshape(5, -1), tables[0], strides_pair
    )
    blade_next = blade_first - time_step * residual_of(
        blade_padded(blade_first), blade_flux
    ).reshape(5, -1)
    back_next = back_first - time_step * residual_of(back_padded(back_first), back_flux).reshape(
        5, -1
    )
    blade_second, back_second = fill_fringe(blade_next, back_next, tables[1], strides_pair)
    blade_cot = blade_cotangent[:, 0]
    back_cot = back_cotangent.reshape(5, -1)
    blade_mu = blade_cot - time_step * adjoint_of(
        blade_second.reshape(blade_shape), blade_padded(blade_cot), blade_flux
    ).reshape(5, -1)
    back_mu = back_cot - time_step * adjoint_of(
        back_second.reshape(back_shape), back_padded(back_cot), back_flux
    ).reshape(5, -1)
    blade_mid, back_mid = transpose_fringe(blade_mu, back_mu, tables[1], strides_pair)
    blade_mu = blade_mid - time_step * adjoint_of(
        blade_first.reshape(blade_shape), blade_padded(blade_mid), blade_flux
    ).reshape(5, -1)
    back_mu = back_mid - time_step * adjoint_of(
        back_first.reshape(back_shape), back_padded(back_mid), back_flux
    ).reshape(5, -1)
    blade_last, back_last = transpose_fringe(blade_mu, back_mu, tables[0], strides_pair)
    return (blade_last.reshape(blade_state.shape), back_last.reshape(back_state.shape))


def solution(mesh):
    return jax.shard_map(
        body,
        mesh=mesh,
        in_specs=(
            P(None, "gx", "gy"),
            P(None, "gx", "gy"),
            P(None, "gx", "gy"),
            P(None, "gx", "gy"),
            P(),
            P(),
            P(None, ("gx", "gy"), None),
            P(None, ("gx", "gy")),
            P(None, None, ("gx", "gy")),
            P(None, ("gx", "gy")),
            P(None, ("gx", "gy"), None),
            P(None, ("gx", "gy")),
            P(None, None, ("gx", "gy")),
        ),
        out_specs=(P(None, "gx", "gy"), P(None, "gx", "gy")),
        check_vma=False,
    )
```

profile of v0, /device:TPU:1, one launch (start us, length us, event | category | flops | bytes accessed | tf_op | source)
XLA Modules:
  0.0 1152.9 jit_solution(189182811744353135)
XLA Ops:
  23.1 52.3 %concatenate.133 = f32[40,32768]{1,0:T(8,128)} concatenate(f32[5,32768]{1,0:T(8,128)S(1)} %bitcast.485, f32[5,32768]{1,0:T(8,128)} %get-tuple-element.299, f32[5,32768]{1,0:T(8,128)} %get-tuple-element.294, f32[5,32768]{1,0:T(8,128)} %get-tuple-element.295, f32[5,32768]{1,0:T(8,128)} %get-tuple-element.296, f32[5,32768]{1,0:T(8,128)} %get-tuple-element.297, ...), dimensions={0} | concatenate | bytes 10485760 | tf_op jit(solution)/shard_map/concatenate | solution.py:118
  75.5 11.0 copy.590
  86.5 19.8 %gather_fusion.2 = f32[4096,40]{1,0:T(8,128)} fusion(f32[32768,40]{1,0:T(8,128)} %bitcast.463, s32[4096]{0:T(1024)S(1)} %copy-done.38), kind=kCustom, calls=%fused_computation.2 | custom fusion | bytes 1327104 | tf_op jit(solution)/shard_map/gather | solution.py:122
  110.1 6.2 all-to-all-start.1
  129.3 20.2 %pad_slice_fusion.28 = (f32[5,8192]{0,1:T(8,128)}, f32[5,8192]{0,1:T(8,128)}, f32[5,8192]{0,1:T(8,128)}, f32[5,8192]{0,1:T(8,128)}, f32[5,8192]{0,1:T(8,128)}, /*index=5*/f32[5,8192]{0,1:T(8,128)}, f32[5,8192]{0,1:T(8,128)}) fusion(f32[5,8192]{0,1:T(8,128)} %bitcast.455), kind=kLoop, calls=%fused_computation.104 | loop fusion | bytes 1310720 | tf_op jit(solution)/shard_map/slice | solution.py:115
  150.2 21.2 %concatenate.129 = f32[40,8192]{0,1:T(8,128)} concatenate(f32[5,8192]{0,1:T(8,128)} %bitcast.456, f32[5,8192]{0,1:T(8,128)} %get-tuple-element.267, f32[5,8192]{0,1:T(8,128)} %get-tuple-element.262, f32[5,8192]{0,1:T(8,128)} %get-tuple-element.263, f32[5,8192]{0,1:T(8,128)} %get-tuple-element.264, f32[5,8192]{0,1:T(8,128)} %get-tuple-element.265, f32[5,8192]{0,1:T(8,128)} %get-tuple-element.266, ...), dimensions={0} | concatenate | bytes 2621440 | tf_op jit(solution)/shard_map/concatenate | solution.py:118
  171.3 7.7 gather_fusion
  193.1 12.5 %all-to-all-start = ((f32[5,128,16]{2,0,1:T(8,128)}), f32[5,128,16]{2,0,1:T(8,128)}, u32[]{:S(2)}, u32[]{:S(2)}) async-start(f32[5,128,16]{2,0,1:T(8,128)} %copy.583), calls=%async_computation | async-start | bytes 1048576 | tf_op jit(solution)/shard_map/all_to_all | solution.py:142
  210.3 21.3 %scatter_custom_fusion = f32[8192,5]{1,0:T(8,128)} fusion(f32[8192,5]{1,0:T(8,128)} %bitcast.457, s32[2048]{0:T(1024)S(1)} %bitcast.555, f32[4096,5]{1,0:T(8,128)} %bitcast.500, s32[2048]{0:T(1024)S(1)} %get-tuple-element.351), kind=kCustom, calls=%fused_computation.257 | custom fusion | bytes 163840 | tf_op jit(solution)/shard_map/scatter | solution.py:192
  270.0 6.0 bitcast_subtract_fusion.2
  276.0 20.2 %pad_slice_fusion.21 = (f32[5,8192]{0,1:T(8,128)}, f32[5,8192]{0,1:T(8,128)}, f32[5,8192]{0,1:T(8,128)}, f32[5,8192]{0,1:T(8,128)}, f32[5,8192]{0,1:T(8,128)}, /*index=5*/f32[5,8192]{0,1:T(8,128)}, f32[5,8192]{0,1:T(8,128)}) fusion(f32[5,8192]{0,1:T(8,128)} %bitcast_subtract_fusion.2), kind=kLoop, calls=%fused_computation.97 | loop fusion | bytes 1310720 | tf_op jit(solution)/shard_map/slice | solution.py:115
  296.2 21.2 %concatenate.140 = f32[40,8192]{0,1:T(8,128)} concatenate(f32[5,8192]{0,1:T(8,128)} %bitcast_subtract_fusion.2, f32[5,8192]{0,1:T(8,128)} %get-tuple-element.260, f32[5,8192]{0,1:T(8,128)} %get-tuple-element.255, f32[5,8192]{0,1:T(8,128)} %get-tuple-element.256, f32[5,8192]{0,1:T(8,128)} %get-tuple-element.257, f32[5,8192]{0,1:T(8,128)} %get-tuple-element.258, ...), dimensions={0} | concatenate | bytes 2621440 | tf_op jit(solution)/shard_map/concatenate | solution.py:118
  317.3 10.5 gather_fusion.3
  337.4 13.5 %all-to-all-start.2 = ((f32[5,128,16]{2,0,1:T(8,128)}), f32[5,128,16]{2,0,1:T(8,128)}, u32[]{:S(2)}, u32[]{:S(2)}) async-start(f32[5,128,16]{2,0,1:T(8,128)} %copy.607), calls=%async_computation.2 | async-start | bytes 1048576 | tf_op jit(solution)/shard_map/all_to_all | solution.py:142
  357.2 7.3 all-to-all-done.2
  367.4 5.7 gather_fusion.4
  397.5 54.1 %concatenate.144 = f32[40,32768]{1,0:T(8,128)} concatenate(f32[5,32768]{1,0:T(8,128)} %bitcast.483, f32[5,32768]{1,0:T(8,128)} %get-tuple-element.287, f32[5,32768]{1,0:T(8,128)} %get-tuple-element.282, f32[5,32768]{1,0:T(8,128)} %get-tuple-element.283, f32[5,32768]{1,0:T(8,128)} %get-tuple-element.284, f32[5,32768]{1,0:T(8,128)} %get-tuple-element.285, ...), dimensions={0} | concatenate | bytes 10485760 | tf_op jit(solution)/shard_map/concatenate | solution.py:118
  451.6 11.0 copy.622
  462.6 19.8 %gather_fusion.5 = f32[4096,40]{1,0:T(8,128)} fusion(f32[32768,40]{1,0:T(8,128)} %bitcast.464, s32[4096]{0:T(1024)S(1)} %copy-done.37), kind=kCustom, calls=%fused_computation.6 | custom fusion | bytes 1327104 | tf_op jit(solution)/shard_map/gather | solution.py:122
  488.7 5.3 fusion.49
  518.4 5.8 multiply_subtract_fusion
  538.8 11.9 %all-to-all-done.5 = f32[5,128,16]{2,0,1:T(8,128)S(1)} async-done(((f32[5,128,16]{2,0,1:T(8,128)}), f32[5,128,16]{2,0,1:T(8,128)S(1)}, u32[]{:S(2)}, u32[]{:S(2)}) %all-to-all-start.5) | async-done | bytes 40992 | tf_op jit(solution)/shard_map/all_to_all | solution.py:164
  555.4 13.7 %scatter_custom_fusion.6 = f32[8192,40]{1,0:T(8,128)} fusion(s32[2048]{0:T(1024)} %bitcast.565, f32[2048,40]{1,0:T(8,128)S(1)} %copy.655, f32[]{:T(128)} %constant.374.clone.1), kind=kCustom, calls=%fused_computation.124 | custom fusion | flops 81920 | bytes 1311232 | tf_op jit(solution)/shard_map/scatter-add | solution.py:130
  569.1 24.0 %fusion.236 = (f32[5,8192]{0,1:T(8,128)}, f32[5,8192]{0,1:T(8,128)}, f32[5,8192]{0,1:T(8,128)}, f32[5,8192]{0,1:T(8,128)}, f32[5,8192]{0,1:T(8,128)}, /*index=5*/f32[5,8192]{0,1:T(8,128)}, f32[5,8192]{0,1:T(8,128)}) fusion(f32[40,8192]{0,1:T(8,128)} %bitcast.451), kind=kLoop, calls=%fused_computation.505 | loop fusion | bytes 2293760 | tf_op jit(solution)/shard_map/slice | solution.py:134
  596.4 21.4 %scatter_custom_fusion.1 = f32[8192,5]{1,0:T(8,128)} fusion(f32[8192,5]{1,0:T(8,128)} %bitcast.460, s32[2048]{0:T(1024)} %bitcast.560, f32[4096,5]{1,0:T(8,128)} %bitcast.499, s32[2048]{0:T(1024)} %get-tuple-element.350), kind=kCustom, calls=%fused_computation.255 | custom fusion | bytes 163840 | tf_op jit(solution)/shard_map/scatter | solution.py:192
  617.8 11.7 %fusion.33 = (f32[8192]{0:T(1024)S(1)}, f32[8192]{0:T(1024)S(1)}, f32[8192]{0:T(1024)S(1)}) fusion(f32[5,8192]{0,1:T(8,128)} %bitcast.461), kind=kLoop, calls=%fused_computation.90 | loop fusion | flops 24576 | bytes 196608 | tf_op jit(solution)/shard_map/mul | solution.py:75
  655.8 6.0 bitcast_subtract_fusion.1
  661.8 19.0 %scatter_custom_fusion.2 = f32[4096,5]{1,0:T(8,128)} fusion(s32[2048]{0:T(1024)} %bitcast.563, f32[8192,5]{1,0:T(8,128)} %bitcast.479, s32[2048]{0:T(1024)} %get-tuple-element.353, f32[]{:T(128)} %constant.374.clone.1), kind=kCustom, calls=%fused_computation.253 | custom fusion | bytes 82432 | tf_op jit(solution)/shard_map/scatter | solution.py:206
  680.8 10.0 scatter_custom_fusion.4
  690.8 15.4 %fusion.20 = f32[5,8192]{0,1:T(8,128)} fusion(f32[5,8192]{0,1:T(8,128)} %get-tuple-element.253, f32[5,8192]{0,1:T(8,128)} %get-tuple-element.252, f32[5,8192]{0,1:T(8,128)} %get-tuple-element.251, f32[5,8192]{0,1:T(8,128)} %get-tuple-element.250, f32[5,8192]{0,1:T(8,128)} %get-tuple-element.249, f32[5,8192]{0,1:T(8,128)} %get-tuple-element.248, ...), kind=kLoop, calls=%fused_computation.69 | loop fusion | flops 327680 | bytes 1638400 | tf_op jit(solution)/shard_map/add | solution.py:134
  714.7 11.6 %fusion.30 = (f32[8192]{0:T(1024)S(1)}, f32[8192]{0:T(1024)S(1)}, f32[8192]{0:T(1024)S(1)}) fusion(f32[5,8192]{0,1:T(8,128)} %bitcast.459), kind=kLoop, calls=%fused_computation.83 | loop fusion | flops 24576 | bytes 196608 | tf_op jit(solution)/shard_map/mul | solution.py:75
  729.9 10.0 all-to-all-start.4
  759.9 6.0 bitcast_subtract_fusion
  765.9 17.8 %scatter_custom_fusion.7 = f32[4096,5]{1,0:T(8,128)S(1)} fusion(s32[2048]{0:T(1024)} %bitcast.558, f32[8192,5]{1,0:T(8,128)} %bitcast.477, s32[2048]{0:T(1024)} %get-tuple-element.352, f32[]{:T(128)} %constant.374.clone.1), kind=kCustom, calls=%fused_computation.251 | custom fusion | bytes 82432 | tf_op jit(solution)/shard_map/scatter | solution.py:206
  783.6 9.9 scatter_custom_fusion.9
  795.2 12.3 %all-to-all-start.6 = ((f32[128,1,160]{2,1,0:T(1,128)}), f32[128,1,160]{2,1,0:T(1,128)S(1)}, u32[]{:S(2)}, u32[]{:S(2)}) async-start(f32[128,1,160]{2,1,0:T(1,128)} %reshape.1382), calls=%async_computation.6 | async-start | bytes 262144 | tf_op jit(solution)/shard_map/all_to_all | solution.py:171
  811.1 29.4 %scatter_custom_fusion.3 = f32[32768,40]{1,0:T(8,128)} fusion(s32[4096]{0:T(1024)} %bitcast.547, f32[4096,40]{1,0:T(8,128)} %copy.639, f32[]{:T(128)} %constant.374.clone.1), kind=kCustom, calls=%fused_computation.43 | custom fusion | flops 163840 | bytes 5243392 | tf_op jit(solution)/shard_map/scatter-add | solution.py:130
  840.5 11.7 %copy.640 = f32[32768,40]{0,1:T(8,128)} copy(f32[32768,40]{1,0:T(8,128)} %scatter_custom_fusion.3) | data formatting | bytes 10485760 | tf_op jit(solution)/shard_map/scatter-add | solution.py:130
  869.7 29.5 %scatter_custom_fusion.8 = f32[32768,40]{1,0:T(8,128)} fusion(s32[4096]{0:T(1024)} %bitcast.545, f32[4096,40]{1,0:T(8,128)} %copy.674, f32[]{:T(128)} %constant.374.clone.1), kind=kCustom, calls=%fused_computation.41 | custom fusion | flops 163840 | bytes 5243392 | tf_op jit(solution)/shard_map/scatter-add | solution.py:130
  899.3 80.7 %fusion.233 = (f32[5,32768]{0,1:T(8,128)}, f32[5,32768]{0,1:T(8,128)}, f32[5,32768]{0,1:T(8,128)}, f32[5,32768]{0,1:T(8,128)}, f32[5,32768]{0,1:T(8,128)}, /*index=5*/f32[5,32768]{0,1:T(8,128)}, f32[5,32768]{0,1:T(8,128)}) fusion(f32[40,32768]{0,1:T(8,128)} %bitcast.449), kind=kLoop, calls=%fused_computation.502 | loop fusion | bytes 9175040 | tf_op jit(solution)/shard_map/slice | solution.py:134
  986.5 5.4 fusion.46
  1018.3 6.6 all-to-all-start.7
  1024.9 8.7 copy.651
  1033.6 50.7 %fusion.7 = f32[5,1,32768]{0,2,1:T(8,128)} fusion(f32[5,32768]{0,1:T(8,128)} %get-tuple-element.232, f32[5,32768]{0,1:T(8,128)} %get-tuple-element.231, f32[5,32768]{0,1:T(8,128)} %get-tuple-element.230, f32[5,32768]{0,1:T(8,128)} %get-tuple-element.229, f32[5,32768]{0,1:T(8,128)} %get-tuple-element.228, f32[5,32768]{0,1:T(8,128)} %get-tuple-element.227, ...), kind=kLoop, calls=%fused_computation.36 | loop fusion | flops 1310720 | bytes 6553600 | tf_op jit(solution)/shard_map/reshape | solution.py:278
  1084.3 10.8 copy.679
  1095.8 13.7 %scatter_custom_fusion.11 = f32[8192,40]{1,0:T(8,128)} fusion(s32[2048]{0:T(1024)} %bitcast.553, f32[2048,40]{1,0:T(8,128)S(1)} %copy.678, f32[]{:T(128)} %constant.374.clone.1), kind=kCustom, calls=%fused_computation.122 | custom fusion | flops 81920 | bytes 1311232 | tf_op jit(solution)/shard_map/scatter-add | solution.py:130
  1109.5 24.0 %fusion.235 = (f32[5,8192]{0,1:T(8,128)}, f32[5,8192]{0,1:T(8,128)}, f32[5,8192]{0,1:T(8,128)}, f32[5,8192]{0,1:T(8,128)}, f32[5,8192]{0,1:T(8,128)}, /*index=5*/f32[5,8192]{0,1:T(8,128)}, f32[5,8192]{0,1:T(8,128)}) fusion(f32[40,8192]{0,1:T(8,128)} %bitcast.453), kind=kLoop, calls=%fused_computation.504 | loop fusion | bytes 2293760 | tf_op jit(solution)/shard_map/slice | solution.py:134
  1133.6 15.4 %fusion.27 = f32[5,8192]{0,1:T(8,128)} fusion(f32[5,8192]{0,1:T(8,128)} %get-tuple-element.246, f32[5,8192]{0,1:T(8,128)} %get-tuple-element.245, f32[5,8192]{0,1:T(8,128)} %get-tuple-element.244, f32[5,8192]{0,1:T(8,128)} %get-tuple-element.243, f32[5,8192]{0,1:T(8,128)} %get-tuple-element.242, f32[5,8192]{0,1:T(8,128)} %get-tuple-element.241, ...), kind=kLoop, calls=%fused_computation.76 | loop fusion | flops 327680 | bytes 1638400 | tf_op jit(solution)/shard_map/add | solution.py:134
  (370 shorter events, 310.2 us)
Async XLA Ops:
  0.6 17.0 %copy-start.45 = (s32[2,4096]{1,0:T(2,128)S(1)}, s32[2,4096]{1,0:T(2,128)}, u32[]{:S(2)}) copy-start(s32[2,4096]{1,0:T(2,128)} %param.56) | copy-start | bytes 98308
  0.6 17.7 %copy-start.24 = (f32[2,8,4096]{2,1,0:T(8,128)S(1)}, f32[2,8,4096]{2,1,0:T(8,128)}, u32[]{:S(2)}) copy-start(f32[2,8,4096]{2,1,0:T(8,128)} %param.57) | copy-start | bytes 786436
  0.6 18.5 %copy-start.11 = (f32[5,1,32768]{2,1,0:T(1,128)S(1)}, f32[5,1,32768]{2,1,0:T(1,128)}, u32[]{:S(2)}) copy-start(f32[5,1,32768]{2,1,0:T(1,128)} %param.45) | copy-start | bytes 1966084
  2.7 184.9 %collective-permute-start.9 = (f32[5,1,8,64]{3,0,2,1:T(8,128)}, f32[5,1,8,64]{3,0,2,1:T(8,128)S(1)}, u32[]{:S(2)}, u32[]{:S(2)}) collective-permute-start(f32[5,1,8,64]{3,0,2,1:T(8,128)} %get-tuple-element.318), channel_id=1, source_target_pairs={{16,0},{32,16},{48,32},{64,48},{80,64},{96,80},{112,96},{17,1},{33... | collective-permute-start | bytes 30728 | tf_op jit(solution)/shard_map/ppermute | solution.py:32
  5.9 180.7 %collective-permute-start.8 = (f32[5,1,8,64]{3,0,2,1:T(8,128)}, f32[5,1,8,64]{3,0,2,1:T(8,128)}, u32[]{:S(2)}, u32[]{:S(2)}) collective-permute-start(f32[5,1,8,64]{3,0,2,1:T(8,128)} %get-tuple-element.319), channel_id=1, source_target_pairs={{0,16},{16,32},{32,48},{48,64},{64,80},{80,96},{96,112},{1,17},{17... | collective-permute-start | bytes 30728 | tf_op jit(solution)/shard_map/ppermute | solution.py:29
  11.4 362.9 %collective-permute-start = (f32[5,1,64,128]{3,0,2,1:T(8,128)}, f32[5,1,64,128]{3,0,2,1:T(8,128)}, u32[]{:S(2)}, u32[]{:S(2)}) collective-permute-start(f32[5,1,64,128]{3,0,2,1:T(8,128)} %get-tuple-element.291), channel_id=1, source_target_pairs={{0,1},{1,2},{2,3},{3,4},{4,5},{5,6},{6,7},{7,8},{8,9},{9,10},{10,1... | collective-permute-start | bytes 491528 | tf_op jit(solution)/shard_map/ppermute | solution.py:29
  12.7 361.6 %collective-permute-start.1 = (f32[5,1,64,128]{3,0,2,1:T(8,128)}, f32[5,1,64,128]{3,0,2,1:T(8,128)}, u32[]{:S(2)}, u32[]{:S(2)}) collective-permute-start(f32[5,1,64,128]{3,0,2,1:T(8,128)} %get-tuple-element.292), channel_id=1, source_target_pairs={{1,0},{2,1},{3,2},{4,3},{5,4},{6,5},{7,6},{8,7},{9,8},{10,9},{11,1... | collective-permute-start | bytes 491528 | tf_op jit(solution)/shard_map/ppermute | solution.py:32
  17.7 107.6 %copy-start.36 = (s32[4096,1]{0,1:T(1,128)}, s32[4096,1]{0,1:T(1,128)S(1)}, u32[]{:S(2)}) copy-start(s32[4096,1]{0,1:T(1,128)S(1)} %get-tuple-element.330) | copy-start | bytes 49156
  108.6 11.4 copy-start.56
  108.6 11.4 copy-start.57
  108.7 12.0 %copy-start.34 = (s32[2,2048,1]{1,2,0:T(1,128)S(1)}, s32[2,2048,1]{1,2,0:T(1,128)}, u32[]{:S(2)}) copy-start(s32[2,2048,1]{1,2,0:T(1,128)} %param.55) | copy-start | bytes 49156
  110.1 83.0 %all-to-all-start.1 = ((f32[128,1,160]{2,1,0:T(1,128)}), f32[128,1,160]{2,1,0:T(1,128)}, u32[]{:S(2)}, u32[]{:S(2)}) async-start(f32[128,1,160]{2,1,0:T(1,128)} %reshape.1378), calls=%async_computation.1 | async-start | bytes 262144 | tf_op jit(solution)/shard_map/all_to_all | solution.py:149
  116.9 377.2 %copy-start.39 = (f32[1,5,5]{2,0,1:T(1,128)}, f32[1,5,5]{2,0,1:T(1,128)S(1)}, u32[]{:S(2)}) copy-start(f32[1,5,5]{2,0,1:T(1,128)S(1)} %get-tuple-element.345) | copy-start | bytes 304
  116.9 394.7 %copy-start.32 = (f32[1,5,5]{2,0,1:T(1,128)}, f32[1,5,5]{2,0,1:T(1,128)S(1)}, u32[]{:S(2)}) copy-start(f32[1,5,5]{2,0,1:T(1,128)S(1)} %get-tuple-element.343) | copy-start | bytes 304
  120.0 29.5 %copy-start.47 = (s32[2048,1]{0,1:T(1,128)}, s32[2048,1]{0,1:T(1,128)S(1)}, u32[]{:S(2)}) copy-start(s32[2048,1]{0,1:T(1,128)S(1)} %get-tuple-element.338) | copy-start | bytes 24580
  120.0 29.5 %copy-start.51 = (s32[2048,1]{0,1:T(1,128)}, s32[2048,1]{0,1:T(1,128)S(1)}, u32[]{:S(2)}) copy-start(s32[2048,1]{0,1:T(1,128)S(1)} %get-tuple-element.339) | copy-start | bytes 24580
  188.5 50.3 %collective-permute-start.10 = (f32[5,18,1,64]{3,0,2,1:T(8,128)S(1)}, f32[5,18,1,64]{3,0,2,1:T(8,128)S(1)}, u32[]{:S(2)}, u32[]{:S(2)}) collective-permute-start(f32[5,18,1,64]{3,0,2,1:T(8,128)S(1)} %get-tuple-element.308), channel_id=1, source_target_pairs={{0,1},{1,2},{2,3},{3,4},{4,5},{5,6},{6,7},{7,8},{8,9},{9,10},{10,1... | collective-permute-start | bytes 69128 | tf_op jit(solution)/shard_map/ppermute | solution.py:29
  191.8 48.9 %collective-permute-start.11 = (f32[5,18,1,64]{3,0,2,1:T(8,128)S(1)}, f32[5,18,1,64]{3,0,2,1:T(8,128)}, u32[]{:S(2)}, u32[]{:S(2)}) collective-permute-start(f32[5,18,1,64]{3,0,2,1:T(8,128)S(1)} %get-tuple-element.309), channel_id=1, source_target_pairs={{1,0},{2,1},{3,2},{4,3},{5,4},{6,5},{7,6},{8,7},{9,8},{10,9},{11,1... | collective-permute-start | bytes 69128 | tf_op jit(solution)/shard_map/ppermute | solution.py:32
  193.1 49.0 %all-to-all-start = ((f32[5,128,16]{2,0,1:T(8,128)}), f32[5,128,16]{2,0,1:T(8,128)}, u32[]{:S(2)}, u32[]{:S(2)}) async-start(f32[5,128,16]{2,0,1:T(8,128)} %copy.583), calls=%async_computation | async-start | bytes 1048576 | tf_op jit(solution)/shard_map/all_to_all | solution.py:142
  231.6 13.4 %copy-start.60 = (s32[1024]{0:T(1024)S(1)}, s32[1024]{0:T(1024)}, u32[]{:S(2)}) copy-start(s32[1024]{0:T(1024)} %broadcast_clamp_fusion.9) | copy-start | bytes 12292
  235.2 16.8 %collective-permute-start.5 = (f32[5,1,8,64]{3,0,2,1:T(8,128)}, f32[5,1,8,64]{3,0,2,1:T(8,128)S(1)}, u32[]{:S(2)}, u32[]{:S(2)}) collective-permute-start(f32[5,1,8,64]{3,0,2,1:T(8,128)} %get-tuple-element.320), channel_id=1, source_target_pairs={{0,16},{16,32},{32,48},{48,64},{64,80},{80,96},{96,112},{1,17},{17... | collective-permute-start | bytes 30728 | tf_op jit(solution)/shard_map/ppermute | solution.py:29
  238.8 13.3 %collective-permute-start.4 = (f32[5,1,8,64]{3,0,2,1:T(8,128)}, f32[5,1,8,64]{3,0,2,1:T(8,128)S(1)}, u32[]{:S(2)}, u32[]{:S(2)}) collective-permute-start(f32[5,1,8,64]{3,0,2,1:T(8,128)} %get-tuple-element.321), channel_id=1, source_target_pairs={{16,0},{32,16},{48,32},{64,48},{80,64},{96,80},{112,96},{17,1},{33... | collective-permute-start | bytes 30728 | tf_op jit(solution)/shard_map/ppermute | solution.py:32
  244.9 15.8 %copy-start.43 = (f32[1,5,5]{2,0,1:T(1,128)S(1)}, f32[1,5,5]{2,0,1:T(1,128)}, u32[]{:S(2)}) copy-start(f32[1,5,5]{2,0,1:T(1,128)} %get-tuple-element.342) | copy-start | bytes 304
  250.2 12.2 %copy-start.52 = (f32[1,5,5]{2,0,1:T(1,128)S(1)}, f32[1,5,5]{2,0,1:T(1,128)}, u32[]{:S(2)}) copy-start(f32[1,5,5]{2,0,1:T(1,128)} %get-tuple-element.341) | copy-start | bytes 304
  252.1 5.2 collective-permute-start.7
  255.2 5.1 collective-permute-start.6
  257.2 133.3 %copy-start = (f32[5,4,64,128]{3,0,2,1:T(8,128)}, f32[5,4,64,128]{3,0,2,1:T(8,128)S(1)}, u32[]{:S(2)}) copy-start(f32[5,4,64,128]{3,0,2,1:T(8,128)S(1)} %constant_dynamic-update-slice_fusion.3) | copy-start | bytes 1966084
  317.3 14.6 %copy-start.27 = (f32[2048,8]{0,1:T(8,128)S(1)}, f32[2048,8]{0,1:T(8,128)}, u32[]{:S(2)}) copy-start(f32[2048,8]{0,1:T(8,128)} %get-tuple-element.328) | copy-start | bytes 196612
  337.4 27.2 %all-to-all-start.2 = ((f32[5,128,16]{2,0,1:T(8,128)}), f32[5,128,16]{2,0,1:T(8,128)}, u32[]{:S(2)}, u32[]{:S(2)}) async-start(f32[5,128,16]{2,0,1:T(8,128)} %copy.607), calls=%async_computation.2 | async-start | bytes 1048576 | tf_op jit(solution)/shard_map/all_to_all | solution.py:142
  351.7 26.3 %collective-permute-start.3 = (f32[5,1,64,128]{3,0,2,1:T(8,128)}, f32[5,1,64,128]{3,0,2,1:T(8,128)}, u32[]{:S(2)}, u32[]{:S(2)}) collective-permute-start(f32[5,1,64,128]{3,0,2,1:T(8,128)} %get-tuple-element.300), channel_id=1, source_target_pairs={{0,1},{1,2},{2,3},{3,4},{4,5},{5,6},{6,7},{7,8},{8,9},{9,10},{10,1... | collective-permute-start | bytes 491528 | tf_op jit(solution)/shard_map/ppermute | solution.py:29
  353.0 24.9 %collective-permute-start.2 = (f32[5,1,64,128]{3,0,2,1:T(8,128)}, f32[5,1,64,128]{3,0,2,1:T(8,128)}, u32[]{:S(2)}, u32[]{:S(2)}) collective-permute-start(f32[5,1,64,128]{3,0,2,1:T(8,128)} %get-tuple-element.301), channel_id=1, source_target_pairs={{1,0},{2,1},{3,2},{4,3},{5,4},{6,5},{7,6},{8,7},{9,8},{10,9},{11,1... | collective-permute-start | bytes 491528 | tf_op jit(solution)/shard_map/ppermute | solution.py:32
  524.2 12.3 %copy-start.10 = (f32[4096,8,5]{0,2,1:T(8,128)S(1)}, f32[4096,8,5]{0,2,1:T(8,128)}, u32[]{:S(2)}) copy-start(f32[4096,8,5]{0,2,1:T(8,128)} %reshape.1105) | copy-start | bytes 1966084
  526.7 28.2 %copy-start.26 = (f32[8,2048]{1,0:T(8,128)S(1)}, f32[8,2048]{1,0:T(8,128)}, u32[]{:S(2)}) copy-start(f32[8,2048]{1,0:T(8,128)} %get-tuple-element.329) | copy-start | bytes 196612
  532.5 18.2 %all-to-all-start.5 = ((f32[5,128,16]{2,0,1:T(8,128)}), f32[5,128,16]{2,0,1:T(8,128)S(1)}, u32[]{:S(2)}, u32[]{:S(2)}) async-start(f32[5,128,16]{2,0,1:T(8,128)} %copy.653), calls=%async_computation.5 | async-start | bytes 1048576 | tf_op jit(solution)/shard_map/all_to_all | solution.py:164
  550.7 42.5 %all-to-all-start.3 = ((f32[128,1,160]{2,1,0:T(1,128)}), f32[128,1,160]{2,1,0:T(1,128)S(1)}, u32[]{:S(2)}, u32[]{:S(2)}) async-start(f32[128,1,160]{2,1,0:T(1,128)} %reshape.1380), calls=%async_computation.3 | async-start | bytes 262144 | tf_op jit(solution)/shard_map/all_to_all | solution.py:149
  709.1 30.8 %collective-permute-start.14 = (f32[5,1,8,64]{3,0,2,1:T(8,128)S(1)}, f32[5,1,8,64]{3,0,2,1:T(8,128)S(1)}, u32[]{:S(2)}, u32[]{:S(2)}) collective-permute-start(f32[5,1,8,64]{3,0,2,1:T(8,128)S(1)} %get-tuple-element.316), channel_id=1, source_target_pairs={{0,16},{16,32},{32,48},{48,64},{64,80},{80,96},{96,112},{1,17},{17... | collective-permute-start | bytes 30728 | tf_op jit(solution)/shard_map/ppermute | solution.py:29
  712.8 27.1 %collective-permute-start.15 = (f32[5,1,8,64]{3,0,2,1:T(8,128)S(1)}, f32[5,1,8,64]{3,0,2,1:T(8,128)S(1)}, u32[]{:S(2)}, u32[]{:S(2)}) collective-permute-start(f32[5,1,8,64]{3,0,2,1:T(8,128)S(1)} %get-tuple-element.317), channel_id=1, source_target_pairs={{16,0},{32,16},{48,32},{64,48},{80,64},{96,80},{112,96},{17,1},{33... | collective-permute-start | bytes 30728 | tf_op jit(solution)/shard_map/ppermute | solution.py:32
  729.0 22.1 %copy-start.53 = (f32[1,5,5]{2,0,1:T(1,128)S(1)}, f32[1,5,5]{2,0,1:T(1,128)}, u32[]{:S(2)}) copy-start(f32[1,5,5]{2,0,1:T(1,128)} %get-tuple-element.341) | copy-start | bytes 304
  729.9 65.3 %all-to-all-start.4 = ((f32[128,1,160]{2,1,0:T(1,128)}), f32[128,1,160]{2,1,0:T(1,128)S(1)}, u32[]{:S(2)}, u32[]{:S(2)}) async-start(f32[128,1,160]{2,1,0:T(1,128)} %reshape.1384), calls=%async_computation.4 | async-start | bytes 262144 | tf_op jit(solution)/shard_map/all_to_all | solution.py:171
  739.9 5.5 collective-permute-start.16
  743.2 5.4 collective-permute-start.17
  783.6 25.3 %copy-start.22 = (f32[8,4096]{1,0:T(8,128)S(1)}, f32[8,4096]{1,0:T(8,128)}, u32[]{:S(2)}) copy-start(f32[8,4096]{1,0:T(8,128)} %get-tuple-element.322) | copy-start | bytes 393220
  795.2 71.0 %all-to-all-start.6 = ((f32[128,1,160]{2,1,0:T(1,128)}), f32[128,1,160]{2,1,0:T(1,128)S(1)}, u32[]{:S(2)}, u32[]{:S(2)}) async-start(f32[128,1,160]{2,1,0:T(1,128)} %reshape.1382), calls=%async_computation.6 | async-start | bytes 262144 | tf_op jit(solution)/shard_map/all_to_all | solution.py:171
  860.7 119.3 %collective-permute-start.12 = (f32[5,1,64,128]{3,0,2,1:T(8,128)}, f32[5,1,64,128]{3,0,2,1:T(8,128)S(1)}, u32[]{:S(2)}, u32[]{:S(2)}) collective-permute-start(f32[5,1,64,128]{3,0,2,1:T(8,128)} %get-tuple-element.277), channel_id=1, source_target_pairs={{0,1},{1,2},{2,3},{3,4},{4,5},{5,6},{6,7},{7,8},{8,9},{9,10},{10,1... | collective-permute-start | bytes 491528 | tf_op jit(solution)/shard_map/ppermute | solution.py:29
  862.0 118.0 %collective-permute-start.13 = (f32[5,1,64,128]{3,0,2,1:T(8,128)S(1)}, f32[5,1,64,128]{3,0,2,1:T(8,128)S(1)}, u32[]{:S(2)}, u32[]{:S(2)}) collective-permute-start(f32[5,1,64,128]{3,0,2,1:T(8,128)S(1)} %get-tuple-element.278), channel_id=1, source_target_pairs={{1,0},{2,1},{3,2},{4,3},{5,4},{6,5},{7,6},{8,7},{9,8},{10,9},{11,1... | collective-permute-start | bytes 491528 | tf_op jit(solution)/shard_map/ppermute | solution.py:32
  982.3 15.5 %copy-start.30 = (f32[1,4,64,128]{3,0,2,1:T(1,128)S(1)}, f32[1,4,64,128]{3,0,2,1:T(1,128)}, u32[]{:S(2)}) copy-start(f32[1,4,64,128]{3,0,2,1:T(1,128)} %get-tuple-element.274) | copy-start | bytes 393220
  982.3 15.5 %copy-start.40 = (f32[1,5,5]{2,0,1:T(1,128)S(1)}, f32[1,5,5]{2,0,1:T(1,128)}, u32[]{:S(2)}) copy-start(f32[1,5,5]{2,0,1:T(1,128)} %copy-done.39) | copy-start | bytes 304
  1018.3 76.8 %all-to-all-start.7 = ((f32[5,128,16]{2,0,1:T(8,128)}), f32[5,128,16]{2,0,1:T(8,128)S(1)}, u32[]{:S(2)}, u32[]{:S(2)}) async-start(f32[5,128,16]{2,0,1:T(8,128)} %copy.676), calls=%async_computation.7 | async-start | bytes 1048576 | tf_op jit(solution)/shard_map/all_to_all | solution.py:164
  (41 other events, 210.4 us)
where the time goes:
time: 1170 us; the launch traced here: 1150 us
  local copies, waits for them, and re-layouts  691 us (59%)
  other arithmetic  264 us (23%)
  starting transfers between devices  117 us (10%)
  matrix products  52.5 us (4%)
  waiting for transfers between devices  25.5 us (2%)
    concatenate x6, local copies, waits for them, and re-layouts, corner_stack(): return jnp.concatenate(shifted, axis=0).T  171 us
    slice x4, local copies, waits for them, and re-layouts, spread(): gathered[corner]  134 us
    scatter-add x4, other arithmetic, spread(): gathered = jnp.zeros((cells, 40), jnp.float32).at[base_rows].add(terms)  86.4 us
    gather x8, local copies, waits for them, and re-layouts, interpolate(): corner_stack(values, strides)[base_rows].reshape(base_rows.shape[0], 8, 5)  65.7 us
    reshape x1, other arithmetic, body(): blade_last.reshape(blade_state.shape)  50.7 us
    slice x4, local copies, waits for them, and re-layouts, corner_stack(): widened[:, corner_offset(corner, strides):corner_offset(corner, strides)...  47.8 us
    scatter x2, local copies, waits for them, and re-layouts, fill_fringe(): back_filled = back_flat.T.at[hole_list].set(hole_arrived.T[hole_address]).T  42.7 us
    scatter x2, local copies, waits for them, and re-layouts, transpose_fringe(): jnp.zeros((2 * HOLE_DEV, 5), jnp.float32).at[hole_address]  36.8 us
  transfers between devices with their start and end apart: 26, of which 4 were waited for; matrix products, arithmetic and copies ran while one was open for 55% of the time, Pallas kernels for 0%

commit v1 on v0

v1 whole, which is shorter than its diff:
```python
import functools

import jax
import jax.numpy as jnp
from jax import lax
from jax.experimental import pallas as pl
from jax.experimental.pallas import tpu as pltpu
from jax.sharding import PartitionSpec as P

DEVS = 128
WRAP = 4
WALL = 64
CHORD = 128
EAST = 16
NORTH = 8
VERT = 64
HALF = VERT // 2
RIMS = 1024
HOLES = 2048
QR = 2 * RIMS // DEVS
QH = 2 * HOLES // DEVS
FIELDS = 17

time_step = 0.2
damping = 0.1

F32 = jnp.float32
BF16 = jnp.bfloat16


def split(x):
    hi = x.astype(BF16)
    return hi, (x - hi.astype(F32)).astype(BF16)


def dot_nn(a, b):
    return lax.dot_general(a, b, (((1,), (0,)), ((), ())), preferred_element_type=F32)


def dot_nt(a, b):
    return lax.dot_general(a, b, (((1,), (1,)), ((), ())), preferred_element_type=F32)


def iota(shape, dim):
    return lax.broadcasted_iota(jnp.int32, shape, dim)


def one_hot(rows, index):
    return jnp.where(iota((rows, index.shape[1]), 0) == index, 1.0, 0.0)


def pair_hot(rows, index, first, second):
    position = iota((rows, index.shape[1]), 0)
    return jnp.where(position == index, first, jnp.where(position == index + 1, second, 0.0))


def lane_roll(x, amount):
    amount = amount % x.shape[-1]
    return pltpu.roll(x, amount, x.ndim - 1) if amount else x


def to_planes(block):
    rows = [block[:, y * VERT : (y + 1) * VERT] for y in range(NORTH)]
    return jnp.concatenate(rows, axis=0).T


def from_planes(field):
    turned = field.T
    return [turned[y * EAST : (y + 1) * EAST, :] for y in range(NORTH)]


def donor_parts(weights):
    w = [weights[corner : corner + 1, :] for corner in range(8)]
    x0 = (w[0] + w[1]) + (w[2] + w[3])
    x1 = (w[4] + w[5]) + (w[6] + w[7])
    y0 = (w[0] + w[1]) + (w[4] + w[5])
    y1 = (w[2] + w[3]) + (w[6] + w[7])
    z0 = (w[0] + w[2]) + (w[4] + w[6])
    z1 = (w[1] + w[3]) + (w[5] + w[7])
    return x0, x1, y0, y1, z0, z1


def blade_donors(base, weights):
    x0, x1, y0, y1, z0, z1 = donor_parts(weights)
    wrap = pair_hot(WRAP, base >> 13, x0, x1)
    wall = pair_hot(WALL, (base >> 7) & (WALL - 1), y0, y1)
    rows = jnp.concatenate([wrap[j : j + 1, :] * wall for j in range(WRAP)], axis=0)
    return split(rows), pair_hot(CHORD, base & (CHORD - 1), z0, z1)


def back_donors(base, weights):
    x0, x1, y0, y1, z0, z1 = donor_parts(weights)
    east = pair_hot(EAST, base >> 9, x0, x1)
    north = pair_hot(NORTH, (base >> 6) & (NORTH - 1), y0, y1)
    rows = jnp.concatenate([north[y : y + 1, :] * east for y in range(NORTH)], axis=0)
    return split(rows), pair_hot(HALF, (base & (VERT - 1)) - HALF, z0, z1)


def picked(parts, rows, cols):
    (hi, lo), (row_hi, row_lo) = parts, rows
    table = dot_nn(hi, row_hi) + (dot_nn(hi, row_lo) + dot_nn(lo, row_hi))
    return jnp.sum(table * cols, axis=0, keepdims=True)


def spread_terms(rows, terms):
    (row_hi, row_lo), (hi, lo) = rows, split(terms)
    return dot_nt(row_hi, hi) + (dot_nt(row_hi, lo) + dot_nt(row_lo, hi))


def wall_shift(v, up):
    position = iota(v.shape, 0)
    if up:
        return jnp.where(position == v.shape[0] - 1, 0.0, pltpu.roll(v, v.shape[0] - 1, 0))
    return jnp.where(position == 0, 0.0, pltpu.roll(v, 1, 0))


def lane_shift(v, up, width, period, fill):
    place = (iota(v.shape, 1) // width) % period
    if up:
        return jnp.where(place == period - 1, fill, lane_roll(v, -width))
    return jnp.where(place == 0, fill, lane_roll(v, width))


def flux_of(m_ref, t, v):
    out = []
    for c in range(5):
        total = m_ref[t, c * 5] * v[0]
        for e in range(1, 5):
            total = total + m_ref[t, c * 5 + e] * v[e]
        out.append(total + v[1 + t] * v[c])
    return out


def turned_of(m_ref, t, w):
    out = []
    for c in range(5):
        total = m_ref[t, c] * w[0]
        for e in range(1, 5):
            total = total + m_ref[t, e * 5 + c] * w[e]
        out.append(total)
    return out


PAIRS = [(0, 1), (0, 2), (0, 3), (4, 1), (4, 2), (4, 3), (1, 1), (1, 2), (1, 3), (2, 2), (2, 3), (3, 3)]


def linear_fields(m_ref, center, sides):
    base = [center[c] * (1.0 - 6.0 * damping * time_step) for c in range(5)]
    jumps = []
    for t, (upper, lower) in enumerate(sides):
        jump = [0.5 * (lower[c] - upper[c]) for c in range(5)]
        turned = turned_of(m_ref, t, jump)
        for c in range(5):
            base[c] = base[c] - time_step * (turned[c] - damping * (upper[c] + lower[c]))
        jumps.append(jump)
    out = list(base)
    for a, b in PAIRS:
        if a in (0, 4):
            out.append(jumps[b - 1][a])
        else:
            out.append(jumps[a - 1][b] + jumps[b - 1][a])
    return out


def apply_fields(fields, v):
    out = []
    table = {pair: 5 + n for n, pair in enumerate(PAIRS)}
    for c in range(5):
        total = None
        for e in range(5):
            key = (c, e) if (c, e) in table else (e, c)
            if key in table:
                term = fields[table[key]] * v[e]
                total = term if total is None else total + term
        out.append(fields[c] - time_step * total)
    return out


def adjoint_at(m_ref, v, center, sides):
    out = [center[c] * (1.0 - 6.0 * damping * time_step) for c in range(5)]
    for t, (upper, lower) in enumerate(sides):
        jump = [0.5 * (lower[c] - upper[c]) for c in range(5)]
        turned = turned_of(m_ref, t, jump)
        inner = v[0] * jump[0]
        for e in range(1, 5):
            inner = inner + v[e] * jump[e]
        for c in range(5):
            total = turned[c] + v[1 + t] * jump[c]
            if c == 1 + t:
                total = total + inner
            out[c] = out[c] - time_step * (total - damping * (upper[c] + lower[c]))
    return out


def blade_sides(ref, low, high, j):
    center = [ref[c, j * WALL : (j + 1) * WALL, :] for c in range(5)]
    above = [
        ref[c, (j + 1) * WALL : (j + 2) * WALL, :] if j < WRAP - 1 else high[c] for c in range(5)
    ]
    below = [ref[c, (j - 1) * WALL : j * WALL, :] if j > 0 else low[c] for c in range(5)]
    wall = ([wall_shift(v, True) for v in center], [wall_shift(v, False) for v in center])
    span = (
        [lane_shift(v, True, 1, CHORD, 0.0) for v in center],
        [lane_shift(v, False, 1, CHORD, 0.0) for v in center],
    )
    return center, [(above, below), wall, span]


def back_sides(center, halo):
    east = (
        [lane_shift(v, True, 1, EAST, halo[1][c]) for c, v in enumerate(center)],
        [lane_shift(v, False, 1, EAST, halo[0][c]) for c, v in enumerate(center)],
    )
    north = (
        [lane_shift(v, True, EAST, NORTH, halo[3][c]) for c, v in enumerate(center)],
        [lane_shift(v, False, EAST, NORTH, halo[2][c]) for c, v in enumerate(center)],
    )
    vert = ([wall_shift(v, True) for v in center], [wall_shift(v, False) for v in center])
    return [east, north, vert]


def pack_east(v, x):
    lane = iota((8, DEVS), 1)
    out = jnp.zeros((8, DEVS), F32)
    for g in range(8):
        out = jnp.where(lane % EAST == g, lane_roll(v[g * 8 : g * 8 + 8, :], g - x), out)
    return out


def unpack_east(v, x):
    return jnp.concatenate([lane_roll(v, x - g) for g in range(8)], axis=0)


def pack_north(v, y):
    lane = iota((8, DEVS), 1)
    out = jnp.zeros((8, DEVS), F32)
    for g in range(8):
        out = jnp.where(lane // EAST == g, lane_roll(v[g * 8 : g * 8 + 8, :], (g - y) * EAST), out)
    return out


def unpack_north(v, y):
    return jnp.concatenate([lane_roll(v, (y - g) * EAST) for g in range(8)], axis=0)


def store_edges(blade_at, back, edges):
    to_high, to_low, to_east, to_west = edges
    for c in range(5):
        to_high[c, :WALL, :] = blade_at(c, (WRAP - 1) * WALL)
        to_low[c, :WALL, :] = blade_at(c, 0)
        to_high[c, WALL:, :] = pack_north(back[c], NORTH - 1)
        to_low[c, WALL:, :] = pack_north(back[c], 0)
        to_east[c] = pack_east(back[c], EAST - 1)
        to_west[c] = pack_east(back[c], 0)


EDGE_SHAPES = [
    jax.ShapeDtypeStruct((5, WALL + 8, CHORD), F32),
    jax.ShapeDtypeStruct((5, WALL + 8, CHORD), F32),
    jax.ShapeDtypeStruct((5, 8, DEVS), F32),
    jax.ShapeDtypeStruct((5, 8, DEVS), F32),
]


def read_halo(place_ref, from_low, from_high, from_west, from_east):
    north = place_ref[0]
    keep_low = jnp.where(north > 0, 1.0, 0.0)
    keep_high = jnp.where(north < DEVS // 8 - 1, 1.0, 0.0)
    low = [from_low[c, :WALL, :] for c in range(5)]
    high = [from_high[c, :WALL, :] for c in range(5)]
    west = [unpack_east(from_west[c], 0) for c in range(5)]
    east = [unpack_east(from_east[c], EAST - 1) for c in range(5)]
    south = [unpack_north(from_low[c, WALL:, :] * keep_low, 0) for c in range(5)]
    upper = [unpack_north(from_high[c, WALL:, :] * keep_high, NORTH - 1) for c in range(5)]
    return low, high, [west, east, south, upper]


def exchange(edges):
    gx, gy = lax.axis_size("gx"), lax.axis_size("gy")
    ring = [(i, (i + 1) % gy) for i in range(gy)]
    line = [(i, i + 1) for i in range(gx - 1)]
    to_high, to_low, to_east, to_west = edges
    return (
        lax.ppermute(to_high, "gy", ring),
        lax.ppermute(to_low, "gy", [(b, a) for a, b in ring]),
        lax.ppermute(to_east, "gx", line),
        lax.ppermute(to_west, "gx", [(b, a) for a, b in line]),
    )


def regroup(pieces, width):
    count = DEVS // width
    shape = next(piece.shape for piece in pieces if piece is not None)
    block = iota(shape, 1) // width
    out = []
    for b in range(count):
        total = jnp.zeros(shape, F32)
        for a in range(count):
            if pieces[a] is not None:
                total = jnp.where(block == a, lane_roll(pieces[a], (a - b) * width), total)
        out.append(total)
    return out


def ranks_of(owner_ref, out_ref):
    count = owner_ref.shape[1]
    earlier = jnp.where(iota((256, 256), 0) < iota((256, 256), 1), 1.0, 0.0).astype(BF16)
    carry = jnp.zeros((DEVS, 1), F32)
    for start in range(0, count, 256):
        marks = one_hot(DEVS, owner_ref[:, start : start + 256])
        before = dot_nn(marks.astype(BF16), earlier) + carry
        out_ref[:, start : start + 256] = jnp.sum(marks * before, axis=0, keepdims=True).astype(
            jnp.int32
        )
        carry = carry + jnp.sum(marks, axis=1, keepdims=True)


def send_rows(values, owner, rank, slots, pad_rows):
    marks = one_hot(DEVS, owner).astype(BF16)
    seats = one_hot(slots, rank)
    terms = jnp.concatenate([seats * v for v in values], axis=0)
    before, after = pad_rows
    parts = [terms]
    if before:
        parts.insert(0, jnp.zeros((before, terms.shape[1]), F32))
    if after:
        parts.append(jnp.zeros((after, terms.shape[1]), F32))
    if len(parts) > 1:
        terms = jnp.concatenate(parts, axis=0)
    hi, lo = split(terms)
    return dot_nt(marks, hi) + dot_nt(marks, lo)


def hole_parts(cell):
    row = ((cell >> 6) & (NORTH - 1)) * EAST + (cell >> 9)
    return row, cell & (VERT - 1)


def hole_values(low_half, cell):
    row, vert = hole_parts(cell)
    marks = one_hot(DEVS, row).astype(BF16)
    seats = one_hot(HALF, vert)
    out = []
    for field in low_half:
        hi, lo = split(field)
        table = dot_nn(hi, marks) + dot_nn(lo, marks)
        out.append(jnp.sum(table * seats, axis=0, keepdims=True))
    return out


def hole_mask(cell_ref):
    total = jnp.zeros((HALF, DEVS), F32)
    for start in range(0, HOLES, 512):
        row, vert = hole_parts(cell_ref[:, start : start + 512])
        total = total + dot_nt(one_hot(HALF, vert).astype(BF16), one_hot(DEVS, row).astype(BF16))
    return total


CHUNK = 512


def interpolate_all(blade_parts, back_parts, tables, blade_out, back_out):
    back_base, back_weight, blade_base, blade_weight = tables

    def blade_step(n, carry):
        lanes = pl.ds(pl.multiple_of(n * CHUNK, CHUNK), CHUNK)
        rows, cols = blade_donors(blade_base[:, lanes], blade_weight[0, :, lanes])
        for c in range(5):
            value = picked((blade_parts[0][c], blade_parts[1][c]), rows, cols)
            for m in range(CHUNK // DEVS):
                blade_out[c, pl.ds(n * (CHUNK // DEVS) + m, 1), :] = value[
                    :, m * DEVS : (m + 1) * DEVS
                ]
        return carry

    lax.fori_loop(0, 2 * HOLES // CHUNK, blade_step, 0)

    def back_step(n, carry):
        lanes = pl.ds(pl.multiple_of(n * CHUNK, CHUNK), CHUNK)
        rows, cols = back_donors(back_base[:, lanes], back_weight[0, :, lanes])
        for c in range(5):
            value = picked((back_parts[0][c], back_parts[1][c]), rows, cols)
            for m in range(CHUNK // DEVS):
                back_out[c, pl.ds(n * (CHUNK // DEVS) + m, 1), :] = value[
                    :, m * DEVS : (m + 1) * DEVS
                ]
        return carry

    lax.fori_loop(0, 2 * RIMS // CHUNK, back_step, 0)


def start_kernel(
    blade, back, cot, back_cot, back_base, back_weight, blade_base, blade_weight,
    send, back_planes, cot_planes, to_high, to_low, to_east, to_west,
    blade_hi, blade_lo, back_hi, back_lo, hole_vals, rim_vals,
):
    cots = []
    for c in range(5):
        turned = to_planes(back_cot[c])
        cot_planes[c] = turned
        cots.append(turned)
    store_edges(lambda c, r: cot[c, r : r + WALL, :], cots, (to_high, to_low, to_east, to_west))
    for c in range(5):
        hi, lo = split(blade[c].T)
        blade_hi[c] = hi
        blade_lo[c] = lo
        field = to_planes(back[c])
        back_planes[c] = field
        hi, lo = split(field[HALF:, :])
        back_hi[c] = hi
        back_lo[c] = lo
    interpolate_all(
        (blade_hi, blade_lo), (back_hi, back_lo),
        (back_base, back_weight, blade_base, blade_weight), hole_vals, rim_vals,
    )
    store_slots(hole_vals, rim_vals, send)


def store_slots(hole_vals, rim_vals, send):
    first = regroup([hole_vals[c] for c in range(4)], QH)
    fifth = hole_vals[4]
    tail = regroup([fifth, None, None, None], QH)
    for d in range(DEVS // QH):
        send[pl.ds(d, QH, stride=DEVS // QH), 0, :] = first[d]
        send[pl.ds(d, QH, stride=DEVS // QH), 1, :] = tail[d]
    rims = regroup([None, None] + [rim_vals[c] for c in range(5)] + [None], QR)
    lane = iota((QR, DEVS), 1)
    for d in range(DEVS // QR):
        rows = pl.ds(d, QR, stride=DEVS // QR)
        send[rows, 1, :] = jnp.where(lane < QH, send[rows, 1, :], rims[d])


def cot_kernel(
    place, blade_m, back_m, cot, cot_planes, from_low, from_high, from_west, from_east,
    rim_owner, hole_owner, hole_cell,
    send, blade_fields, back_fields, rim_rank, hole_rank,
):
    low, high, halo = read_halo(place, from_low, from_high, from_west, from_east)
    for j in range(WRAP):
        center, sides = blade_sides(cot, low, high, j)
        fields = linear_fields(blade_m, center, sides)
        for n in range(FIELDS):
            blade_fields[n, j * WALL : (j + 1) * WALL, :] = fields[n]
    center = [cot_planes[c] for c in range(5)]
    fields = linear_fields(back_m, center, back_sides(center, halo))
    for n in range(FIELDS):
        back_fields[n] = fields[n]
    for step in range(2):
        ranks_of(rim_owner.at[step], rim_rank.at[step])
        ranks_of(hole_owner.at[step], hole_rank.at[step])

    total = jnp.zeros((DEVS, FIELDS * QR + 112), F32)
    for j in range(WRAP):
        lanes = slice(j * 256, j * 256 + 256)
        values = [
            jnp.concatenate(
                [
                    blade_fields[n, j * WALL + WALL - 2 + k : j * WALL + WALL - 1 + k, :]
                    for k in range(2)
                ],
                axis=1,
            )
            for n in range(FIELDS)
        ]
        total = total + send_rows(
            values, rim_owner[1, :, lanes], rim_rank[1, :, lanes], QR, (0, 112)
        )
    for m in range(3):
        send[:, 5 + m, :] = total[:, m * DEVS : (m + 1) * DEVS]
    total = jnp.zeros((DEVS, FIELDS * QH + 96), F32)
    low_half = [back_fields[n, :HALF, :] for n in range(FIELDS)]
    for start in range(0, HOLES, 512):
        lanes = slice(start, start + 512)
        values = hole_values(low_half, hole_cell[1:2, lanes])
        total = total + send_rows(
            values, hole_owner[1, :, lanes], hole_rank[1, :, lanes], QH, (0, 96)
        )
    for m in range(5):
        send[:, m, :] = total[:, m * DEVS : (m + 1) * DEVS]


def fill_kernel(
    blade, back_planes, recv, rim_owner, hole_owner, rim_rank, hole_rank, hole_cell,
    blade_first, back_first, to_high, to_low, to_east, to_west,
):
    arrived = jnp.concatenate([recv[:, 0, :].T, recv[:, 1, :].T], axis=0)
    hi, lo = split(arrived)
    for c in range(5):
        for j in range(WRAP):
            rows = slice(j * WALL, (j + 1) * WALL)
            blade_first[c, rows, :] = blade[c, rows, :]
    base = 5 * QH
    for j in range(WRAP):
        lanes = slice(j * 256, j * 256 + 256)
        marks = one_hot(DEVS, rim_owner[0, :, lanes]).astype(BF16)
        seats = one_hot(QR, rim_rank[0, :, lanes])
        table = dot_nn(hi[base : base + 5 * QR], marks) + dot_nn(lo[base : base + 5 * QR], marks)
        for c in range(5):
            value = jnp.sum(table[c * QR : (c + 1) * QR] * seats, axis=0, keepdims=True)
            for k in range(2):
                row = j * WALL + WALL - 2 + k
                blade_first[c, row : row + 1, :] = value[:, k * CHORD : (k + 1) * CHORD]
    filled = [jnp.zeros((HALF, DEVS), F32) for _ in range(5)]
    mask = jnp.zeros((HALF, DEVS), F32)
    for start in range(0, HOLES, 512):
        lanes = slice(start, start + 512)
        marks = one_hot(DEVS, hole_owner[0, :, lanes]).astype(BF16)
        seats = one_hot(QH, hole_rank[0, :, lanes])
        row, vert = hole_parts(hole_cell[0:1, lanes])
        row_marks = one_hot(DEVS, row).astype(BF16)
        vert_marks = one_hot(HALF, vert)
        table = dot_nn(hi[: 5 * QH], marks) + dot_nn(lo[: 5 * QH], marks)
        mask = mask + dot_nt(vert_marks.astype(BF16), row_marks)
        for c in range(5):
            value = jnp.sum(table[c * QH : (c + 1) * QH] * seats, axis=0, keepdims=True)
            value_hi, value_lo = split(vert_marks * value)
            filled[c] = filled[c] + (dot_nt(value_hi, row_marks) + dot_nt(value_lo, row_marks))
    backs = []
    for c in range(5):
        top = jnp.where(mask > 0.5, filled[c], back_planes[c, :HALF, :])
        field = jnp.concatenate([top, back_planes[c, HALF:, :]], axis=0)
        back_first[c] = field
        backs.append(field)
    store_edges(
        lambda c, r: blade_first[c, r : r + WALL, :], backs, (to_high, to_low, to_east, to_west)
    )


def residual_step(m_ref, center, halo_flux):
    out = [center[c] * (1.0 - 6.0 * damping * time_step) for c in range(5)]
    for t in range(3):
        upper, lower = halo_flux(t)
        for c in range(5):
            out[c] = out[c] - time_step * (upper[c] - lower[c])
    return out


def side_terms(m_ref, t, v):
    flux = flux_of(m_ref, t, v)
    upper = [0.5 * flux[c] - damping * v[c] for c in range(5)]
    lower = [0.5 * flux[c] + damping * v[c] for c in range(5)]
    return upper, lower


def middle_kernel(
    place, blade_m, back_m, blade_first, back_first, from_low, from_high, from_west, from_east,
    blade_fields, back_fields, recv, back_base, back_weight, blade_base, blade_weight, hole_cell,
    blade_mid, back_mid, to_high, to_low, to_east, to_west,
    blade_next, back_next, blade_hi, blade_lo, back_hi, back_lo, hole_lin, rim_lin,
):
    low, high, halo = read_halo(place, from_low, from_high, from_west, from_east)

    for j in range(WRAP):
        center, sides = blade_sides(blade_first, low, high, j)

        def around(t, center=center, sides=sides):
            if t == 0:
                return side_terms(blade_m, 0, sides[0][0])[0], side_terms(blade_m, 0, sides[0][1])[1]
            upper, lower = side_terms(blade_m, t, center)
            if t == 1:
                return [wall_shift(v, True) for v in upper], [wall_shift(v, False) for v in lower]
            return (
                [lane_shift(v, True, 1, CHORD, 0.0) for v in upper],
                [lane_shift(v, False, 1, CHORD, 0.0) for v in lower],
            )

        out = residual_step(blade_m, center, around)
        for c in range(5):
            blade_next[c, j * WALL : (j + 1) * WALL, :] = out[c]
    center = [back_first[c] for c in range(5)]

    def across(t):
        upper, lower = side_terms(back_m, t, center)
        if t == 2:
            return [wall_shift(v, True) for v in upper], [wall_shift(v, False) for v in lower]
        width, period = ((1, EAST), (EAST, NORTH))[t]
        below = side_terms(back_m, t, halo[2 * t])[1]
        above = side_terms(back_m, t, halo[2 * t + 1])[0]
        return (
            [lane_shift(upper[c], True, width, period, above[c]) for c in range(5)],
            [lane_shift(lower[c], False, width, period, below[c]) for c in range(5)],
        )

    out = residual_step(back_m, center, across)
    for c in range(5):
        back_next[c] = out[c]
        hi, lo = split(out[c][HALF:, :])
        back_hi[c] = hi
        back_lo[c] = lo
        hi, lo = split(blade_next[c].T)
        blade_hi[c] = hi
        blade_lo[c] = lo

    for j in range(WRAP):
        rows = slice(j * WALL, (j + 1) * WALL)
        v = [blade_next[c, rows, :] for c in range(5)]
        own = apply_fields([blade_fields[n, rows, :] for n in range(FIELDS)], v)
        inside = iota((WALL, CHORD), 0) < WALL - 2
        for c in range(5):
            blade_mid[c, rows, :] = jnp.where(inside, own[c], 0.0)
    mask = hole_mask(hole_cell)
    own = apply_fields([back_fields[n] for n in range(FIELDS)], [back_next[c] for c in range(5)])
    for c in range(5):
        back_mid[c, :HALF, :] = jnp.where(mask > 0.5, 0.0, own[c][:HALF, :])
        back_mid[c, HALF:, :] = own[c][HALF:, :]

    for m in range(5):
        pieces = [recv[pl.ds(d, QH, stride=DEVS // QH), m, :] for d in range(DEVS // QH)]
        for b, piece in enumerate(regroup(pieces, QH)):
            if m * 4 + b < FIELDS:
                hole_lin[m * 4 + b] = piece
    for m in range(3):
        pieces = [recv[pl.ds(d, QR, stride=DEVS // QR), 5 + m, :] for d in range(DEVS // QR)]
        for b, piece in enumerate(regroup(pieces, QR)):
            if m * 8 + b < FIELDS:
                rim_lin[m * 8 + b] = piece

    def lanes_of(ref, n, k):
        count = CHUNK // DEVS
        return jnp.concatenate([ref[k, pl.ds(n * count + m, 1), :] for m in range(count)], axis=1)

    def blade_step(n, carry):
        lanes = pl.ds(pl.multiple_of(n * CHUNK, CHUNK), CHUNK)
        rows, cols = blade_donors(blade_base[:, lanes], blade_weight[0, :, lanes])
        value = [picked((blade_hi[c], blade_lo[c]), rows, cols) for c in range(5)]
        mu = apply_fields([lanes_of(hole_lin, n, k) for k in range(FIELDS)], value)
        for c in range(5):
            blade_mid[c] = blade_mid[c] + spread_terms(rows, cols * mu[c])
        return carry

    lax.fori_loop(0, 2 * HOLES // CHUNK, blade_step, 0)

    def back_step(n, carry):
        lanes = pl.ds(pl.multiple_of(n * CHUNK, CHUNK), CHUNK)
        rows, cols = back_donors(back_base[:, lanes], back_weight[0, :, lanes])
        value = [picked((back_hi[c], back_lo[c]), rows, cols) for c in range(5)]
        mu = apply_fields([lanes_of(rim_lin, n, k) for k in range(FIELDS)], value)
        spread_back(back_mid, rows, cols, mu)
        return carry

    lax.fori_loop(0, 2 * RIMS // CHUNK, back_step, 0)
    store_edges(
        lambda c, r: blade_mid[c, r : r + WALL, :],
        [back_mid[c] for c in range(5)],
        (to_high, to_low, to_east, to_west),
    )


def spread_back(target, rows, cols, mu):
    row_hi, row_lo = rows
    for c in range(5):
        hi, lo = split(cols * mu[c])
        target[c, HALF:, :] = target[c, HALF:, :] + (
            dot_nt(hi, row_hi) + (dot_nt(lo, row_hi) + dot_nt(hi, row_lo))
        )


def last_kernel(
    place, blade_m, back_m, blade_first, back_first, blade_mid, back_mid,
    from_low, from_high, from_west, from_east,
    rim_owner, hole_owner, rim_rank, hole_rank, hole_cell,
    send, blade_kept, back_kept,
):
    low, high, halo = read_halo(place, from_low, from_high, from_west, from_east)
    rims = jnp.zeros((DEVS, DEVS), F32)
    for j in range(WRAP):
        rows = slice(j * WALL, (j + 1) * WALL)
        center, sides = blade_sides(blade_mid, low, high, j)
        out = adjoint_at(blade_m, [blade_first[c, rows, :] for c in range(5)], center, sides)
        inside = iota((WALL, CHORD), 0) < WALL - 2
        values = []
        for c in range(5):
            blade_kept[c, rows, :] = jnp.where(inside, out[c], 0.0)
            values.append(
                jnp.concatenate([out[c][WALL - 2 : WALL - 1, :], out[c][WALL - 1 :, :]], axis=1)
            )
        lanes = slice(j * 256, j * 256 + 256)
        rims = rims + send_rows(
            values, rim_owner[0, :, lanes], rim_rank[0, :, lanes], QR, (QH, DEVS - QH - 5 * QR)
        )
    center = [back_mid[c] for c in range(5)]
    out = adjoint_at(back_m, [back_first[c] for c in range(5)], center, back_sides(center, halo))
    mask = hole_mask(hole_cell)
    low_half = []
    for c in range(5):
        back_kept[c, :HALF, :] = jnp.where(mask > 0.5, 0.0, out[c][:HALF, :])
        back_kept[c, HALF:, :] = out[c][HALF:, :]
        low_half.append(out[c][:HALF, :])
    holes = jnp.zeros((DEVS, 2 * DEVS), F32)
    for start in range(0, HOLES, 512):
        lanes = slice(start, start + 512)
        values = hole_values(low_half, hole_cell[0:1, lanes])
        holes = holes + send_rows(
            values, hole_owner[0, :, lanes], hole_rank[0, :, lanes], QH, (0, 2 * DEVS - 5 * QH)
        )
    send[:, 0, :] = holes[:, :DEVS]
    send[:, 1, :] = holes[:, DEVS:] + rims


def end_kernel(
    blade_kept, back_kept, recv, back_base, back_weight, blade_base, blade_weight,
    blade_out, back_out, hole_mu, rim_mu, back_acc,
):
    count = DEVS // QH
    pieces = [recv[pl.ds(d, QH, stride=count), 0, :] for d in range(count)]
    for c, piece in enumerate(regroup(pieces, QH)):
        hole_mu[c] = piece
    pieces = [recv[pl.ds(d, QH, stride=count), 1, :] for d in range(count)]
    hole_mu[4] = regroup(pieces, QH)[0]
    count = DEVS // QR
    pieces = [recv[pl.ds(d, QR, stride=count), 1, :] for d in range(count)]
    groups = regroup(pieces, QR)
    for c in range(5):
        rim_mu[c] = groups[QH // QR + c]
        blade_out[c] = blade_kept[c]
        back_acc[c] = back_kept[c]

    def lanes_of(ref, n, k):
        count = CHUNK // DEVS
        return jnp.concatenate([ref[k, pl.ds(n * count + m, 1), :] for m in range(count)], axis=1)

    def blade_step(n, carry):
        lanes = pl.ds(pl.multiple_of(n * CHUNK, CHUNK), CHUNK)
        rows, cols = blade_donors(blade_base[:, lanes], blade_weight[0, :, lanes])
        for c in range(5):
            blade_out[c] = blade_out[c] + spread_terms(rows, cols * lanes_of(hole_mu, n, c))
        return carry

    lax.fori_loop(0, 2 * HOLES // CHUNK, blade_step, 0)

    def back_step(n, carry):
        lanes = pl.ds(pl.multiple_of(n * CHUNK, CHUNK), CHUNK)
        rows, cols = back_donors(back_base[:, lanes], back_weight[0, :, lanes])
        spread_back(back_acc, rows, cols, [lanes_of(rim_mu, n, c) for c in range(5)])
        return carry

    lax.fori_loop(0, 2 * RIMS // CHUNK, back_step, 0)
    for c in range(5):
        parts = from_planes(back_acc[c])
        for y in range(0, NORTH, 2):
            back_out[c, :, y * VERT : (y + 2) * VERT] = jnp.concatenate(parts[y : y + 2], axis=1)


VMEM = pl.BlockSpec(memory_space=pltpu.VMEM)
SMEM = pl.BlockSpec(memory_space=pltpu.SMEM)
BLADE = jax.ShapeDtypeStruct((5, WRAP * WALL, CHORD), F32)
PLANES = jax.ShapeDtypeStruct((5, VERT, DEVS), F32)
DONOR_PARTS = [
    pltpu.VMEM((5, CHORD, WRAP * WALL), BF16),
    pltpu.VMEM((5, CHORD, WRAP * WALL), BF16),
    pltpu.VMEM((5, HALF, DEVS), BF16),
    pltpu.VMEM((5, HALF, DEVS), BF16),
]


def run(kernel, name, args, out_shape, scratch=(), scalars=0, flops=0):
    size = sum(4 * a.size for a in args) + sum(4 * o.size for o in out_shape)
    return pl.pallas_call(
        kernel,
        name=name,
        out_shape=list(out_shape),
        in_specs=[SMEM] * scalars + [VMEM] * (len(args) - scalars),
        out_specs=[VMEM] * len(out_shape),
        scratch_shapes=list(scratch),
        cost_estimate=pl.CostEstimate(flops=flops, bytes_accessed=size, transcendentals=0),
    )(*args)


def swap(rows):
    return lax.all_to_all(rows, ("gx", "gy"), split_axis=0, concat_axis=0, tiled=True)


def body(
    blade_state,
    back_state,
    blade_cotangent,
    back_cotangent,
    blade_flux,
    back_flux,
    blade_owner,
    back_donor_cell,
    back_donor_weight,
    hole_cell,
    hole_owner,
    blade_donor_cell,
    blade_donor_weight,
):
    shape = jax.ShapeDtypeStruct
    place = lax.axis_index("gy").astype(jnp.int32).reshape(1)
    blade = blade_state.reshape(5, WRAP * WALL, CHORD)
    cot = blade_cotangent.reshape(5, WRAP * WALL, CHORD)
    blade_m = blade_flux.reshape(3, 25)
    back_m = back_flux.reshape(3, 25)
    rim_owner = blade_owner.reshape(2, 1, RIMS)
    holes_owner = hole_owner.reshape(2, 1, HOLES)
    tables = [
        (
            back_donor_cell[s : s + 1],
            back_donor_weight[s : s + 1],
            blade_donor_cell[s : s + 1],
            blade_donor_weight[s : s + 1],
        )
        for s in range(2)
    ]

    send, back_planes, cot_planes, *edges = run(
        start_kernel,
        "start",
        (blade, back_state, cot, back_cotangent) + tables[0],
        [shape((DEVS, 2, DEVS), F32), PLANES, PLANES] + EDGE_SHAPES,
        DONOR_PARTS + [pltpu.VMEM((5, QH, DEVS), F32), pltpu.VMEM((5, QR, DEVS), F32)],
        flops=5 * 10**9,
    )
    recv = swap(send)
    cot_halo = exchange(edges)
    lin_send, blade_fields, back_fields, rim_rank, hole_rank = run(
        cot_kernel,
        "cotangent",
        (place, blade_m, back_m, cot, cot_planes, *cot_halo, rim_owner, holes_owner, hole_cell),
        [
            shape((DEVS, 8, DEVS), F32),
            shape((FIELDS, WRAP * WALL, CHORD), F32),
            shape((FIELDS, VERT, DEVS), F32),
            shape((2, 1, RIMS), jnp.int32),
            shape((2, 1, HOLES), jnp.int32),
        ],
        scalars=3,
        flops=2 * 10**9,
    )
    lin_recv = swap(lin_send)
    slots = (rim_owner, holes_owner, rim_rank, hole_rank)
    blade_first, back_first, *edges = run(
        fill_kernel,
        "fill",
        (blade, back_planes, recv) + slots + (hole_cell[0:1],),
        [BLADE, PLANES] + EDGE_SHAPES,
        flops=10**9,
    )
    first_halo = exchange(edges)
    blade_mid, back_mid, *edges = run(
        middle_kernel,
        "middle",
        (place, blade_m, back_m, blade_first, back_first, *first_halo, blade_fields, back_fields)
        + (lin_recv,)
        + tables[1]
        + (hole_cell[1:2],),
        [BLADE, PLANES] + EDGE_SHAPES,
        [pltpu.VMEM(BLADE.shape, F32), pltpu.VMEM(PLANES.shape, F32)]
        + DONOR_PARTS
        + [pltpu.VMEM((FIELDS, QH, DEVS), F32), pltpu.VMEM((FIELDS, QR, DEVS), F32)],
        scalars=3,
        flops=10**10,
    )
    mid_halo = exchange(edges)
    send, blade_kept, back_kept = run(
        last_kernel,
        "last",
        (place, blade_m, back_m, blade_first, back_first, blade_mid, back_mid, *mid_halo)
        + slots
        + (hole_cell[0:1],),
        [shape((DEVS, 2, DEVS), F32), BLADE, PLANES],
        scalars=3,
        flops=10**9,
    )
    recv = swap(send)
    blade_last, back_last = run(
        end_kernel,
        "end",
        (blade_kept, back_kept, recv) + tables[0],
        [BLADE, shape((5, EAST, NORTH * VERT), F32)],
        [
            pltpu.VMEM((5, QH, DEVS), F32),
            pltpu.VMEM((5, QR, DEVS), F32),
            pltpu.VMEM(PLANES.shape, F32),
        ],
        flops=5 * 10**9,
    )
    return (blade_last.reshape(blade_state.shape), back_last)


def solution(mesh):
    return jax.shard_map(
        body,
        mesh=mesh,
        in_specs=(
            P(None, "gx", "gy"),
            P(None, "gx", "gy"),
            P(None, "gx", "gy"),
            P(None, "gx", "gy"),
            P(),
            P(),
            P(None, ("gx", "gy"), None),
            P(None, ("gx", "gy")),
            P(None, None, ("gx", "gy")),
            P(None, ("gx", "gy")),
            P(None, ("gx", "gy"), None),
            P(None, ("gx", "gy")),
            P(None, None, ("gx", "gy")),
        ),
        out_specs=(P(None, "gx", "gy"), P(None, "gx", "gy")),
        check_vma=False,
    )
```

time: 1170 us -> 159 us (0.14); the launches traced: 1150 us -> 158 us
  local copies, waits for them, and re-layouts: 691 us -> 10.4 us
  other arithmetic: 264 us -> 0 us
  Pallas kernels: 0 us -> 74 us
  starting transfers between devices: 117 us -> 49.5 us
  matrix products: 52.5 us -> 0 us
  waiting for transfers between devices: 25.5 us -> 6.54 us
  blocking collectives: 0 us -> 16.6 us
    slice x23 -> x5, local copies, waits for them, and re-layouts: 188 us -> 6.7 us  [the longest x1 1.69 us: body(): blade_donor_weight[s:s + 1]]
    concatenate x7 -> x0, local copies, waits for them, and re-layouts: 171 us -> none  [the longest x6 171 us: corner_stack(): return jnp.concatenate(shifted, axis=0).T]
    scatter x12 -> x0, local copies, waits for them, and re-layouts: 118 us -> none  [the longest x2 42.7 us: fill_fringe(): back_filled = back_flat.T.at[hole_list].set(hole_arrived.T[hole_address]).T]
    scatter-add x4 -> x0, other arithmetic: 86.4 us -> none  [spread(): gathered = jnp.zeros((cells, 40), jnp.float32).at[base_rows].add(terms)]
    gather x10 -> x0, local copies, waits for them, and re-layouts: 76.7 us -> none  [the longest x8 65.7 us: interpolate(): corner_stack(values, strides)[base_rows].reshape(base_rows.shape[0], 8, 5)]
    pallas_call x0 -> x6, Pallas kernels: none -> 74 us  [run(): pl.pallas_call(kernel, name=name, out_shape=list(out_shape), in_specs=[SM...]
    all_to_all x8 -> x2, starting transfers between devices: 69.1 us -> 15.9 us  [swap(): lax.all_to_all(rows, ('gx', 'gy'), split_axis=0, concat_axis=0, tiled=True)]
    dot_general x28 -> x0, matrix products: 52.5 us -> none  [the longest x12 31.5 us: adjoint_of(): jnp.einsum('ec,e...->c...', matrices[direction], jump_half, precision=exa...]
  transfers between devices with their start and end apart: 26 -> 14, of which waited for: 4 -> 2; matrix products, arithmetic and copies ran while one was open for 55% -> 1% of each run, Pallas kernels for 0% -> 9%
where the time goes in v1:
time: 159 us; the launch traced here: 158 us
  Pallas kernels  74 us (47%)
  starting transfers between devices  49.5 us (31%)
  blocking collectives  16.6 us (10%)
  local copies, waits for them, and re-layouts  10.4 us (7%)
  waiting for transfers between devices  6.54 us (4%)
    pallas_call x6, Pallas kernels, run(): pl.pallas_call(kernel, name=name, out_shape=list(out_shape), in_specs=[SM...  74 us
    all_to_all x1, blocking collectives, swap(): lax.all_to_all(rows, ('gx', 'gy'), split_axis=0, concat_axis=0, tiled=True)  16.6 us
    all_to_all x2, starting transfers between devices, swap(): lax.all_to_all(rows, ('gx', 'gy'), split_axis=0, concat_axis=0, tiled=True)  15.9 us
    ppermute x3, starting transfers between devices, exchange(): lax.ppermute(to_low, 'gy', [(b, a) for a, b in ring])  14 us
    ppermute x3, starting transfers between devices, exchange(): lax.ppermute(to_east, 'gx', line)  10.1 us
    ppermute x3, waiting for transfers between devices, exchange(): lax.ppermute(to_west, 'gx', [(b, a) for a, b in line])  6.51 us
    ppermute x3, starting transfers between devices, exchange(): lax.ppermute(to_west, 'gx', [(b, a) for a, b in line])  5.98 us
    ppermute x3, starting transfers between devices, exchange(): lax.ppermute(to_high, 'gy', ring)  3.54 us
  transfers between devices with their start and end apart: 14, of which 2 were waited for; matrix products, arithmetic and copies ran while one was open for 1% of the time, Pallas kernels for 9%

profile of v1, /device:TPU:1, one launch (start us, length us, event | category | flops | bytes accessed | tf_op | source)
XLA Modules:
  0.0 157.9 jit_solution(1022069804888103423)
XLA Ops:
  0.6 1.4 fusion.4
  2.0 1.5 fusion.2
  3.5 1.5 fusion.1
  5.0 1.7 %fusion = (f32[1,8,4096]{2,1,0:T(8,128)}, f32[1,8,4096]{2,1,0:T(8,128)}) fusion(f32[2,8,4096]{2,1,0:T(8,128)} %param.25), kind=kLoop, calls=%fused_computation | loop fusion | bytes 524288 | tf_op jit(solution)/shard_map/slice | solution.py:801
  6.7 11.2 %start.1 = (f32[128,2,128]{2,1,0:T(2,128)}, f32[5,64,128]{2,1,0:T(8,128)}, f32[5,64,128]{2,1,0:T(8,128)}, f32[5,72,128]{2,1,0:T(8,128)}, f32[5,72,128]{2,1,0:T(8...) custom-call(f32[5,256,128]{2,1,0:T(8,128)} %bitcast.8, f32[5,16,512]{2,1,0:T(8,128)} %back.1, f32[5,256,128]{2,1,0:T(8,128)} %bitcast.6, ...), custom_call_target="tpu_custom_call" | custom-call | flops 5000000000 | bytes 2727936 | tf_op jit(solution)/shard_map/start/pallas_call | solution.py:758
  17.9 2.1 %collective-permute-start = (f32[5,72,128]{2,1,0:T(8,128)}, f32[5,72,128]{2,1,0:T(8,128)S(1)}, u32[]{:S(2)}, u32[]{:S(2)}) collective-permute-start(f32[5,72,128]{2,1,0:T(8,128)} %get-tuple-element.34), channel_id=1, source_target_pairs={{0,1},{1,2},{2,3},{3,4},{4,5},{5,6},{6,7},{7,8},{8,9},{9,10},{10,1... | collective-permute-start | bytes 552968 | tf_op jit(solution)/shard_map/ppermute | solution.py:284
  20.1 5.0 %collective-permute-start.1 = (f32[5,72,128]{2,1,0:T(8,128)}, f32[5,72,128]{2,1,0:T(8,128)S(1)}, u32[]{:S(2)}, u32[]{:S(2)}) collective-permute-start(f32[5,72,128]{2,1,0:T(8,128)} %get-tuple-element.35), channel_id=1, source_target_pairs={{1,0},{2,1},{3,2},{4,3},{5,4},{6,5},{7,6},{8,7},{9,8},{10,9},{11,1... | collective-permute-start | bytes 552968 | tf_op jit(solution)/shard_map/ppermute | solution.py:285
  25.1 4.0 %collective-permute-start.2 = (f32[5,8,128]{2,1,0:T(8,128)}, f32[5,8,128]{2,1,0:T(8,128)S(1)}, u32[]{:S(2)}, u32[]{:S(2)}) collective-permute-start(f32[5,8,128]{2,1,0:T(8,128)} %get-tuple-element.36), channel_id=1, source_target_pairs={{0,16},{16,32},{32,48},{48,64},{64,80},{80,96},{96,112},{1,17},{17... | collective-permute-start | bytes 61448 | tf_op jit(solution)/shard_map/ppermute | solution.py:286
  29.0 1.9 %collective-permute-start.3 = (f32[5,8,128]{2,1,0:T(8,128)}, f32[5,8,128]{2,1,0:T(8,128)S(1)}, u32[]{:S(2)}, u32[]{:S(2)}) collective-permute-start(f32[5,8,128]{2,1,0:T(8,128)} %get-tuple-element.37), channel_id=1, source_target_pairs={{16,0},{32,16},{48,32},{64,48},{80,64},{96,80},{112,96},{17,1},{33... | collective-permute-start | bytes 61448 | tf_op jit(solution)/shard_map/ppermute | solution.py:287
  30.9 6.1 %all-to-all-start = ((f32[128,2,128]{2,1,0:T(2,128)}), f32[128,2,128]{2,1,0:T(2,128)S(1)}, u32[]{:S(2)}, u32[]{:S(2)}) async-start(f32[128,2,128]{2,1,0:T(2,128)} %get-tuple-element.32), calls=%async_computation | async-start | bytes 262144 | tf_op jit(solution)/shard_map/all_to_all | solution.py:770
  37.1 0.7 reshape.29.blade_m
  37.7 0.7 reshape.30.back_m
  38.4 0.0 collective-permute-done.2.from_west
  38.4 0.0 collective-permute-done.3.from_east
  38.4 0.0 copy-start.6
  38.5 0.0 collective-permute-done.1.from_high
  38.5 0.5 copy-done.12
  39.0 0.0 copy-done.14
  39.0 0.1 copy-done.6
  39.1 0.1 copy-done.8
  39.2 9.3 %cotangent.1 = (f32[128,8,128]{2,1,0:T(8,128)}, f32[17,256,128]{2,1,0:T(8,128)}, f32[17,64,128]{2,1,0:T(8,128)}, s32[2,1,1024]{2,1,0:T(1,128)}, s32[2,1,2048]{2,1,0:T(1,128)}) custom-call(s32[1]{0:T(128)} %bitcast.place, f32[3,25]{1,0:T(4,128)} %reshape.29.blade_m, f32[3,25]{1,0:T(4,128)} %reshape.30.back_m, f32[5,256,128]{2,1,0:T(8,128)} %bitcast.7, ...), custom_call_target="tpu_custom_call" | custom-call | flops 2000000000 | bytes 4604508 | tf_op jit(solution)/shard_map/cotangent/pallas_call | solution.py:758
  48.5 0.0 all-to-all-done.recv
  48.5 9.8 %all-to-all-start.1 = ((f32[128,8,128]{2,1,0:T(8,128)}), f32[128,8,128]{2,1,0:T(8,128)S(1)}, u32[]{:S(2)}, u32[]{:S(2)}) async-start(f32[128,8,128]{2,1,0:T(8,128)} %get-tuple-element.48), calls=%async_computation.1 | async-start | bytes 1048576 | tf_op jit(solution)/shard_map/all_to_all | solution.py:770
  58.3 0.6 fusion.3
  58.9 4.8 %fill.1 = (f32[5,256,128]{2,1,0:T(8,128)}, f32[5,64,128]{2,1,0:T(8,128)}, f32[5,72,128]{2,1,0:T(8,128)}, f32[5,72,128]{2,1,0:T(8,128)}, f32[5,8,128]{2,1,0:T(8,128)}, /*index=5*/f32[5,8,128]{2,1,0:T(8,128)}) custom-call(f32[5,256,128]{2,1,0:T(8,128)} %bitcast.9, f32[5,64,128]{2,1,0:T(8,128)} %get-tuple-element.31.back_planes, f32[128,2,128]{2,1,0:T(2,128)} %copy-done.1, ...), custom_call_target="tpu_custom_call" | custom-call | flops 1000000000 | bytes 2236416 | tf_op jit(solution)/shard_map/fill/pallas_call | solution.py:758
  63.8 1.4 collective-permute-start.4
  65.1 4.3 %collective-permute-start.5 = (f32[5,72,128]{2,1,0:T(8,128)}, f32[5,72,128]{2,1,0:T(8,128)S(1)}, u32[]{:S(2)}, u32[]{:S(2)}) collective-permute-start(f32[5,72,128]{2,1,0:T(8,128)} %get-tuple-element.43), channel_id=1, source_target_pairs={{1,0},{2,1},{3,2},{4,3},{5,4},{6,5},{7,6},{8,7},{9,8},{10,9},{11,1... | collective-permute-start | bytes 552968 | tf_op jit(solution)/shard_map/ppermute | solution.py:285
  69.4 3.6 %collective-permute-start.6 = (f32[5,8,128]{2,1,0:T(8,128)}, f32[5,8,128]{2,1,0:T(8,128)S(1)}, u32[]{:S(2)}, u32[]{:S(2)}) collective-permute-start(f32[5,8,128]{2,1,0:T(8,128)} %get-tuple-element.44), channel_id=1, source_target_pairs={{0,16},{16,32},{32,48},{48,64},{64,80},{80,96},{96,112},{1,17},{17... | collective-permute-start | bytes 61448 | tf_op jit(solution)/shard_map/ppermute | solution.py:286
  73.0 1.9 %collective-permute-start.7 = (f32[5,8,128]{2,1,0:T(8,128)}, f32[5,8,128]{2,1,0:T(8,128)S(1)}, u32[]{:S(2)}, u32[]{:S(2)}) collective-permute-start(f32[5,8,128]{2,1,0:T(8,128)} %get-tuple-element.45), channel_id=1, source_target_pairs={{16,0},{32,16},{48,32},{64,48},{80,64},{96,80},{112,96},{17,1},{33... | collective-permute-start | bytes 61448 | tf_op jit(solution)/shard_map/ppermute | solution.py:287
  75.0 0.0 collective-permute-done.6.from_west
  75.0 3.4 %collective-permute-done.7.from_east = f32[5,8,128]{2,1,0:T(8,128)S(1)} collective-permute-done((f32[5,8,128]{2,1,0:T(8,128)}, f32[5,8,128]{2,1,0:T(8,128)S(1)}, u32[]{:S(2)}, u32[]{:S(2)}) %collective-permute-start.7) | collective-permute-done | bytes 20512 | tf_op jit(solution)/shard_map/ppermute | solution.py:287
  78.3 0.0 collective-permute-done.5.from_high
  78.4 0.5 copy-done.13
  78.9 0.1 copy-done.5
  79.0 0.1 copy-done.7
  79.1 0.1 copy-done
  79.2 26.8 %middle.1 = (f32[5,256,128]{2,1,0:T(8,128)}, f32[5,64,128]{2,1,0:T(8,128)}, f32[5,72,128]{2,1,0:T(8,128)}, f32[5,72,128]{2,1,0:T(8,128)}, f32[5,8,128]{2,1,0:T(8,128)}, /*index=5*/f32[5,8,128]{2,1,0:T(8,128)}) custom-call(s32[1]{0:T(128)} %bitcast.place, f32[3,25]{1,0:T(4,128)} %reshape.29.blade_m, f32[3,25]{1,0:T(4,128)} %reshape.30.back_m, ...), custom_call_target="tpu_custom_call" | custom-call | flops 10000000000 | bytes 5997148 | tf_op jit(solution)/shard_map/middle/pallas_call | solution.py:758
  106.0 0.1 collective-permute-start.8
  106.1 4.8 %collective-permute-start.9 = (f32[5,72,128]{2,1,0:T(8,128)}, f32[5,72,128]{2,1,0:T(8,128)S(1)}, u32[]{:S(2)}, u32[]{:S(2)}) collective-permute-start(f32[5,72,128]{2,1,0:T(8,128)} %get-tuple-element.52), channel_id=1, source_target_pairs={{1,0},{2,1},{3,2},{4,3},{5,4},{6,5},{7,6},{8,7},{9,8},{10,9},{11,1... | collective-permute-start | bytes 552968 | tf_op jit(solution)/shard_map/ppermute | solution.py:285
  110.9 2.5 %collective-permute-start.10 = (f32[5,8,128]{2,1,0:T(8,128)}, f32[5,8,128]{2,1,0:T(8,128)S(1)}, u32[]{:S(2)}, u32[]{:S(2)}) collective-permute-start(f32[5,8,128]{2,1,0:T(8,128)} %get-tuple-element.53), channel_id=1, source_target_pairs={{0,16},{16,32},{32,48},{48,64},{64,80},{80,96},{96,112},{1,17},{17... | collective-permute-start | bytes 61448 | tf_op jit(solution)/shard_map/ppermute | solution.py:286
  113.4 2.1 %collective-permute-start.11 = (f32[5,8,128]{2,1,0:T(8,128)}, f32[5,8,128]{2,1,0:T(8,128)S(1)}, u32[]{:S(2)}, u32[]{:S(2)}) collective-permute-start(f32[5,8,128]{2,1,0:T(8,128)} %get-tuple-element.54), channel_id=1, source_target_pairs={{16,0},{32,16},{48,32},{64,48},{80,64},{96,80},{112,96},{17,1},{33... | collective-permute-start | bytes 61448 | tf_op jit(solution)/shard_map/ppermute | solution.py:287
  115.5 3.1 %collective-permute-done.11.from_east = f32[5,8,128]{2,1,0:T(8,128)S(1)} collective-permute-done((f32[5,8,128]{2,1,0:T(8,128)}, f32[5,8,128]{2,1,0:T(8,128)S(1)}, u32[]{:S(2)}, u32[]{:S(2)}) %collective-permute-start.11) | collective-permute-done | bytes 20512 | tf_op jit(solution)/shard_map/ppermute | solution.py:287
  118.7 0.6 copy-done.16
  119.3 0.1 copy-done.9
  119.4 0.1 copy-done.10
  119.5 6.1 %last.1 = (f32[128,2,128]{2,1,0:T(2,128)}, f32[5,256,128]{2,1,0:T(8,128)}, f32[5,64,128]{2,1,0:T(8,128)}) custom-call(s32[1]{0:T(128)} %bitcast.place, f32[3,25]{1,0:T(4,128)} %reshape.29.blade_m, f32[3,25]{1,0:T(4,128)} %reshape.30.back_m, f32[5,256,128]{2,1,0:T(8,128)} %get-tuple-element.40.blade_first, f32[5,64,128]{2,1,0:T(8,128)} %get-tuple-element.41.back_first, ...), custom_call_target="tpu_custom_call" | custom-call | flops 1000000000 | bytes 3056220 | tf_op jit(solution)/shard_map/last/pallas_call | solution.py:758
  125.6 16.6 %all_to_all.15.recv = f32[128,2,128]{2,1,0:T(2,128)} all-to-all(f32[128,2,128]{2,1,0:T(2,128)} %get-tuple-element.57), channel_id=1, replica_groups=mesh['gx'=8,'gy'=16] {'gx','gy'}, dimensions={0} | all-to-all | bytes 262144 | tf_op jit(solution)/shard_map/all_to_all | solution.py:770
  142.1 15.8 %end.1 = (f32[5,256,128]{2,1,0:T(8,128)}, f32[5,16,512]{2,1,0:T(8,128)}) custom-call(f32[5,256,128]{2,1,0:T(8,128)} %get-tuple-element.55.blade_kept, f32[5,64,128]{2,1,0:T(8,128)} %get-tuple-element.56.back_kept, f32[128,2,128]{2,1,0:T(2,128)} %all_to_all.15.recv, s32[1,2048]{1,0:T(1,128)} %get-tuple-element.73.back_base, ...), custom_call_target="tpu_custom_call" | custom-call | flops 5000000000 | bytes 1990656 | tf_op jit(solution)/shard_map/end/pallas_call | solution.py:758
  (30 shorter events, 0.1 us)
Async XLA Ops:
  6.7 30.3 %copy-start.3 = (f32[3,5,5]{2,0,1:T(4,128)S(1)}, f32[3,5,5]{2,0,1:T(4,128)}, u32[]{:S(2)}) copy-start(f32[3,5,5]{2,0,1:T(4,128)} %param.17) | copy-start | bytes 904
  6.7 31.0 %copy-start.4 = (f32[3,5,5]{2,0,1:T(4,128)S(1)}, f32[3,5,5]{2,0,1:T(4,128)}, u32[]{:S(2)}) copy-start(f32[3,5,5]{2,0,1:T(4,128)} %param.18) | copy-start | bytes 904
  17.9 20.5 %collective-permute-start = (f32[5,72,128]{2,1,0:T(8,128)}, f32[5,72,128]{2,1,0:T(8,128)S(1)}, u32[]{:S(2)}, u32[]{:S(2)}) collective-permute-start(f32[5,72,128]{2,1,0:T(8,128)} %get-tuple-element.34), channel_id=1, source_target_pairs={{0,1},{1,2},{2,3},{3,4},{4,5},{5,6},{6,7},{7,8},{8,9},{9,10},{10,1... | collective-permute-start | bytes 552968 | tf_op jit(solution)/shard_map/ppermute | solution.py:284
  20.1 18.4 %collective-permute-start.1 = (f32[5,72,128]{2,1,0:T(8,128)}, f32[5,72,128]{2,1,0:T(8,128)S(1)}, u32[]{:S(2)}, u32[]{:S(2)}) collective-permute-start(f32[5,72,128]{2,1,0:T(8,128)} %get-tuple-element.35), channel_id=1, source_target_pairs={{1,0},{2,1},{3,2},{4,3},{5,4},{6,5},{7,6},{8,7},{9,8},{10,9},{11,1... | collective-permute-start | bytes 552968 | tf_op jit(solution)/shard_map/ppermute | solution.py:285
  25.1 13.4 %collective-permute-start.2 = (f32[5,8,128]{2,1,0:T(8,128)}, f32[5,8,128]{2,1,0:T(8,128)S(1)}, u32[]{:S(2)}, u32[]{:S(2)}) collective-permute-start(f32[5,8,128]{2,1,0:T(8,128)} %get-tuple-element.36), channel_id=1, source_target_pairs={{0,16},{16,32},{32,48},{48,64},{64,80},{80,96},{96,112},{1,17},{17... | collective-permute-start | bytes 61448 | tf_op jit(solution)/shard_map/ppermute | solution.py:286
  29.0 9.4 %collective-permute-start.3 = (f32[5,8,128]{2,1,0:T(8,128)}, f32[5,8,128]{2,1,0:T(8,128)S(1)}, u32[]{:S(2)}, u32[]{:S(2)}) collective-permute-start(f32[5,8,128]{2,1,0:T(8,128)} %get-tuple-element.37), channel_id=1, source_target_pairs={{16,0},{32,16},{48,32},{64,48},{80,64},{96,80},{112,96},{17,1},{33... | collective-permute-start | bytes 61448 | tf_op jit(solution)/shard_map/ppermute | solution.py:287
  30.9 17.6 %all-to-all-start = ((f32[128,2,128]{2,1,0:T(2,128)}), f32[128,2,128]{2,1,0:T(2,128)S(1)}, u32[]{:S(2)}, u32[]{:S(2)}) async-start(f32[128,2,128]{2,1,0:T(2,128)} %get-tuple-element.32), calls=%async_computation | async-start | bytes 262144 | tf_op jit(solution)/shard_map/all_to_all | solution.py:770
  38.4 0.6 copy-start.12
  38.4 0.6 copy-start.14
  38.4 0.7 copy-start.6
  38.5 0.7 copy-start.8
  39.2 19.1 %copy-start.2 = (s32[2,2048]{1,0:T(2,128)S(1)}, s32[2,2048]{1,0:T(2,128)}, u32[]{:S(2)}) copy-start(s32[2,2048]{1,0:T(2,128)} %hole_cell.1) | copy-start | bytes 49156
  48.5 10.4 %copy-start.1 = (f32[128,2,128]{2,1,0:T(2,128)}, f32[128,2,128]{2,1,0:T(2,128)S(1)}, u32[]{:S(2)}) copy-start(f32[128,2,128]{2,1,0:T(2,128)S(1)} %all-to-all-done.recv) | copy-start | bytes 393220
  48.5 29.9 %all-to-all-start.1 = ((f32[128,8,128]{2,1,0:T(8,128)}), f32[128,8,128]{2,1,0:T(8,128)S(1)}, u32[]{:S(2)}, u32[]{:S(2)}) async-start(f32[128,8,128]{2,1,0:T(8,128)} %get-tuple-element.48), calls=%async_computation.1 | async-start | bytes 1048576 | tf_op jit(solution)/shard_map/all_to_all | solution.py:770
  63.8 14.6 %collective-permute-start.4 = (f32[5,72,128]{2,1,0:T(8,128)}, f32[5,72,128]{2,1,0:T(8,128)S(1)}, u32[]{:S(2)}, u32[]{:S(2)}) collective-permute-start(f32[5,72,128]{2,1,0:T(8,128)} %get-tuple-element.42), channel_id=1, source_target_pairs={{0,1},{1,2},{2,3},{3,4},{4,5},{5,6},{6,7},{7,8},{8,9},{9,10},{10,1... | collective-permute-start | bytes 552968 | tf_op jit(solution)/shard_map/ppermute | solution.py:284
  65.1 13.2 %collective-permute-start.5 = (f32[5,72,128]{2,1,0:T(8,128)}, f32[5,72,128]{2,1,0:T(8,128)S(1)}, u32[]{:S(2)}, u32[]{:S(2)}) collective-permute-start(f32[5,72,128]{2,1,0:T(8,128)} %get-tuple-element.43), channel_id=1, source_target_pairs={{1,0},{2,1},{3,2},{4,3},{5,4},{6,5},{7,6},{8,7},{9,8},{10,9},{11,1... | collective-permute-start | bytes 552968 | tf_op jit(solution)/shard_map/ppermute | solution.py:285
  69.4 5.6 %collective-permute-start.6 = (f32[5,8,128]{2,1,0:T(8,128)}, f32[5,8,128]{2,1,0:T(8,128)S(1)}, u32[]{:S(2)}, u32[]{:S(2)}) collective-permute-start(f32[5,8,128]{2,1,0:T(8,128)} %get-tuple-element.44), channel_id=1, source_target_pairs={{0,16},{16,32},{32,48},{48,64},{64,80},{80,96},{96,112},{1,17},{17... | collective-permute-start | bytes 61448 | tf_op jit(solution)/shard_map/ppermute | solution.py:286
  73.0 5.3 %collective-permute-start.7 = (f32[5,8,128]{2,1,0:T(8,128)}, f32[5,8,128]{2,1,0:T(8,128)S(1)}, u32[]{:S(2)}, u32[]{:S(2)}) collective-permute-start(f32[5,8,128]{2,1,0:T(8,128)} %get-tuple-element.45), channel_id=1, source_target_pairs={{16,0},{32,16},{48,32},{64,48},{80,64},{96,80},{112,96},{17,1},{33... | collective-permute-start | bytes 61448 | tf_op jit(solution)/shard_map/ppermute | solution.py:287
  75.0 3.4 %copy-start.11 = (f32[5,8,128]{2,1,0:T(8,128)}, f32[5,8,128]{2,1,0:T(8,128)S(1)}, u32[]{:S(2)}) copy-start(f32[5,8,128]{2,1,0:T(8,128)S(1)} %collective-permute-done.6.from_west) | copy-start | bytes 61444
  78.3 0.6 copy-start.13
  78.3 0.7 copy-start.5
  78.4 0.8 copy-start.7
  78.4 0.9 copy-start
  106.0 12.7 %collective-permute-start.8 = (f32[5,72,128]{2,1,0:T(8,128)}, f32[5,72,128]{2,1,0:T(8,128)S(1)}, u32[]{:S(2)}, u32[]{:S(2)}) collective-permute-start(f32[5,72,128]{2,1,0:T(8,128)} %get-tuple-element.51), channel_id=1, source_target_pairs={{0,1},{1,2},{2,3},{3,4},{4,5},{5,6},{6,7},{7,8},{8,9},{9,10},{10,1... | collective-permute-start | bytes 552968 | tf_op jit(solution)/shard_map/ppermute | solution.py:284
  106.1 12.6 %collective-permute-start.9 = (f32[5,72,128]{2,1,0:T(8,128)}, f32[5,72,128]{2,1,0:T(8,128)S(1)}, u32[]{:S(2)}, u32[]{:S(2)}) collective-permute-start(f32[5,72,128]{2,1,0:T(8,128)} %get-tuple-element.52), channel_id=1, source_target_pairs={{1,0},{2,1},{3,2},{4,3},{5,4},{6,5},{7,6},{8,7},{9,8},{10,9},{11,1... | collective-permute-start | bytes 552968 | tf_op jit(solution)/shard_map/ppermute | solution.py:285
  110.9 4.7 %collective-permute-start.10 = (f32[5,8,128]{2,1,0:T(8,128)}, f32[5,8,128]{2,1,0:T(8,128)S(1)}, u32[]{:S(2)}, u32[]{:S(2)}) collective-permute-start(f32[5,8,128]{2,1,0:T(8,128)} %get-tuple-element.53), channel_id=1, source_target_pairs={{0,16},{16,32},{32,48},{48,64},{64,80},{80,96},{96,112},{1,17},{17... | collective-permute-start | bytes 61448 | tf_op jit(solution)/shard_map/ppermute | solution.py:286
  113.4 5.3 %collective-permute-start.11 = (f32[5,8,128]{2,1,0:T(8,128)}, f32[5,8,128]{2,1,0:T(8,128)S(1)}, u32[]{:S(2)}, u32[]{:S(2)}) collective-permute-start(f32[5,8,128]{2,1,0:T(8,128)} %get-tuple-element.54), channel_id=1, source_target_pairs={{16,0},{32,16},{48,32},{64,48},{80,64},{96,80},{112,96},{17,1},{33... | collective-permute-start | bytes 61448 | tf_op jit(solution)/shard_map/ppermute | solution.py:287
  115.5 3.2 %copy-start.15 = (f32[5,8,128]{2,1,0:T(8,128)}, f32[5,8,128]{2,1,0:T(8,128)S(1)}, u32[]{:S(2)}) copy-start(f32[5,8,128]{2,1,0:T(8,128)S(1)} %collective-permute-done.10.from_west) | copy-start | bytes 61444
  118.7 0.6 copy-start.16
  118.7 0.7 copy-start.9
  118.7 0.8 copy-start.10

commit v2 on v1

v2 whole, which is shorter than its diff:
```python
import jax
import jax.numpy as jnp
from jax import lax
from jax.experimental import pallas as pl
from jax.experimental.pallas import tpu as pltpu
from jax.sharding import PartitionSpec as P


DEVS = 128
WRAP = 4
WALL = 64
CHORD = 128
EAST = 16
NORTH = 8
VERT = 64
HALF = VERT // 2
RIMS = 1024
HOLES = 2048
QR = 2 * RIMS // DEVS
QH = 2 * HOLES // DEVS
FIELDS = 17

time_step = 0.2
damping = 0.1

F32 = jnp.float32
BF16 = jnp.bfloat16


def split(x):
    hi = x.astype(BF16)
    return hi, (x - hi.astype(F32)).astype(BF16)


def dot_nn(a, b):
    return lax.dot_general(a, b, (((1,), (0,)), ((), ())), preferred_element_type=F32)


def dot_nt(a, b):
    return lax.dot_general(a, b, (((1,), (1,)), ((), ())), preferred_element_type=F32)


def iota(shape, dim):
    return lax.broadcasted_iota(jnp.int32, shape, dim)


def one_hot(rows, index):
    return jnp.where(iota((rows, index.shape[1]), 0) == index, 1.0, 0.0)


def pair_hot(rows, index, first, second):
    position = iota((rows, index.shape[1]), 0)
    return jnp.where(position == index, first, jnp.where(position == index + 1, second, 0.0))


def lane_roll(x, amount):
    amount = amount % x.shape[-1]
    return pltpu.roll(x, amount, x.ndim - 1) if amount else x


def to_planes(block):
    rows = [block[:, y * VERT : (y + 1) * VERT] for y in range(NORTH)]
    return jnp.concatenate(rows, axis=0).T


def from_planes(field):
    turned = field.T
    return [turned[y * EAST : (y + 1) * EAST, :] for y in range(NORTH)]


def donor_parts(weights):
    w = [weights[corner : corner + 1, :] for corner in range(8)]
    x0 = (w[0] + w[1]) + (w[2] + w[3])
    x1 = (w[4] + w[5]) + (w[6] + w[7])
    y0 = (w[0] + w[1]) + (w[4] + w[5])
    y1 = (w[2] + w[3]) + (w[6] + w[7])
    z0 = (w[0] + w[2]) + (w[4] + w[6])
    z1 = (w[1] + w[3]) + (w[5] + w[7])
    return x0, x1, y0, y1, z0, z1


def short_marks(size, index):
    position = iota((size, index.shape[1]), 0).astype(jnp.int16)
    return position == index.astype(jnp.int16), position == (index + 1).astype(jnp.int16)


def pair_split(marks, first, second):
    (first_hi, first_lo), (second_hi, second_lo) = split(first), split(second)
    zero = jnp.zeros((), BF16)

    def place(a, b):
        return jnp.where(marks[0], a, jnp.where(marks[1], b, zero))

    return place(first_hi, second_hi), place(first_lo, second_lo)


def donor_rows(outer, outer_index, outer_pair, inner, inner_index, inner_pair):
    hot = pair_hot(outer, outer_index, *outer_pair)
    marks = short_marks(inner, inner_index)
    parts = [
        pair_split(marks, hot[n : n + 1, :] * inner_pair[0], hot[n : n + 1, :] * inner_pair[1])
        for n in range(outer)
    ]
    return tuple(jnp.concatenate([p[k] for p in parts], axis=0) for k in range(2))


def blade_donors(base, weights):
    x0, x1, y0, y1, z0, z1 = donor_parts(weights)
    wall = (base >> 7) & (WALL - 1)
    rows = donor_rows(WRAP, base >> 13, (x0, x1), WALL, wall, (y0, y1))
    return rows, (CHORD, base & (CHORD - 1), z0, z1)


def back_donors(base, weights):
    x0, x1, y0, y1, z0, z1 = donor_parts(weights)
    north = (base >> 6) & (NORTH - 1)
    rows = donor_rows(NORTH, north, (y0, y1), EAST, base >> 9, (x0, x1))
    return rows, (HALF, (base & (VERT - 1)) - HALF, z0, z1)


def triple_rows(rows):
    hi, lo = rows
    return jnp.concatenate([hi, lo, hi], axis=0)


def triple_lanes(rows):
    hi, lo = rows
    return jnp.concatenate([hi, hi, lo], axis=1)


def store_parts(target, place, size, field):
    hi, lo = split(field)
    rows = slice(place, place + size)
    target[rows, :] = jnp.concatenate([hi, hi, lo], axis=1)


def picked(parts, rows, cols):
    size = cols[0]
    hot = pair_hot(*cols)
    table = dot_nn(parts[...], triple_rows(rows))
    return [
        jnp.sum(table[c * size : (c + 1) * size] * hot, axis=0, keepdims=True) for c in range(5)
    ]


def spread_terms(rows, cols, mu):
    size, index, first, second = cols
    pairs = [(first * mu[c], second * mu[c]) for c in range(5)]
    tiles = {c: [] for c in range(5)}
    for start in range(0, size, 16):
        marks = short_marks(16, index - start)
        for c in range(5):
            tiles[c].append(pair_split(marks, *pairs[c]))
    hi, lo = (
        jnp.concatenate([t[k] for c in range(5) for t in tiles[c]], axis=0) for k in range(2)
    )
    return dot_nt(jnp.concatenate([hi, lo, hi], axis=1), triple_lanes(rows))


def exact_nt(terms, marks):
    hi, lo = split(terms)
    return dot_nt(jnp.concatenate([hi, lo], axis=1), jnp.concatenate([marks, marks], axis=1))


def doubled(field):
    hi, lo = split(field)
    return jnp.concatenate([hi, lo], axis=1)


def twice(marks):
    return jnp.concatenate([marks, marks], axis=0)


def wall_shift(v, up):
    position = iota(v.shape, 0)
    if up:
        return jnp.where(position == v.shape[0] - 1, 0.0, pltpu.roll(v, v.shape[0] - 1, 0))
    return jnp.where(position == 0, 0.0, pltpu.roll(v, 1, 0))


def lane_shift(v, up, width, period, fill):
    place = (iota(v.shape, 1) // width) % period
    if up:
        return jnp.where(place == period - 1, fill, lane_roll(v, -width))
    return jnp.where(place == 0, fill, lane_roll(v, width))


def flux_of(m_ref, t, v):
    out = []
    half = 0.5 * time_step * v[1 + t]
    for c in range(5):
        total = half * v[c]
        for e in range(5):
            total = total + m_ref[t, c * 5 + e] * v[e]
        out.append(total)
    return out


def turned_of(m_ref, t, w):
    out = []
    for c in range(5):
        total = m_ref[t, c] * w[0]
        for e in range(1, 5):
            total = total + m_ref[t, e * 5 + c] * w[e]
        out.append(total)
    return out


PAIRS = [(0, 1), (0, 2), (0, 3), (4, 1), (4, 2), (4, 3), (1, 1), (1, 2), (1, 3), (2, 2), (2, 3), (3, 3)]


def linear_fields(m_ref, center, sides):
    base = [center[c] * (1.0 - 6.0 * damping * time_step) for c in range(5)]
    jumps = []
    for t, (upper, lower) in enumerate(sides):
        jump = [0.5 * time_step * (lower[c] - upper[c]) for c in range(5)]
        turned = turned_of(m_ref, t, jump)
        for c in range(5):
            base[c] = base[c] - turned[c] + damping * time_step * (upper[c] + lower[c])
        jumps.append(jump)
    out = list(base)
    for a, b in PAIRS:
        if a in (0, 4):
            out.append(jumps[b - 1][a])
        else:
            out.append(jumps[a - 1][b] + jumps[b - 1][a])
    return out


def apply_fields(fields, v):
    out = []
    table = {pair: 5 + n for n, pair in enumerate(PAIRS)}
    for c in range(5):
        total = fields[c]
        for e in range(5):
            key = (c, e) if (c, e) in table else (e, c)
            if key in table:
                total = total - fields[table[key]] * v[e]
        out.append(total)
    return out


def adjoint_at(m_ref, v, center, sides):
    out = [center[c] * (1.0 - 6.0 * damping * time_step) for c in range(5)]
    for t, (upper, lower) in enumerate(sides):
        jump = [0.5 * time_step * (lower[c] - upper[c]) for c in range(5)]
        turned = turned_of(m_ref, t, jump)
        inner = v[0] * jump[0]
        for e in range(1, 5):
            inner = inner + v[e] * jump[e]
        for c in range(5):
            total = turned[c] + v[1 + t] * jump[c]
            if c == 1 + t:
                total = total + inner
            out[c] = out[c] - total + damping * time_step * (upper[c] + lower[c])
    return out


def blade_sides(ref, low, high, j, part=slice(0, WALL)):
    def plane(n):
        if n < 0 or n >= WRAP:
            return [v[part, :] for v in (low if n < 0 else high)]
        rows = slice(n * WALL + part.start, n * WALL + part.stop)
        return [ref[c, rows, :] for c in range(5)]

    center, above, below = plane(j), plane(j + 1), plane(j - 1)
    wall = ([wall_shift(v, True) for v in center], [wall_shift(v, False) for v in center])
    span = (
        [lane_shift(v, True, 1, CHORD, 0.0) for v in center],
        [lane_shift(v, False, 1, CHORD, 0.0) for v in center],
    )
    return center, [(above, below), wall, span]


def back_sides(center, halo):
    east = (
        [lane_shift(v, True, 1, EAST, halo[1][c]) for c, v in enumerate(center)],
        [lane_shift(v, False, 1, EAST, halo[0][c]) for c, v in enumerate(center)],
    )
    north = (
        [lane_shift(v, True, EAST, NORTH, halo[3][c]) for c, v in enumerate(center)],
        [lane_shift(v, False, EAST, NORTH, halo[2][c]) for c, v in enumerate(center)],
    )
    vert = ([wall_shift(v, True) for v in center], [wall_shift(v, False) for v in center])
    return [east, north, vert]


def pack_east(v, x):
    lane = iota((8, DEVS), 1)
    out = jnp.zeros((8, DEVS), F32)
    for g in range(8):
        out = jnp.where(lane % EAST == g, lane_roll(v[g * 8 : g * 8 + 8, :], g - x), out)
    return out


def unpack_east(v, x):
    return jnp.concatenate([lane_roll(v, x - g) for g in range(8)], axis=0)


def pack_north(v, y):
    lane = iota((8, DEVS), 1)
    out = jnp.zeros((8, DEVS), F32)
    for g in range(8):
        out = jnp.where(lane // EAST == g, lane_roll(v[g * 8 : g * 8 + 8, :], (g - y) * EAST), out)
    return out


def unpack_north(v, y):
    return jnp.concatenate([lane_roll(v, (y - g) * EAST) for g in range(8)], axis=0)


def store_edges(place_ref, blade_at, back, edges):
    first_y, second_y, first_x, second_x = edges
    even_y = place_ref[0] % 2 == 0
    even_x = place_ref[1] % 2 == 0
    for c in range(5):
        high, low = blade_at(c, (WRAP - 1) * WALL), blade_at(c, 0)
        first_y[c, :WALL, :] = jnp.where(even_y, high, low)
        second_y[c, :WALL, :] = jnp.where(even_y, low, high)
        high, low = pack_north(back[c], NORTH - 1), pack_north(back[c], 0)
        first_y[c, WALL:, :] = jnp.where(even_y, high, low)
        second_y[c, WALL:, :] = jnp.where(even_y, low, high)
        high, low = pack_east(back[c], EAST - 1), pack_east(back[c], 0)
        first_x[c] = jnp.where(even_x, high, low)
        second_x[c] = jnp.where(even_x, low, high)


EDGE_SHAPES = [
    jax.ShapeDtypeStruct((5, WALL + 8, CHORD), F32),
    jax.ShapeDtypeStruct((5, WALL + 8, CHORD), F32),
    jax.ShapeDtypeStruct((5, 8, DEVS), F32),
    jax.ShapeDtypeStruct((5, 8, DEVS), F32),
]


def read_halo(place_ref, first_y, second_y, first_x, second_x):
    north = place_ref[0]
    even_y = north % 2 == 0
    even_x = place_ref[1] % 2 == 0
    keep_low = jnp.where(north > 0, 1.0, 0.0)
    keep_high = jnp.where(north < DEVS // 8 - 1, 1.0, 0.0)
    both = [(first_y[c], second_y[c]) for c in range(5)]
    above = [jnp.where(even_y, a, b) for a, b in both]
    below = [jnp.where(even_y, b, a) for a, b in both]
    both = [(first_x[c], second_x[c]) for c in range(5)]
    east = [unpack_east(jnp.where(even_x, a, b), EAST - 1) for a, b in both]
    west = [unpack_east(jnp.where(even_x, b, a), 0) for a, b in both]
    south = [unpack_north(v[WALL:, :] * keep_low, 0) for v in below]
    upper = [unpack_north(v[WALL:, :] * keep_high, NORTH - 1) for v in above]
    return [v[:WALL, :] for v in below], [v[:WALL, :] for v in above], [west, east, south, upper]


def exchange(edges):
    gx, gy = lax.axis_size("gx"), lax.axis_size("gy")

    def pairs(start, stop, count):
        there = [(i, (i + 1) % count) for i in range(start, stop, 2)]
        return there + [(b, a) for a, b in there]

    first_y, second_y, first_x, second_x = edges
    got_y = lax.ppermute(first_y, "gy", pairs(0, gy, gy))
    got_x = lax.ppermute(first_x, "gx", pairs(0, gx, gx))
    got_x2 = lax.ppermute(second_x, "gx", pairs(1, gx - 1, gx))
    got_y2 = lax.ppermute(second_y, "gy", pairs(1, gy, gy))
    return got_y, got_y2, got_x, got_x2


def regroup(pieces, width):
    count = DEVS // width
    shape = next(piece.shape for piece in pieces if piece is not None)
    block = iota(shape, 1) // width
    out = []
    for b in range(count):
        total = jnp.zeros(shape, F32)
        for a in range(count):
            if pieces[a] is not None:
                total = jnp.where(block == a, lane_roll(pieces[a], (a - b) * width), total)
        out.append(total)
    return out


def ranks_of(owner_ref, out_ref):
    count = owner_ref.shape[1]
    earlier = jnp.where(iota((256, 256), 0) < iota((256, 256), 1), 1.0, 0.0).astype(BF16)
    carry = jnp.zeros((DEVS, 1), F32)
    for start in range(0, count, 256):
        marks = one_hot(DEVS, owner_ref[:, start : start + 256])
        before = dot_nn(marks.astype(BF16), earlier) + carry
        out_ref[:, start : start + 256] = jnp.sum(marks * before, axis=0, keepdims=True).astype(
            jnp.int32
        )
        carry = carry + jnp.sum(marks, axis=1, keepdims=True)


def send_rows(values, owner, rank, slots):
    seats = one_hot(slots, rank)
    terms = jnp.concatenate([seats * v for v in values], axis=0)
    return exact_nt(terms, one_hot(DEVS, owner).astype(BF16))


def hole_parts(cell):
    row = ((cell >> 6) & (NORTH - 1)) * EAST + (cell >> 9)
    return row, cell & (VERT - 1)


def hole_values(low_half, cell):
    row, vert = hole_parts(cell)
    seats = one_hot(HALF, vert)
    table = dot_nn(low_half, twice(one_hot(DEVS, row).astype(BF16)))
    return [
        jnp.sum(table[n : n + HALF] * seats, axis=0, keepdims=True)
        for n in range(0, table.shape[0], HALF)
    ]


def hole_mask(cell_ref):
    total = jnp.zeros((HALF, DEVS), F32)
    for start in range(0, HOLES, 512):
        row, vert = hole_parts(cell_ref[:, start : start + 512])
        total = total + dot_nt(one_hot(HALF, vert).astype(BF16), one_hot(DEVS, row).astype(BF16))
    return total


CHUNK = 512


def chunk_lanes(n):
    return pl.ds(pl.multiple_of(n * CHUNK, CHUNK), CHUNK)


def lanes_of(ref, n, k):
    count = CHUNK // DEVS
    return jnp.concatenate([ref[k, pl.ds(n * count + m, 1), :] for m in range(count)], axis=1)


def store_chunk(out, n, values):
    for c in range(5):
        for m in range(CHUNK // DEVS):
            row = pl.ds(n * (CHUNK // DEVS) + m, 1)
            out[c, row, :] = values[c][:, m * DEVS : (m + 1) * DEVS]


def edge_kernel(place, cot, back_cot, cot_planes, first_y, second_y, first_x, second_x):
    cots = []
    for c in range(5):
        turned = to_planes(back_cot[c])
        cot_planes[c] = turned
        cots.append(turned)
    store_edges(
        place, lambda c, r: cot[c, r : r + WALL, :], cots, (first_y, second_y, first_x, second_x)
    )


def start_kernel(
    blade, back, back_base, back_weight, blade_base, blade_weight,
    send, back_planes,
    blade_parts, back_parts, hole_vals, rim_vals,
):
    for c in range(5):
        store_parts(blade_parts, c * CHORD, CHORD, blade[c].T)
        field = to_planes(back[c])
        back_planes[c] = field
        store_parts(back_parts, c * HALF, HALF, field[HALF:, :])

    def blade_step(n, carry):
        lanes = chunk_lanes(n)
        rows, cols = blade_donors(blade_base[0:1, lanes], blade_weight[0, :, lanes])
        store_chunk(hole_vals, n, picked(blade_parts, rows, cols))
        return carry

    lax.fori_loop(0, 2 * HOLES // CHUNK, blade_step, 0, unroll=2)

    def back_step(n, carry):
        lanes = chunk_lanes(n)
        rows, cols = back_donors(back_base[0:1, lanes], back_weight[0, :, lanes])
        store_chunk(rim_vals, n, picked(back_parts, rows, cols))
        return carry

    lax.fori_loop(0, 2 * RIMS // CHUNK, back_step, 0)
    store_slots(hole_vals, rim_vals, send)


def store_slots(hole_vals, rim_vals, send):
    first = regroup([hole_vals[c] for c in range(4)], QH)
    fifth = hole_vals[4]
    tail = regroup([fifth, None, None, None], QH)
    for d in range(DEVS // QH):
        send[pl.ds(d, QH, stride=DEVS // QH), 0, :] = first[d]
        send[pl.ds(d, QH, stride=DEVS // QH), 1, :] = tail[d]
    rims = regroup([None, None] + [rim_vals[c] for c in range(5)] + [None], QR)
    lane = iota((QR, DEVS), 1)
    for d in range(DEVS // QR):
        rows = pl.ds(d, QR, stride=DEVS // QR)
        send[rows, 1, :] = jnp.where(lane < QH, send[rows, 1, :], rims[d])


def cot_kernel(
    place, blade_m, back_m, cot, cot_planes, got_y, got_y2, got_x, got_x2,
    rim_owner, hole_owner, hole_cell,
    send, blade_fields, back_fields, rim_rank, hole_rank,
):
    low, high, halo = read_halo(place, got_y, got_y2, got_x, got_x2)
    for j in range(WRAP):
        center, sides = blade_sides(cot, low, high, j)
        fields = linear_fields(blade_m, center, sides)
        for n in range(FIELDS):
            blade_fields[n, j * WALL : (j + 1) * WALL, :] = fields[n]
    center = [cot_planes[c] for c in range(5)]
    fields = linear_fields(back_m, center, back_sides(center, halo))
    for n in range(FIELDS):
        back_fields[n] = fields[n]
    for step in range(2):
        ranks_of(rim_owner.at[step], rim_rank.at[step])
        ranks_of(hole_owner.at[step], hole_rank.at[step])

    total = jnp.zeros((FIELDS * QR, DEVS), F32)
    for j in range(WRAP):
        lanes = slice(j * 256, j * 256 + 256)
        top = j * WALL + WALL - 2
        values = [
            jnp.concatenate(
                [blade_fields[n, top + k : top + k + 1, :] for k in range(2)], axis=1
            )
            for n in range(FIELDS)
        ]
        total = total + send_rows(values, rim_owner[1, :, lanes], rim_rank[1, :, lanes], QR)
    total = jnp.concatenate([total, jnp.zeros((112, DEVS), F32)], axis=0)
    for m in range(3):
        send[:, 5 + m, :] = total[m * DEVS : (m + 1) * DEVS].T
    total = jnp.zeros((FIELDS * QH, DEVS), F32)
    low_half = doubled(jnp.concatenate([back_fields[n, :HALF, :] for n in range(FIELDS)], axis=0))
    for start in range(0, HOLES, 512):
        lanes = slice(start, start + 512)
        values = hole_values(low_half, hole_cell[1:2, lanes])
        total = total + send_rows(values, hole_owner[1, :, lanes], hole_rank[1, :, lanes], QH)
    total = jnp.concatenate([total, jnp.zeros((96, DEVS), F32)], axis=0)
    for m in range(5):
        send[:, m, :] = total[m * DEVS : (m + 1) * DEVS].T


def fill_kernel(
    place, blade, back_planes, recv, rim_owner, hole_owner, rim_rank, hole_rank, hole_cell,
    blade_first, back_first, first_y, second_y, first_x, second_x,
):
    arrived = doubled(jnp.concatenate([recv[:, 0, :].T, recv[:, 1, :].T], axis=0))
    for c in range(5):
        for j in range(WRAP):
            rows = slice(j * WALL, (j + 1) * WALL)
            blade_first[c, rows, :] = blade[c, rows, :]
    base = 5 * QH
    for j in range(WRAP):
        lanes = slice(j * 256, j * 256 + 256)
        marks = one_hot(DEVS, rim_owner[0, :, lanes]).astype(BF16)
        seats = one_hot(QR, rim_rank[0, :, lanes])
        table = dot_nn(arrived[base : base + 5 * QR], twice(marks))
        for c in range(5):
            value = jnp.sum(table[c * QR : (c + 1) * QR] * seats, axis=0, keepdims=True)
            for k in range(2):
                row = j * WALL + WALL - 2 + k
                blade_first[c, row : row + 1, :] = value[:, k * CHORD : (k + 1) * CHORD]
    filled = jnp.zeros((6 * HALF, DEVS), F32)
    for start in range(0, HOLES, 512):
        lanes = slice(start, start + 512)
        marks = one_hot(DEVS, hole_owner[0, :, lanes]).astype(BF16)
        seats = one_hot(QH, hole_rank[0, :, lanes])
        row, vert = hole_parts(hole_cell[0:1, lanes])
        vert_marks = one_hot(HALF, vert)
        table = dot_nn(arrived[:base], twice(marks))
        terms = [
            vert_marks * jnp.sum(table[c * QH : (c + 1) * QH] * seats, axis=0, keepdims=True)
            for c in range(5)
        ]
        terms = jnp.concatenate(terms + [vert_marks], axis=0)
        filled = filled + exact_nt(terms, one_hot(DEVS, row).astype(BF16))
    mask = filled[5 * HALF :]
    backs = []
    for c in range(5):
        top = jnp.where(mask > 0.5, filled[c * HALF : (c + 1) * HALF], back_planes[c, :HALF, :])
        field = jnp.concatenate([top, back_planes[c, HALF:, :]], axis=0)
        back_first[c] = field
        backs.append(field)
    store_edges(
        place,
        lambda c, r: blade_first[c, r : r + WALL, :],
        backs,
        (first_y, second_y, first_x, second_x),
    )


def residual_step(center, halo_flux):
    out = [center[c] * (1.0 - 6.0 * damping * time_step) for c in range(5)]
    for t in range(3):
        upper, lower = halo_flux(t)
        for c in range(5):
            out[c] = out[c] - upper[c] + lower[c]
    return out


def side_terms(m_ref, t, v):
    flux = flux_of(m_ref, t, v)
    damped = [damping * time_step * v[c] for c in range(5)]
    upper = [flux[c] - damped[c] for c in range(5)]
    lower = [flux[c] + damped[c] for c in range(5)]
    return upper, lower


def middle_kernel(
    place, blade_m, back_m, blade_first, back_first, got_y, got_y2, got_x, got_x2,
    blade_fields, back_fields, recv, back_base, back_weight, blade_base, blade_weight, hole_cell,
    blade_mid, back_mid, first_y, second_y, first_x, second_x,
    blade_next, back_next, blade_parts, back_parts, hole_lin, rim_lin, blade_acc, back_acc,
):
    low, high, halo = read_halo(place, got_y, got_y2, got_x, got_x2)

    planes = [low]
    for j in range(WRAP):
        planes.append([blade_first[c, j * WALL : (j + 1) * WALL, :] for c in range(5)])
    planes.append(high)
    turns = [side_terms(blade_m, 0, plane) for plane in planes]
    for j in range(WRAP):
        center = planes[j + 1]

        def around(t, j=j, center=center):
            if t == 0:
                return turns[j + 2][0], turns[j][1]
            upper, lower = side_terms(blade_m, t, center)
            if t == 1:
                return [wall_shift(v, True) for v in upper], [wall_shift(v, False) for v in lower]
            return (
                [lane_shift(v, True, 1, CHORD, 0.0) for v in upper],
                [lane_shift(v, False, 1, CHORD, 0.0) for v in lower],
            )

        out = residual_step(center, around)
        for c in range(5):
            blade_next[c, j * WALL : (j + 1) * WALL, :] = out[c]
    center = [back_first[c] for c in range(5)]

    def across(t):
        upper, lower = side_terms(back_m, t, center)
        if t == 2:
            return [wall_shift(v, True) for v in upper], [wall_shift(v, False) for v in lower]
        width, period = ((1, EAST), (EAST, NORTH))[t]
        below = side_terms(back_m, t, halo[2 * t])[1]
        above = side_terms(back_m, t, halo[2 * t + 1])[0]
        return (
            [lane_shift(upper[c], True, width, period, above[c]) for c in range(5)],
            [lane_shift(lower[c], False, width, period, below[c]) for c in range(5)],
        )

    out = residual_step(center, across)
    for c in range(5):
        back_next[c] = out[c]
        store_parts(back_parts, c * HALF, HALF, out[c][HALF:, :])
        store_parts(blade_parts, c * CHORD, CHORD, blade_next[c].T)

    for j in range(WRAP):
        rows = slice(j * WALL, (j + 1) * WALL)
        v = [blade_next[c, rows, :] for c in range(5)]
        own = apply_fields([blade_fields[n, rows, :] for n in range(FIELDS)], v)
        inside = iota((WALL, CHORD), 0) < WALL - 2
        for c in range(5):
            blade_mid[c, rows, :] = jnp.where(inside, own[c], 0.0)
    mask = hole_mask(hole_cell.at[1:2])
    own = apply_fields([back_fields[n] for n in range(FIELDS)], [back_next[c] for c in range(5)])
    for c in range(5):
        back_mid[c, :HALF, :] = jnp.where(mask > 0.5, 0.0, own[c][:HALF, :])
        back_mid[c, HALF:, :] = own[c][HALF:, :]

    for m in range(5):
        pieces = [recv[pl.ds(d, QH, stride=DEVS // QH), m, :] for d in range(DEVS // QH)]
        for b, piece in enumerate(regroup(pieces, QH)):
            if m * 4 + b < FIELDS:
                hole_lin[m * 4 + b] = piece
    for m in range(3):
        pieces = [recv[pl.ds(d, QR, stride=DEVS // QR), 5 + m, :] for d in range(DEVS // QR)]
        for b, piece in enumerate(regroup(pieces, QR)):
            if m * 8 + b < FIELDS:
                rim_lin[m * 8 + b] = piece

    blade_acc[...] = jnp.zeros(blade_acc.shape, F32)
    back_acc[...] = jnp.zeros(back_acc.shape, F32)

    def blade_step(n, carry):
        lanes = chunk_lanes(n)
        rows, cols = blade_donors(blade_base[1:2, lanes], blade_weight[1, :, lanes])
        value = picked(blade_parts, rows, cols)
        mu = apply_fields([lanes_of(hole_lin, n, k) for k in range(FIELDS)], value)
        blade_acc[...] += spread_terms(rows, cols, mu)
        return carry

    lax.fori_loop(0, 2 * HOLES // CHUNK, blade_step, 0, unroll=2)

    def back_step(n, carry):
        lanes = chunk_lanes(n)
        rows, cols = back_donors(back_base[1:2, lanes], back_weight[1, :, lanes])
        value = picked(back_parts, rows, cols)
        mu = apply_fields([lanes_of(rim_lin, n, k) for k in range(FIELDS)], value)
        back_acc[...] += spread_terms(rows, cols, mu)
        return carry

    lax.fori_loop(0, 2 * RIMS // CHUNK, back_step, 0)
    for c in range(5):
        blade_mid[c] = blade_mid[c] + blade_acc[c * CHORD : (c + 1) * CHORD, :].T
        back_mid[c, HALF:, :] = back_mid[c, HALF:, :] + back_acc[c * HALF : (c + 1) * HALF, :]
    store_edges(
        place,
        lambda c, r: blade_mid[c, r : r + WALL, :],
        [back_mid[c] for c in range(5)],
        (first_y, second_y, first_x, second_x),
    )


def give_kernel(
    place, blade_m, back_m, blade_first, back_first, blade_mid, back_mid,
    got_y, got_y2, got_x, got_x2,
    rim_owner, hole_owner, rim_rank, hole_rank, hole_cell,
    send,
):
    low, high, halo = read_halo(place, got_y, got_y2, got_x, got_x2)
    rims = jnp.zeros((5 * QR, DEVS), F32)
    for j in range(WRAP):
        outer = slice(WALL - 8, WALL)
        rows = slice(j * WALL + WALL - 8, (j + 1) * WALL)
        center, sides = blade_sides(blade_mid, low, high, j, outer)
        out = adjoint_at(blade_m, [blade_first[c, rows, :] for c in range(5)], center, sides)
        values = [jnp.concatenate([out[c][6:7, :], out[c][7:8, :]], axis=1) for c in range(5)]
        lanes = slice(j * 256, j * 256 + 256)
        rims = rims + send_rows(values, rim_owner[0, :, lanes], rim_rank[0, :, lanes], QR)
    part = HALF + 8
    center = [back_mid[c, :part, :] for c in range(5)]
    halo = [[v[:part, :] for v in side] for side in halo]
    out = adjoint_at(
        back_m, [back_first[c, :part, :] for c in range(5)], center, back_sides(center, halo)
    )
    holes = jnp.zeros((5 * QH, DEVS), F32)
    low_half = doubled(jnp.concatenate([out[c][:HALF, :] for c in range(5)], axis=0))
    for start in range(0, HOLES, 512):
        lanes = slice(start, start + 512)
        values = hole_values(low_half, hole_cell[0:1, lanes])
        holes = holes + send_rows(values, hole_owner[0, :, lanes], hole_rank[0, :, lanes], QH)
    rest = jnp.zeros((2 * DEVS - 5 * QH - 5 * QR, DEVS), F32)
    total = jnp.concatenate([holes, rims, rest], axis=0)
    send[:, 0, :] = total[:DEVS].T
    send[:, 1, :] = total[DEVS:].T


def keep_kernel(
    place, blade_m, back_m, blade_first, back_first, blade_mid, back_mid,
    got_y, got_y2, got_x, got_x2, hole_cell,
    blade_kept, back_kept,
):
    low, high, halo = read_halo(place, got_y, got_y2, got_x, got_x2)
    for j in range(WRAP):
        rows = slice(j * WALL, (j + 1) * WALL)
        center, sides = blade_sides(blade_mid, low, high, j)
        out = adjoint_at(blade_m, [blade_first[c, rows, :] for c in range(5)], center, sides)
        inside = iota((WALL, CHORD), 0) < WALL - 2
        for c in range(5):
            blade_kept[c, rows, :] = jnp.where(inside, out[c], 0.0)
    center = [back_mid[c] for c in range(5)]
    out = adjoint_at(back_m, [back_first[c] for c in range(5)], center, back_sides(center, halo))
    mask = hole_mask(hole_cell.at[0:1])
    for c in range(5):
        back_kept[c, :HALF, :] = jnp.where(mask > 0.5, 0.0, out[c][:HALF, :])
        back_kept[c, HALF:, :] = out[c][HALF:, :]


def end_kernel(
    blade_kept, back_kept, recv, back_base, back_weight, blade_base, blade_weight,
    blade_out, back_out, hole_mu, rim_mu, blade_acc, back_acc,
):
    count = DEVS // QH
    pieces = [recv[pl.ds(d, QH, stride=count), 0, :] for d in range(count)]
    for c, piece in enumerate(regroup(pieces, QH)):
        hole_mu[c] = piece
    pieces = [recv[pl.ds(d, QH, stride=count), 1, :] for d in range(count)]
    hole_mu[4] = regroup(pieces, QH)[0]
    count = DEVS // QR
    pieces = [recv[pl.ds(d, QR, stride=count), 1, :] for d in range(count)]
    groups = regroup(pieces, QR)
    for c in range(5):
        rim_mu[c] = groups[QH // QR + c]
    blade_acc[...] = jnp.zeros(blade_acc.shape, F32)
    back_acc[...] = jnp.zeros(back_acc.shape, F32)

    def blade_step(n, carry):
        lanes = chunk_lanes(n)
        rows, cols = blade_donors(blade_base[0:1, lanes], blade_weight[0, :, lanes])
        blade_acc[...] += spread_terms(rows, cols, [lanes_of(hole_mu, n, c) for c in range(5)])
        return carry

    lax.fori_loop(0, 2 * HOLES // CHUNK, blade_step, 0, unroll=2)

    def back_step(n, carry):
        lanes = chunk_lanes(n)
        rows, cols = back_donors(back_base[0:1, lanes], back_weight[0, :, lanes])
        back_acc[...] += spread_terms(rows, cols, [lanes_of(rim_mu, n, c) for c in range(5)])
        return carry

    lax.fori_loop(0, 2 * RIMS // CHUNK, back_step, 0)
    for c in range(5):
        blade_out[c] = blade_kept[c] + blade_acc[c * CHORD : (c + 1) * CHORD, :].T
        top = back_kept[c, HALF:, :] + back_acc[c * HALF : (c + 1) * HALF, :]
        parts = from_planes(jnp.concatenate([back_kept[c, :HALF, :], top], axis=0))
        for y in range(0, NORTH, 2):
            back_out[c, :, y * VERT : (y + 2) * VERT] = jnp.concatenate(parts[y : y + 2], axis=1)


VMEM = pl.BlockSpec(memory_space=pltpu.VMEM)
SMEM = pl.BlockSpec(memory_space=pltpu.SMEM)
BLADE = jax.ShapeDtypeStruct((5, WRAP * WALL, CHORD), F32)
PLANES = jax.ShapeDtypeStruct((5, VERT, DEVS), F32)
DONOR_PARTS = [
    pltpu.VMEM((5 * CHORD, 3 * WRAP * WALL), BF16),
    pltpu.VMEM((5 * HALF, 3 * DEVS), BF16),
]
SUMS = [pltpu.VMEM((5 * CHORD, WRAP * WALL), F32), pltpu.VMEM((5 * HALF, DEVS), F32)]


def run(kernel, args, out_shape, scratch=(), scalars=0, flops=0):
    size = sum(4 * a.size for a in args) + sum(4 * o.size for o in out_shape)
    return pl.pallas_call(
        kernel,
        out_shape=list(out_shape),
        in_specs=[SMEM] * scalars + [VMEM] * (len(args) - scalars),
        out_specs=[VMEM] * len(out_shape),
        scratch_shapes=list(scratch),
        cost_estimate=pl.CostEstimate(flops=flops, bytes_accessed=size, transcendentals=0),
    )(*args)


def swap(rows):
    return lax.all_to_all(rows, ("gx", "gy"), split_axis=0, concat_axis=0, tiled=True)


def body(
    blade_state,
    back_state,
    blade_cotangent,
    back_cotangent,
    blade_flux,
    back_flux,
    blade_owner,
    back_donor_cell,
    back_donor_weight,
    hole_cell,
    hole_owner,
    blade_donor_cell,
    blade_donor_weight,
):
    shape = jax.ShapeDtypeStruct
    place = jnp.stack([lax.axis_index("gy"), lax.axis_index("gx")]).astype(jnp.int32)
    blade = blade_state.reshape(5, WRAP * WALL, CHORD)
    cot = blade_cotangent.reshape(5, WRAP * WALL, CHORD)
    matrices = (blade_flux.reshape(3, 25), back_flux.reshape(3, 25))
    scaled = tuple(0.5 * time_step * m for m in matrices)
    owners = (blade_owner.reshape(2, 1, RIMS), hole_owner.reshape(2, 1, HOLES))
    tables = (back_donor_cell, back_donor_weight, blade_donor_cell, blade_donor_weight)

    cot_planes, *edges = run(
        edge_kernel, (place, cot, back_cotangent), [PLANES] + EDGE_SHAPES, scalars=1
    )
    cot_halo = exchange(edges)
    send, back_planes = run(
        start_kernel,
        (blade, back_state) + tables,
        [shape((DEVS, 2, DEVS), F32), PLANES],
        DONOR_PARTS + [pltpu.VMEM((5, QH, DEVS), F32), pltpu.VMEM((5, QR, DEVS), F32)],
        flops=5 * 10**9,
    )
    recv = swap(send)
    lin_send, blade_fields, back_fields, rim_rank, hole_rank = run(
        cot_kernel,
        (place, *matrices, cot, cot_planes, *cot_halo, *owners, hole_cell),
        [
            shape((DEVS, 8, DEVS), F32),
            shape((FIELDS, WRAP * WALL, CHORD), F32),
            shape((FIELDS, VERT, DEVS), F32),
            shape((2, 1, RIMS), jnp.int32),
            shape((2, 1, HOLES), jnp.int32),
        ],
        scalars=3,
        flops=2 * 10**9,
    )
    lin_recv = swap(lin_send)
    slots = (*owners, rim_rank, hole_rank, hole_cell)
    blade_first, back_first, *edges = run(
        fill_kernel,
        (place, blade, back_planes, recv) + slots,
        [BLADE, PLANES] + EDGE_SHAPES,
        scalars=1,
        flops=10**9,
    )
    first_halo = exchange(edges)
    blade_mid, back_mid, *edges = run(
        middle_kernel,
        (place, *scaled, blade_first, back_first, *first_halo, blade_fields, back_fields)
        + (lin_recv,)
        + tables
        + (hole_cell,),
        [BLADE, PLANES] + EDGE_SHAPES,
        [pltpu.VMEM(BLADE.shape, F32), pltpu.VMEM(PLANES.shape, F32)]
        + DONOR_PARTS
        + [pltpu.VMEM((FIELDS, QH, DEVS), F32), pltpu.VMEM((FIELDS, QR, DEVS), F32)]
        + SUMS,
        scalars=3,
        flops=10**10,
    )
    mid_halo = exchange(edges)
    both = (place, *matrices, blade_first, back_first, blade_mid, back_mid, *mid_halo)
    (send,) = run(give_kernel, both + slots, [shape((DEVS, 2, DEVS), F32)], scalars=3, flops=10**9)
    recv = swap(send)
    blade_kept, back_kept = run(
        keep_kernel, both + (hole_cell,), [BLADE, PLANES], scalars=3, flops=10**9
    )
    blade_last, back_last = run(
        end_kernel,
        (blade_kept, back_kept, recv) + tables,
        [BLADE, shape((5, EAST, NORTH * VERT), F32)],
        [pltpu.VMEM((5, QH, DEVS), F32), pltpu.VMEM((5, QR, DEVS), F32)] + SUMS,
        flops=5 * 10**9,
    )
    return (blade_last.reshape(blade_state.shape), back_last)


def solution(mesh):
    return jax.shard_map(
        body,
        mesh=mesh,
        in_specs=(
            P(None, "gx", "gy"),
            P(None, "gx", "gy"),
            P(None, "gx", "gy"),
            P(None, "gx", "gy"),
            P(),
            P(),
            P(None, ("gx", "gy"), None),
            P(None, ("gx", "gy")),
            P(None, None, ("gx", "gy")),
            P(None, ("gx", "gy")),
            P(None, ("gx", "gy"), None),
            P(None, ("gx", "gy")),
            P(None, None, ("gx", "gy")),
        ),
        out_specs=(P(None, "gx", "gy"), P(None, "gx", "gy")),
        check_vma=False,
    )
```

time: 159 us -> 136 us (0.86)
  blocking collectives: 16.6 us -> 0 us
  Pallas kernels: 74 us -> 63.9 us
  local copies, waits for them, and re-layouts: 10.4 us -> 4.27 us
  starting transfers between devices: 49.5 us -> 54.3 us
  waiting for transfers between devices: 6.54 us -> 10.7 us
    all_to_all x1 -> x0, blocking collectives: 16.6 us -> none  [swap(): lax.all_to_all(rows, ('gx', 'gy'), split_axis=0, concat_axis=0, tiled=True)]
    pallas_call x6 -> x8, Pallas kernels: 74 us -> 63.9 us  [run(): pl.pallas_call(kernel, out_shape=list(out_shape), in_specs=[SMEM] * scala...]
    all_to_all x2 -> x3, starting transfers between devices: 15.9 us -> 23.2 us  [swap(): lax.all_to_all(rows, ('gx', 'gy'), split_axis=0, concat_axis=0, tiled=True)]
    slice x5 -> x0, local copies, waits for them, and re-layouts: 6.7 us -> none  [the longest x1 1.69 us: body(): blade_donor_weight[s:s + 1]]
    all_to_all x2 -> x3, waiting for transfers between devices: 0.01 us -> 5.78 us  [swap(): lax.all_to_all(rows, ('gx', 'gy'), split_axis=0, concat_axis=0, tiled=True)]
    ppermute x12, starting transfers between devices: 33.6 us -> 31.2 us  [the longest x3 14.6 us: exchange(): got_y2 = lax.ppermute(second_y, 'gy', pairs(1, gy, gy))]
    ppermute x12, waiting for transfers between devices: 6.53 us -> 4.92 us  [the longest x3 3.26 us: exchange(): got_y2 = lax.ppermute(second_y, 'gy', pairs(1, gy, gy))]
  transfers between devices with their start and end apart: 14 -> 15, of which waited for: 2 -> 3; matrix products, arithmetic and copies ran while one was open for 1% -> 1% of each run, Pallas kernels for 9% -> 19%
where the time goes in v2:
time: 136 us; the launch traced here: 135 us
  Pallas kernels  63.9 us (47%)
  starting transfers between devices  54.3 us (40%)
  waiting for transfers between devices  10.7 us (8%)
  local copies, waits for them, and re-layouts  4.27 us (3%)
    pallas_call x8, Pallas kernels, run(): pl.pallas_call(kernel, out_shape=list(out_shape), in_specs=[SMEM] * scala...  63.9 us
    all_to_all x3, starting transfers between devices, swap(): lax.all_to_all(rows, ('gx', 'gy'), split_axis=0, concat_axis=0, tiled=True)  23.2 us
    ppermute x3, starting transfers between devices, exchange(): got_y2 = lax.ppermute(second_y, 'gy', pairs(1, gy, gy))  14.6 us
    ppermute x3, starting transfers between devices, exchange(): got_x2 = lax.ppermute(second_x, 'gx', pairs(1, gx - 1, gx))  11.2 us
    all_to_all x3, waiting for transfers between devices, swap(): lax.all_to_all(rows, ('gx', 'gy'), split_axis=0, concat_axis=0, tiled=True)  5.78 us
    ppermute x3, waiting for transfers between devices, exchange(): got_y2 = lax.ppermute(second_y, 'gy', pairs(1, gy, gy))  3.26 us
    unnamed x40, local copies, waits for them, and re-layouts  2.94 us
    ppermute x3, starting transfers between devices, exchange(): got_y = lax.ppermute(first_y, 'gy', pairs(0, gy, gy))  2.73 us
  transfers between devices with their start and end apart: 15, of which 3 were waited for; matrix products, arithmetic and copies ran while one was open for 1% of the time, Pallas kernels for 19%

profile of v2, /device:TPU:1, one launch (start us, length us, event | category | flops | bytes accessed | tf_op | source)
XLA Modules:
  0.0 135.3 jit_solution(15175596689887703271)
XLA Ops:
  0.6 0.6 pad_add_fusion.place
  1.2 2.3 %shard_map.141 = (f32[5,64,128]{2,1,0:T(8,128)}, f32[5,72,128]{2,1,0:T(8,128)}, f32[5,72,128]{2,1,0:T(8,128)}, f32[5,8,128]{2,1,0:T(8,128)}, f32[5,8,128]{2,1,0:T(8,128)}) custom-call(s32[2]{0:T(128)} %pad_add_fusion.place, f32[5,256,128]{2,1,0:T(8,128)} %bitcast.7, f32[5,16,512]{2,1,0:T(8,128)} %back_cot.1), custom_call_target="tpu_custom_call" | custom-call | bytes 1392648 | tf_op jit(solution)/shard_map/pallas_call | solution.py:823
  3.5 1.4 %collective-permute-start.2 = (f32[5,8,128]{2,1,0:T(8,128)}, f32[5,8,128]{2,1,0:T(8,128)S(1)}, u32[]{:S(2)}, u32[]{:S(2)}) collective-permute-start(f32[5,8,128]{2,1,0:T(8,128)} %get-tuple-element.35), channel_id=1, source_target_pairs={{0,16},{32,48},{64,80},{96,112},{16,0},{48,32},{80,64},{112,96},{1... | collective-permute-start | bytes 61448 | tf_op jit(solution)/shard_map/ppermute | solution.py:362
  4.9 3.1 %collective-permute-start.3 = (f32[5,8,128]{2,1,0:T(8,128)}, f32[5,8,128]{2,1,0:T(8,128)S(1)}, u32[]{:S(2)}, u32[]{:S(2)}) collective-permute-start(f32[5,8,128]{2,1,0:T(8,128)} %get-tuple-element.36), channel_id=1, source_target_pairs={{16,32},{48,64},{80,96},{32,16},{64,48},{96,80},{17,33},{49,65},{8... | collective-permute-start | bytes 61448 | tf_op jit(solution)/shard_map/ppermute | solution.py:363
  8.0 1.4 %collective-permute-start = (f32[5,72,128]{2,1,0:T(8,128)}, f32[5,72,128]{2,1,0:T(8,128)S(1)}, u32[]{:S(2)}, u32[]{:S(2)}) collective-permute-start(f32[5,72,128]{2,1,0:T(8,128)} %get-tuple-element.33), channel_id=1, source_target_pairs={{0,1},{2,3},{4,5},{6,7},{8,9},{10,11},{12,13},{14,15},{1,0},{3,2},... | collective-permute-start | bytes 552968 | tf_op jit(solution)/shard_map/ppermute | solution.py:361
  9.4 5.4 %collective-permute-start.1 = (f32[5,72,128]{2,1,0:T(8,128)}, f32[5,72,128]{2,1,0:T(8,128)S(1)}, u32[]{:S(2)}, u32[]{:S(2)}) collective-permute-start(f32[5,72,128]{2,1,0:T(8,128)} %get-tuple-element.34), channel_id=1, source_target_pairs={{1,2},{3,4},{5,6},{7,8},{9,10},{11,12},{13,14},{15,0},{2,1},{4,3},... | collective-permute-start | bytes 552968 | tf_op jit(solution)/shard_map/ppermute | solution.py:364
  14.8 8.9 %shard_map.140 = (f32[128,2,128]{2,1,0:T(2,128)}, f32[5,64,128]{2,1,0:T(8,128)}) custom-call(f32[5,256,128]{2,1,0:T(8,128)} %bitcast.9, f32[5,16,512]{2,1,0:T(8,128)} %back.1, s32[2,2048]{1,0:T(2,128)} %back_base.5, f32[2,8,2048]{2,1,0:T(8,128)} %back_weight.5, s32[2,4096]{1,0:T(2,128)} %blade_base.5, f32[2,8,4096]{2,1,0:T(8,128)} %blade_weight.5), custom_call_target="tpu_custom_call" | custom-call | flops 5000000000 | bytes 1556480 | tf_op jit(solution)/shard_map/pallas_call | solution.py:823
  23.7 5.4 %all-to-all-start = ((f32[128,2,128]{2,1,0:T(2,128)}), f32[128,2,128]{2,1,0:T(2,128)S(1)}, u32[]{:S(2)}, u32[]{:S(2)}) async-start(f32[128,2,128]{2,1,0:T(2,128)} %get-tuple-element.31), calls=%async_computation | async-start | bytes 262144 | tf_op jit(solution)/shard_map/all_to_all | solution.py:834
  29.1 0.7 reshape.25.blade_m
  29.8 0.7 reshape.26.back_m
  30.5 0.0 collective-permute-done.2.got_x
  30.5 0.0 collective-permute-done.3.got_x2
  30.5 0.0 collective-permute-done.got_y
  30.5 0.0 copy-start.8
  30.5 0.0 collective-permute-done.1.got_y2
  30.5 0.6 copy-done.13
  31.1 0.1 copy-done.8
  31.2 0.0 copy-done.11
  31.2 8.1 %shard_map.142 = (f32[128,8,128]{2,1,0:T(8,128)}, f32[17,256,128]{2,1,0:T(8,128)}, f32[17,64,128]{2,1,0:T(8,128)}, s32[2,1,1024]{2,1,0:T(1,128)}, s32[2,1,2048]{2,1,0:T(1,128)}) custom-call(s32[2]{0:T(128)} %pad_add_fusion.place, f32[3,25]{1,0:T(4,128)} %reshape.25.blade_m, f32[3,25]{1,0:T(4,128)} %reshape.26.back_m, f32[5,256,128]{2,1,0:T(8,128)} %bitcast.8, ...), custom_call_target="tpu_custom_call" | custom-call | flops 2000000000 | bytes 4604512 | tf_op jit(solution)/shard_map/pallas_call | solution.py:823
  39.3 0.0 all-to-all-done.recv
  39.3 9.8 %all-to-all-start.1 = ((f32[128,8,128]{2,1,0:T(8,128)}), f32[128,8,128]{2,1,0:T(8,128)S(1)}, u32[]{:S(2)}, u32[]{:S(2)}) async-start(f32[128,8,128]{2,1,0:T(8,128)} %get-tuple-element.47), calls=%async_computation.1 | async-start | bytes 1048576 | tf_op jit(solution)/shard_map/all_to_all | solution.py:834
  49.1 3.8 %shard_map.143 = (f32[5,256,128]{2,1,0:T(8,128)}, f32[5,64,128]{2,1,0:T(8,128)}, f32[5,72,128]{2,1,0:T(8,128)}, f32[5,72,128]{2,1,0:T(8,128)}, f32[5,8,128]{2,1,0:T(8,128)}, /*index=5*/f32[5,8,128]{2,1,0:T(8,128)}) custom-call(s32[2]{0:T(128)} %pad_add_fusion.place, f32[5,256,128]{2,1,0:T(8,128)} %bitcast.10, f32[5,64,128]{2,1,0:T(8,128)} %get-tuple-element.30.back_planes, ...), custom_call_target="tpu_custom_call" | custom-call | flops 1000000000 | bytes 2244616 | tf_op jit(solution)/shard_map/pallas_call | solution.py:823
  52.9 1.3 collective-permute-start.6
  54.2 2.6 %collective-permute-start.7 = (f32[5,8,128]{2,1,0:T(8,128)}, f32[5,8,128]{2,1,0:T(8,128)S(1)}, u32[]{:S(2)}, u32[]{:S(2)}) collective-permute-start(f32[5,8,128]{2,1,0:T(8,128)} %get-tuple-element.44), channel_id=1, source_target_pairs={{16,32},{48,64},{80,96},{32,16},{64,48},{96,80},{17,33},{49,65},{8... | collective-permute-start | bytes 61448 | tf_op jit(solution)/shard_map/ppermute | solution.py:363
  56.8 1.3 collective-permute-start.4
  58.1 4.7 %collective-permute-start.5 = (f32[5,72,128]{2,1,0:T(8,128)}, f32[5,72,128]{2,1,0:T(8,128)S(1)}, u32[]{:S(2)}, u32[]{:S(2)}) collective-permute-start(f32[5,72,128]{2,1,0:T(8,128)} %get-tuple-element.42), channel_id=1, source_target_pairs={{1,2},{3,4},{5,6},{7,8},{9,10},{11,12},{13,14},{15,0},{2,1},{4,3},... | collective-permute-start | bytes 552968 | tf_op jit(solution)/shard_map/ppermute | solution.py:364
  62.8 0.6 broadcast_multiply_fusion
  63.4 0.0 collective-permute-done.6.got_x
  63.4 0.0 collective-permute-done.7.got_x2
  63.4 0.0 collective-permute-done.4.got_y
  63.4 3.3 %collective-permute-done.5.got_y2 = f32[5,72,128]{2,1,0:T(8,128)S(1)} collective-permute-done((f32[5,72,128]{2,1,0:T(8,128)}, f32[5,72,128]{2,1,0:T(8,128)S(1)}, u32[]{:S(2)}, u32[]{:S(2)}) %collective-permute-start.5) | collective-permute-done | bytes 184352 | tf_op jit(solution)/shard_map/ppermute | solution.py:364
  66.7 0.6 copy-done.12
  67.3 0.2 copy-done
  67.5 22.6 %shard_map.144 = (f32[5,256,128]{2,1,0:T(8,128)}, f32[5,64,128]{2,1,0:T(8,128)}, f32[5,72,128]{2,1,0:T(8,128)}, f32[5,72,128]{2,1,0:T(8,128)}, f32[5,8,128]{2,1,0:T(8,128)}, /*index=5*/f32[5,8,128]{2,1,0:T(8,128)}) custom-call(s32[2]{0:T(128)} %pad_add_fusion.place, f32[3,25]{1,0:T(4,128)} %get-tuple-element.63.blade_m, f32[3,25]{1,0:T(4,128)} %get-tuple-element.62.back_m, ...), custom_call_target="tpu_custom_call" | custom-call | flops 10000000000 | bytes 6226528 | tf_op jit(solution)/shard_map/pallas_call | solution.py:823
  90.1 0.1 collective-permute-start.8
  90.2 4.5 %collective-permute-start.9 = (f32[5,72,128]{2,1,0:T(8,128)}, f32[5,72,128]{2,1,0:T(8,128)S(1)}, u32[]{:S(2)}, u32[]{:S(2)}) collective-permute-start(f32[5,72,128]{2,1,0:T(8,128)} %get-tuple-element.51), channel_id=1, source_target_pairs={{1,2},{3,4},{5,6},{7,8},{9,10},{11,12},{13,14},{15,0},{2,1},{4,3},... | collective-permute-start | bytes 552968 | tf_op jit(solution)/shard_map/ppermute | solution.py:364
  94.7 5.5 %collective-permute-start.11 = (f32[5,8,128]{2,1,0:T(8,128)}, f32[5,8,128]{2,1,0:T(8,128)S(1)}, u32[]{:S(2)}, u32[]{:S(2)}) collective-permute-start(f32[5,8,128]{2,1,0:T(8,128)} %get-tuple-element.53), channel_id=1, source_target_pairs={{16,32},{48,64},{80,96},{32,16},{64,48},{96,80},{17,33},{49,65},{8... | collective-permute-start | bytes 61448 | tf_op jit(solution)/shard_map/ppermute | solution.py:363
  100.3 1.6 %collective-permute-done.11.got_x2 = f32[5,8,128]{2,1,0:T(8,128)S(1)} collective-permute-done((f32[5,8,128]{2,1,0:T(8,128)}, f32[5,8,128]{2,1,0:T(8,128)S(1)}, u32[]{:S(2)}, u32[]{:S(2)}) %collective-permute-start.11) | collective-permute-done | bytes 20512 | tf_op jit(solution)/shard_map/ppermute | solution.py:363
  101.9 0.0 collective-permute-done.8.got_y
  101.9 0.6 copy-done.18
  102.5 0.1 copy-done.7
  102.6 0.1 copy-done.9
  102.7 4.0 %shard_map.146 = f32[128,2,128]{2,1,0:T(2,128)} custom-call(s32[2]{0:T(128)} %pad_add_fusion.place, f32[3,25]{1,0:T(4,128)} %reshape.25.blade_m, f32[3,25]{1,0:T(4,128)} %reshape.26.back_m, f32[5,256,128]{2,1,0:T(8,128)} %get-tuple-element.39.blade_first, f32[5,64,128]{2,1,0:T(8,128)} %get-tuple-element.40.back_first, ...), custom_call_target="tpu_custom_call" | custom-call | flops 1000000000 | bytes 2245216 | tf_op jit(solution)/shard_map/pallas_call | solution.py:823
  106.7 8.0 %all-to-all-start.2 = ((f32[128,2,128]{2,1,0:T(2,128)}), f32[128,2,128]{2,1,0:T(2,128)S(1)}, u32[]{:S(2)}, u32[]{:S(2)}) async-start(f32[128,2,128]{2,1,0:T(2,128)} %shard_map.146), calls=%async_computation.2 | async-start | bytes 262144 | tf_op jit(solution)/shard_map/all_to_all | solution.py:834
  114.7 4.4 %shard_map.145 = (f32[5,256,128]{2,1,0:T(8,128)}, f32[5,64,128]{2,1,0:T(8,128)}) custom-call(s32[2]{0:T(128)} %pad_add_fusion.place, f32[3,25]{1,0:T(4,128)} %reshape.25.blade_m, f32[3,25]{1,0:T(4,128)} %reshape.26.back_m, f32[5,256,128]{2,1,0:T(8,128)} %get-tuple-element.39.blade_first, f32[5,64,128]{2,1,0:T(8,128)} %get-tuple-element.40.back_first, ...), custom_call_target="tpu_custom_call" | custom-call | flops 1000000000 | bytes 2884192 | tf_op jit(solution)/shard_map/pallas_call | solution.py:823
  119.1 5.8 %all-to-all-done.2.recv = f32[128,2,128]{2,1,0:T(2,128)S(1)} async-done(((f32[128,2,128]{2,1,0:T(2,128)}), f32[128,2,128]{2,1,0:T(2,128)S(1)}, u32[]{:S(2)}, u32[]{:S(2)}) %all-to-all-start.2) | async-done | bytes 131104 | tf_op jit(solution)/shard_map/all_to_all | solution.py:834
  124.9 0.7 copy-done.2
  125.5 9.8 %shard_map.147 = (f32[5,256,128]{2,1,0:T(8,128)}, f32[5,16,512]{2,1,0:T(8,128)}) custom-call(f32[5,256,128]{2,1,0:T(8,128)} %get-tuple-element.54.blade_kept, f32[5,64,128]{2,1,0:T(8,128)} %get-tuple-element.55.back_kept, f32[128,2,128]{2,1,0:T(2,128)} %copy-done.2, s32[2,2048]{1,0:T(2,128)} %back_base.5, f32[2,8,2048]{2,1,0:T(8,128)} %back_weight.5, ...), custom_call_target="tpu_custom_call" | custom-call | flops 5000000000 | bytes 2211840 | tf_op jit(solution)/shard_map/pallas_call | solution.py:823
  (34 shorter events, 0.1 us)
Async XLA Ops:
  3.5 26.9 %collective-permute-start.2 = (f32[5,8,128]{2,1,0:T(8,128)}, f32[5,8,128]{2,1,0:T(8,128)S(1)}, u32[]{:S(2)}, u32[]{:S(2)}) collective-permute-start(f32[5,8,128]{2,1,0:T(8,128)} %get-tuple-element.35), channel_id=1, source_target_pairs={{0,16},{32,48},{64,80},{96,112},{16,0},{48,32},{80,64},{112,96},{1... | collective-permute-start | bytes 61448 | tf_op jit(solution)/shard_map/ppermute | solution.py:362
  4.9 25.6 %collective-permute-start.3 = (f32[5,8,128]{2,1,0:T(8,128)}, f32[5,8,128]{2,1,0:T(8,128)S(1)}, u32[]{:S(2)}, u32[]{:S(2)}) collective-permute-start(f32[5,8,128]{2,1,0:T(8,128)} %get-tuple-element.36), channel_id=1, source_target_pairs={{16,32},{48,64},{80,96},{32,16},{64,48},{96,80},{17,33},{49,65},{8... | collective-permute-start | bytes 61448 | tf_op jit(solution)/shard_map/ppermute | solution.py:363
  8.0 22.5 %collective-permute-start = (f32[5,72,128]{2,1,0:T(8,128)}, f32[5,72,128]{2,1,0:T(8,128)S(1)}, u32[]{:S(2)}, u32[]{:S(2)}) collective-permute-start(f32[5,72,128]{2,1,0:T(8,128)} %get-tuple-element.33), channel_id=1, source_target_pairs={{0,1},{2,3},{4,5},{6,7},{8,9},{10,11},{12,13},{14,15},{1,0},{3,2},... | collective-permute-start | bytes 552968 | tf_op jit(solution)/shard_map/ppermute | solution.py:361
  9.4 21.1 %collective-permute-start.1 = (f32[5,72,128]{2,1,0:T(8,128)}, f32[5,72,128]{2,1,0:T(8,128)S(1)}, u32[]{:S(2)}, u32[]{:S(2)}) collective-permute-start(f32[5,72,128]{2,1,0:T(8,128)} %get-tuple-element.34), channel_id=1, source_target_pairs={{1,2},{3,4},{5,6},{7,8},{9,10},{11,12},{13,14},{15,0},{2,1},{4,3},... | collective-permute-start | bytes 552968 | tf_op jit(solution)/shard_map/ppermute | solution.py:364
  14.8 14.3 %copy-start.3 = (f32[3,5,5]{2,0,1:T(4,128)S(1)}, f32[3,5,5]{2,0,1:T(4,128)}, u32[]{:S(2)}) copy-start(f32[3,5,5]{2,0,1:T(4,128)} %param.17) | copy-start | bytes 904
  14.8 15.0 %copy-start.4 = (f32[3,5,5]{2,0,1:T(4,128)S(1)}, f32[3,5,5]{2,0,1:T(4,128)}, u32[]{:S(2)}) copy-start(f32[3,5,5]{2,0,1:T(4,128)} %param.18) | copy-start | bytes 904
  23.7 15.6 %all-to-all-start = ((f32[128,2,128]{2,1,0:T(2,128)}), f32[128,2,128]{2,1,0:T(2,128)S(1)}, u32[]{:S(2)}, u32[]{:S(2)}) async-start(f32[128,2,128]{2,1,0:T(2,128)} %get-tuple-element.31), calls=%async_computation | async-start | bytes 262144 | tf_op jit(solution)/shard_map/all_to_all | solution.py:834
  30.5 0.6 copy-start.13
  30.5 0.6 copy-start.15
  30.5 0.7 copy-start.8
  30.5 0.7 copy-start.11
  39.3 9.8 %copy-start.1 = (f32[128,2,128]{2,1,0:T(2,128)}, f32[128,2,128]{2,1,0:T(2,128)S(1)}, u32[]{:S(2)}) copy-start(f32[128,2,128]{2,1,0:T(2,128)S(1)} %all-to-all-done.recv) | copy-start | bytes 393220
  39.3 23.5 %copy-start.5 = (f32[3,25]{1,0:T(4,128)S(1)}, f32[3,25]{1,0:T(4,128)}, u32[]{:S(2)}) copy-start(f32[3,25]{1,0:T(4,128)} %reshape.25.blade_m) | copy-start | bytes 904
  39.3 23.5 %copy-start.6 = (f32[3,25]{1,0:T(4,128)S(1)}, f32[3,25]{1,0:T(4,128)}, u32[]{:S(2)}) copy-start(f32[3,25]{1,0:T(4,128)} %reshape.26.back_m) | copy-start | bytes 904
  39.3 27.3 %all-to-all-start.1 = ((f32[128,8,128]{2,1,0:T(8,128)}), f32[128,8,128]{2,1,0:T(8,128)S(1)}, u32[]{:S(2)}, u32[]{:S(2)}) async-start(f32[128,8,128]{2,1,0:T(8,128)} %get-tuple-element.47), calls=%async_computation.1 | async-start | bytes 1048576 | tf_op jit(solution)/shard_map/all_to_all | solution.py:834
  52.9 10.4 %collective-permute-start.6 = (f32[5,8,128]{2,1,0:T(8,128)}, f32[5,8,128]{2,1,0:T(8,128)S(1)}, u32[]{:S(2)}, u32[]{:S(2)}) collective-permute-start(f32[5,8,128]{2,1,0:T(8,128)} %get-tuple-element.43), channel_id=1, source_target_pairs={{0,16},{32,48},{64,80},{96,112},{16,0},{48,32},{80,64},{112,96},{1... | collective-permute-start | bytes 61448 | tf_op jit(solution)/shard_map/ppermute | solution.py:362
  54.2 9.2 %collective-permute-start.7 = (f32[5,8,128]{2,1,0:T(8,128)}, f32[5,8,128]{2,1,0:T(8,128)S(1)}, u32[]{:S(2)}, u32[]{:S(2)}) collective-permute-start(f32[5,8,128]{2,1,0:T(8,128)} %get-tuple-element.44), channel_id=1, source_target_pairs={{16,32},{48,64},{80,96},{32,16},{64,48},{96,80},{17,33},{49,65},{8... | collective-permute-start | bytes 61448 | tf_op jit(solution)/shard_map/ppermute | solution.py:363
  56.8 6.6 %collective-permute-start.4 = (f32[5,72,128]{2,1,0:T(8,128)}, f32[5,72,128]{2,1,0:T(8,128)S(1)}, u32[]{:S(2)}, u32[]{:S(2)}) collective-permute-start(f32[5,72,128]{2,1,0:T(8,128)} %get-tuple-element.41), channel_id=1, source_target_pairs={{0,1},{2,3},{4,5},{6,7},{8,9},{10,11},{12,13},{14,15},{1,0},{3,2},... | collective-permute-start | bytes 552968 | tf_op jit(solution)/shard_map/ppermute | solution.py:361
  58.1 8.6 %collective-permute-start.5 = (f32[5,72,128]{2,1,0:T(8,128)}, f32[5,72,128]{2,1,0:T(8,128)S(1)}, u32[]{:S(2)}, u32[]{:S(2)}) collective-permute-start(f32[5,72,128]{2,1,0:T(8,128)} %get-tuple-element.42), channel_id=1, source_target_pairs={{1,2},{3,4},{5,6},{7,8},{9,10},{11,12},{13,14},{15,0},{2,1},{4,3},... | collective-permute-start | bytes 552968 | tf_op jit(solution)/shard_map/ppermute | solution.py:364
  63.4 3.3 %copy-start.14 = (f32[5,8,128]{2,1,0:T(8,128)}, f32[5,8,128]{2,1,0:T(8,128)S(1)}, u32[]{:S(2)}) copy-start(f32[5,8,128]{2,1,0:T(8,128)S(1)} %collective-permute-done.6.got_x) | copy-start | bytes 61444
  63.4 3.3 %copy-start.16 = (f32[5,8,128]{2,1,0:T(8,128)}, f32[5,8,128]{2,1,0:T(8,128)S(1)}, u32[]{:S(2)}) copy-start(f32[5,8,128]{2,1,0:T(8,128)S(1)} %collective-permute-done.7.got_x2) | copy-start | bytes 61444
  63.4 3.3 %copy-start.10 = (f32[5,72,128]{2,1,0:T(8,128)}, f32[5,72,128]{2,1,0:T(8,128)S(1)}, u32[]{:S(2)}) copy-start(f32[5,72,128]{2,1,0:T(8,128)S(1)} %collective-permute-done.4.got_y) | copy-start | bytes 552964
  66.7 0.7 copy-start.12
  66.7 0.9 copy-start
  90.1 11.8 %collective-permute-start.8 = (f32[5,72,128]{2,1,0:T(8,128)}, f32[5,72,128]{2,1,0:T(8,128)S(1)}, u32[]{:S(2)}, u32[]{:S(2)}) collective-permute-start(f32[5,72,128]{2,1,0:T(8,128)} %get-tuple-element.50), channel_id=1, source_target_pairs={{0,1},{2,3},{4,5},{6,7},{8,9},{10,11},{12,13},{14,15},{1,0},{3,2},... | collective-permute-start | bytes 552968 | tf_op jit(solution)/shard_map/ppermute | solution.py:361
  90.2 11.7 %collective-permute-start.9 = (f32[5,72,128]{2,1,0:T(8,128)}, f32[5,72,128]{2,1,0:T(8,128)S(1)}, u32[]{:S(2)}, u32[]{:S(2)}) collective-permute-start(f32[5,72,128]{2,1,0:T(8,128)} %get-tuple-element.51), channel_id=1, source_target_pairs={{1,2},{3,4},{5,6},{7,8},{9,10},{11,12},{13,14},{15,0},{2,1},{4,3},... | collective-permute-start | bytes 552968 | tf_op jit(solution)/shard_map/ppermute | solution.py:364
  94.7 5.6 %collective-permute-start.10 = (f32[5,8,128]{2,1,0:T(8,128)}, f32[5,8,128]{2,1,0:T(8,128)S(1)}, u32[]{:S(2)}, u32[]{:S(2)}) collective-permute-start(f32[5,8,128]{2,1,0:T(8,128)} %get-tuple-element.52), channel_id=1, source_target_pairs={{0,16},{32,48},{64,80},{96,112},{16,0},{48,32},{80,64},{112,96},{1... | collective-permute-start | bytes 61448 | tf_op jit(solution)/shard_map/ppermute | solution.py:362
  94.7 7.2 %collective-permute-start.11 = (f32[5,8,128]{2,1,0:T(8,128)}, f32[5,8,128]{2,1,0:T(8,128)S(1)}, u32[]{:S(2)}, u32[]{:S(2)}) collective-permute-start(f32[5,8,128]{2,1,0:T(8,128)} %get-tuple-element.53), channel_id=1, source_target_pairs={{16,32},{48,64},{80,96},{32,16},{64,48},{96,80},{17,33},{49,65},{8... | collective-permute-start | bytes 61448 | tf_op jit(solution)/shard_map/ppermute | solution.py:363
  100.3 1.7 %copy-start.17 = (f32[5,8,128]{2,1,0:T(8,128)}, f32[5,8,128]{2,1,0:T(8,128)S(1)}, u32[]{:S(2)}) copy-start(f32[5,8,128]{2,1,0:T(8,128)S(1)} %collective-permute-done.10.got_x) | copy-start | bytes 61444
  101.9 0.6 copy-start.18
  101.9 0.7 copy-start.7
  101.9 0.7 copy-start.9
  106.7 18.2 %all-to-all-start.2 = ((f32[128,2,128]{2,1,0:T(2,128)}), f32[128,2,128]{2,1,0:T(2,128)S(1)}, u32[]{:S(2)}, u32[]{:S(2)}) async-start(f32[128,2,128]{2,1,0:T(2,128)} %shard_map.146), calls=%async_computation.2 | async-start | bytes 262144 | tf_op jit(solution)/shard_map/all_to_all | solution.py:834
  124.9 0.7 copy-start.2

commit v3 on v2

--- a/solution.py
+++ b/solution.py
@@ -185,13 +185,20 @@
     return jnp.where(place == 0, fill, lane_roll(v, width))
 
 
-def flux_of(m_ref, t, v):
+class Matrices:
+    def __init__(self, ref, start):
+        self.ref, self.start = ref, start
+
+    def __getitem__(self, place):
+        return self.ref[self.start + place[0], place[1]]
+
+
+def flux_of(m_ref, t, v, scaled):
     out = []
-    half = 0.5 * time_step * v[1 + t]
-    for c in range(5):
-        total = half * v[c]
+    for c in range(5):
+        total = v[1 + t] * scaled[c]
         for e in range(5):
-            total = total + m_ref[t, c * 5 + e] * v[e]
+            total = total + m_ref[t, c * 5 + e] * scaled[e]
         out.append(total)
     return out
 
@@ -256,12 +263,11 @@
     return out
 
 
-def blade_sides(ref, low, high, j, part=slice(0, WALL)):
+def blade_sides(ref, low, high, j):
     def plane(n):
         if n < 0 or n >= WRAP:
-            return [v[part, :] for v in (low if n < 0 else high)]
-        rows = slice(n * WALL + part.start, n * WALL + part.stop)
-        return [ref[c, rows, :] for c in range(5)]
+            return low if n < 0 else high
+        return [ref[c, n * WALL : (n + 1) * WALL, :] for c in range(5)]
 
     center, above, below = plane(j), plane(j + 1), plane(j - 1)
     wall = ([wall_shift(v, True) for v in center], [wall_shift(v, False) for v in center])
@@ -309,45 +315,54 @@
     return jnp.concatenate([lane_roll(v, (y - g) * EAST) for g in range(8)], axis=0)
 
 
-def store_edges(place_ref, blade_at, back, edges):
+def store_blade_edges(ref, rows, edges, at=0):
+    even_y = lax.axis_index("gy") % 2 == 0
+    first_y, second_y = edges
+    count = rows.stop - rows.start
+    top = (WRAP - 1) * WALL
+    for c in range(5):
+        high, low = ref[c, top + rows.start : top + rows.stop, :], ref[c, rows, :]
+        first_y[c, at : at + count, :] = jnp.where(even_y, high, low)
+        second_y[c, at : at + count, :] = jnp.where(even_y, low, high)
+
+
+def store_back_edges(back, edges, at):
     first_y, second_y, first_x, second_x = edges
-    even_y = place_ref[0] % 2 == 0
-    even_x = place_ref[1] % 2 == 0
-    for c in range(5):
-        high, low = blade_at(c, (WRAP - 1) * WALL), blade_at(c, 0)
-        first_y[c, :WALL, :] = jnp.where(even_y, high, low)
-        second_y[c, :WALL, :] = jnp.where(even_y, low, high)
+    even_y = lax.axis_index("gy") % 2 == 0
+    even_x = lax.axis_index("gx") % 2 == 0
+    for c in range(5):
         high, low = pack_north(back[c], NORTH - 1), pack_north(back[c], 0)
-        first_y[c, WALL:, :] = jnp.where(even_y, high, low)
-        second_y[c, WALL:, :] = jnp.where(even_y, low, high)
+        first_y[c, at : at + 8, :] = jnp.where(even_y, high, low)
+        second_y[c, at : at + 8, :] = jnp.where(even_y, low, high)
         high, low = pack_east(back[c], EAST - 1), pack_east(back[c], 0)
         first_x[c] = jnp.where(even_x, high, low)
         second_x[c] = jnp.where(even_x, low, high)
 
 
-EDGE_SHAPES = [
-    jax.ShapeDtypeStruct((5, WALL + 8, CHORD), F32),
-    jax.ShapeDtypeStruct((5, WALL + 8, CHORD), F32),
-    jax.ShapeDtypeStruct((5, 8, DEVS), F32),
-    jax.ShapeDtypeStruct((5, 8, DEVS), F32),
-]
-
-
-def read_halo(place_ref, first_y, second_y, first_x, second_x):
-    north = place_ref[0]
-    even_y = north % 2 == 0
-    even_x = place_ref[1] % 2 == 0
+def edge_shapes(rows):
+    ends = jax.ShapeDtypeStruct((5, rows, CHORD), F32)
+    sides = jax.ShapeDtypeStruct((5, 8, DEVS), F32)
+    return [ends, ends, sides, sides]
+
+
+def read_ends(first_y, second_y, rows):
+    even_y = lax.axis_index("gy") % 2 == 0
+    both = [(first_y[c, rows, :], second_y[c, rows, :]) for c in range(5)]
+    return [jnp.where(even_y, b, a) for a, b in both], [jnp.where(even_y, a, b) for a, b in both]
+
+
+def read_back(first_y, second_y, first_x, second_x, at):
+    north = lax.axis_index("gy")
+    even_x = lax.axis_index("gx") % 2 == 0
     keep_low = jnp.where(north > 0, 1.0, 0.0)
     keep_high = jnp.where(north < DEVS // 8 - 1, 1.0, 0.0)
-    both = [(first_y[c], second_y[c]) for c in range(5)]
-    above = [jnp.where(even_y, a, b) for a, b in both]
-    below = [jnp.where(even_y, b, a) for a, b in both]
+    below, above = read_ends(first_y, second_y, slice(at, at + 8))
     both = [(first_x[c], second_x[c]) for c in range(5)]
     east = [unpack_east(jnp.where(even_x, a, b), EAST - 1) for a, b in both]
     west = [unpack_east(jnp.where(even_x, b, a), 0) for a, b in both]
-    south = [unpack_north(v[WALL:, :] * keep_low, 0) for v in below]
-    upper = [unpack_north(v[WALL:, :] * keep_high, NORTH - 1) for v in above]
-    return [v[:WALL, :] for v in below], [v[:WALL, :] for v in above], [west, east, south, upper]
+    south = [unpack_north(v * keep_low, 0) for v in below]
+    upper = [unpack_north(v * keep_high, NORTH - 1) for v in above]
+    return [west, east, south, upper]
 
 
 def exchange(edges):
@@ -440,15 +455,15 @@
             out[c, row, :] = values[c][:, m * DEVS : (m + 1) * DEVS]
 
 
-def edge_kernel(place, cot, back_cot, cot_planes, first_y, second_y, first_x, second_x):
+def edge_kernel(blade, cot, back_cot, cot_planes, first_y, second_y, first_x, second_x):
     cots = []
     for c in range(5):
         turned = to_planes(back_cot[c])
         cot_planes[c] = turned
         cots.append(turned)
-    store_edges(
-        place, lambda c, r: cot[c, r : r + WALL, :], cots, (first_y, second_y, first_x, second_x)
-    )
+    store_blade_edges(cot, slice(0, WALL), (first_y, second_y))
+    store_blade_edges(blade, slice(0, WALL - 8), (first_y, second_y), WALL + 8)
+    store_back_edges(cots, (first_y, second_y, first_x, second_x), WALL)
 
 
 def start_kernel(
@@ -468,7 +483,7 @@
         store_chunk(hole_vals, n, picked(blade_parts, rows, cols))
         return carry
 
-    lax.fori_loop(0, 2 * HOLES // CHUNK, blade_step, 0, unroll=2)
+    lax.fori_loop(0, 2 * HOLES // CHUNK, blade_step, 0, unroll=4)
 
     def back_step(n, carry):
         lanes = chunk_lanes(n)
@@ -495,11 +510,12 @@
 
 
 def cot_kernel(
-    place, blade_m, back_m, cot, cot_planes, got_y, got_y2, got_x, got_x2,
-    rim_owner, hole_owner, hole_cell,
+    matrices, cot, cot_planes, got_y, got_y2, got_x, got_x2, rim_owner, hole_owner, hole_cell,
     send, blade_fields, back_fields, rim_rank, hole_rank,
 ):
-    low, high, halo = read_halo(place, got_y, got_y2, got_x, got_x2)
+    blade_m, back_m = Matrices(matrices, 0), Matrices(matrices, 3)
+    low, high = read_ends(got_y, got_y2, slice(0, WALL))
+    halo = read_back(got_y, got_y2, got_x, got_x2, WALL)
     for j in range(WRAP):
         center, sides = blade_sides(cot, low, high, j)
         fields = linear_fields(blade_m, center, sides)
@@ -539,7 +555,7 @@
 
 
 def fill_kernel(
-    place, blade, back_planes, recv, rim_owner, hole_owner, rim_rank, hole_rank, hole_cell,
+    blade, back_planes, recv, rim_owner, hole_owner, rim_rank, hole_rank, hole_cell,
     blade_first, back_first, first_y, second_y, first_x, second_x,
 ):
     arrived = doubled(jnp.concatenate([recv[:, 0, :].T, recv[:, 1, :].T], axis=0))
@@ -579,12 +595,8 @@
         field = jnp.concatenate([top, back_planes[c, HALF:, :]], axis=0)
         back_first[c] = field
         backs.append(field)
-    store_edges(
-        place,
-        lambda c, r: blade_first[c, r : r + WALL, :],
-        backs,
-        (first_y, second_y, first_x, second_x),
-    )
+    store_blade_edges(blade_first, slice(WALL - 8, WALL), (first_y, second_y))
+    store_back_edges(backs, (first_y, second_y, first_x, second_x), 8)
 
 
 def residual_step(center, halo_flux):
@@ -597,7 +609,7 @@
 
 
 def side_terms(m_ref, t, v):
-    flux = flux_of(m_ref, t, v)
+    flux = flux_of(m_ref, t, v, [0.5 * time_step * v[c] for c in range(5)])
     damped = [damping * time_step * v[c] for c in range(5)]
     upper = [flux[c] - damped[c] for c in range(5)]
     lower = [flux[c] + damped[c] for c in range(5)]
@@ -605,20 +617,27 @@
 
 
 def middle_kernel(
-    place, blade_m, back_m, blade_first, back_first, got_y, got_y2, got_x, got_x2,
+    matrices, blade_first, back_first, old_y, old_y2, got_y, got_y2, got_x, got_x2,
     blade_fields, back_fields, recv, back_base, back_weight, blade_base, blade_weight, hole_cell,
     blade_mid, back_mid, first_y, second_y, first_x, second_x,
     blade_next, back_next, blade_parts, back_parts, hole_lin, rim_lin, blade_acc, back_acc,
 ):
-    low, high, halo = read_halo(place, got_y, got_y2, got_x, got_x2)
-
-    planes = [low]
+    blade_m, back_m = Matrices(matrices, 0), Matrices(matrices, 3)
+    planes = zip(
+        read_ends(old_y, old_y2, slice(WALL + 8, 2 * WALL)), read_ends(got_y, got_y2, slice(0, 8))
+    )
+    low, high = (
+        [jnp.concatenate([a, b], axis=0) for a, b in zip(inner, outer)] for inner, outer in planes
+    )
+    halo = read_back(got_y, got_y2, got_x, got_x2, 8)
+
+    sections = [low]
     for j in range(WRAP):
-        planes.append([blade_first[c, j * WALL : (j + 1) * WALL, :] for c in range(5)])
-    planes.append(high)
-    turns = [side_terms(blade_m, 0, plane) for plane in planes]
+        sections.append([blade_first[c, j * WALL : (j + 1) * WALL, :] for c in range(5)])
+    sections.append(high)
+    turns = [side_terms(blade_m, 0, plane) for plane in sections]
     for j in range(WRAP):
-        center = planes[j + 1]
+        center = sections[j + 1]
 
         def around(t, j=j, center=center):
             if t == 0:
@@ -689,7 +708,7 @@
         blade_acc[...] += spread_terms(rows, cols, mu)
         return carry
 
-    lax.fori_loop(0, 2 * HOLES // CHUNK, blade_step, 0, unroll=2)
+    lax.fori_loop(0, 2 * HOLES // CHUNK, blade_step, 0, unroll=4)
 
     def back_step(n, carry):
         lanes = chunk_lanes(n)
@@ -703,36 +722,89 @@
     for c in range(5):
         blade_mid[c] = blade_mid[c] + blade_acc[c * CHORD : (c + 1) * CHORD, :].T
         back_mid[c, HALF:, :] = back_mid[c, HALF:, :] + back_acc[c * HALF : (c + 1) * HALF, :]
-    store_edges(
-        place,
-        lambda c, r: blade_mid[c, r : r + WALL, :],
-        [back_mid[c] for c in range(5)],
-        (first_y, second_y, first_x, second_x),
-    )
-
-
-def give_kernel(
-    place, blade_m, back_m, blade_first, back_first, blade_mid, back_mid,
+    store_blade_edges(blade_mid, slice(0, WALL), (first_y, second_y))
+    store_back_edges(
+        [back_mid[c] for c in range(5)], (first_y, second_y, first_x, second_x), WALL
+    )
+
+
+def inner_kernel(
+    matrices, blade_first, back_first, blade_mid, back_mid, hole_cell, blade_part, back_part, mask
+):
+    blade_m, back_m = Matrices(matrices, 0), Matrices(matrices, 3)
+    nothing = [jnp.zeros((WALL, CHORD), F32)] * 5
+    for j in range(WRAP):
+        rows = slice(j * WALL, (j + 1) * WALL)
+        center, sides = blade_sides(blade_mid, nothing, nothing, j)
+        out = adjoint_at(blade_m, [blade_first[c, rows, :] for c in range(5)], center, sides)
+        for c in range(5):
+            blade_part[c, rows, :] = out[c]
+    nothing = [jnp.zeros((VERT, DEVS), F32)] * 5
+    center = [back_mid[c] for c in range(5)]
+    sides = back_sides(center, [nothing] * 4)
+    out = adjoint_at(back_m, [back_first[c] for c in range(5)], center, sides)
+    for c in range(5):
+        back_part[c] = out[c]
+    mask[...] = hole_mask(hole_cell.at[0:1])
+
+
+def outside_terms(m_ref, t, v, beyond, sign):
+    jump = [-sign * 0.5 * time_step * beyond[c] for c in range(5)]
+    turned = turned_of(m_ref, t, jump)
+    inner = v[0] * jump[0]
+    for e in range(1, 5):
+        inner = inner + v[e] * jump[e]
+    out = []
+    for c in range(5):
+        total = turned[c] + v[1 + t] * jump[c]
+        if c == 1 + t:
+            total = total + inner
+        out.append(damping * time_step * beyond[c] - total)
+    return out
+
+
+def last_kernel(
+    matrices, blade_first, back_first, blade_part, back_part, mask,
     got_y, got_y2, got_x, got_x2,
     rim_owner, hole_owner, rim_rank, hole_rank, hole_cell,
-    send,
+    send, blade_kept, back_kept,
 ):
-    low, high, halo = read_halo(place, got_y, got_y2, got_x, got_x2)
+    blade_m, back_m = Matrices(matrices, 0), Matrices(matrices, 3)
+    low, high = read_ends(got_y, got_y2, slice(0, WALL))
+    halo = read_back(got_y, got_y2, got_x, got_x2, WALL)
     rims = jnp.zeros((5 * QR, DEVS), F32)
     for j in range(WRAP):
-        outer = slice(WALL - 8, WALL)
-        rows = slice(j * WALL + WALL - 8, (j + 1) * WALL)
-        center, sides = blade_sides(blade_mid, low, high, j, outer)
-        out = adjoint_at(blade_m, [blade_first[c, rows, :] for c in range(5)], center, sides)
-        values = [jnp.concatenate([out[c][6:7, :], out[c][7:8, :]], axis=1) for c in range(5)]
+        rows = slice(j * WALL, (j + 1) * WALL)
+        out = [blade_part[c, rows, :] for c in range(5)]
+        if j in (0, WRAP - 1):
+            v = [blade_first[c, rows, :] for c in range(5)]
+            beyond, sign = (high, 1.0) if j else (low, -1.0)
+            more = outside_terms(blade_m, 0, v, beyond, sign)
+            out = [out[c] + more[c] for c in range(5)]
+        inside = iota((WALL, CHORD), 0) < WALL - 2
+        values = []
+        for c in range(5):
+            blade_kept[c, rows, :] = jnp.where(inside, out[c], 0.0)
+            outer = [out[c][WALL - 2 + k : WALL - 1 + k, :] for k in range(2)]
+            values.append(jnp.concatenate(outer, axis=1))
         lanes = slice(j * 256, j * 256 + 256)
         rims = rims + send_rows(values, rim_owner[0, :, lanes], rim_rank[0, :, lanes], QR)
-    part = HALF + 8
-    center = [back_mid[c, :part, :] for c in range(5)]
-    halo = [[v[:part, :] for v in side] for side in halo]
-    out = adjoint_at(
-        back_m, [back_first[c, :part, :] for c in range(5)], center, back_sides(center, halo)
-    )
+    v = [back_first[c] for c in range(5)]
+    out = [back_part[c] for c in range(5)]
+    place = iota((VERT, DEVS), 1)
+    east, north = place % EAST, place // EAST
+    for t, beyond, sign, at in (
+        (0, halo[0], -1.0, east == 0),
+        (0, halo[1], 1.0, east == EAST - 1),
+        (1, halo[2], -1.0, north == 0),
+        (1, halo[3], 1.0, north == NORTH - 1),
+    ):
+        more = outside_terms(back_m, t, v, [jnp.where(at, x, 0.0) for x in beyond], sign)
+        out = [out[c] + more[c] for c in range(5)]
+    holes_here = mask[...] > 0.5
+    for c in range(5):
+        back_kept[c, :HALF, :] = jnp.where(holes_here, 0.0, out[c][:HALF, :])
+        back_kept[c, HALF:, :] = out[c][HALF:, :]
     holes = jnp.zeros((5 * QH, DEVS), F32)
     low_half = doubled(jnp.concatenate([out[c][:HALF, :] for c in range(5)], axis=0))
     for start in range(0, HOLES, 512):
@@ -743,27 +815,6 @@
     total = jnp.concatenate([holes, rims, rest], axis=0)
     send[:, 0, :] = total[:DEVS].T
     send[:, 1, :] = total[DEVS:].T
-
-
-def keep_kernel(
-    place, blade_m, back_m, blade_first, back_first, blade_mid, back_mid,
-    got_y, got_y2, got_x, got_x2, hole_cell,
-    blade_kept, back_kept,
-):
-    low, high, halo = read_halo(place, got_y, got_y2, got_x, got_x2)
-    for j in range(WRAP):
-        rows = slice(j * WALL, (j + 1) * WALL)
-        center, sides = blade_sides(blade_mid, low, high, j)
-        out = adjoint_at(blade_m, [blade_first[c, rows, :] for c in range(5)], center, sides)
-        inside = iota((WALL, CHORD), 0) < WALL - 2
-        for c in range(5):
-            blade_kept[c, rows, :] = jnp.where(inside, out[c], 0.0)
-    center = [back_mid[c] for c in range(5)]
-    out = adjoint_at(back_m, [back_first[c] for c in range(5)], center, back_sides(center, halo))
-    mask = hole_mask(hole_cell.at[0:1])
-    for c in range(5):
-        back_kept[c, :HALF, :] = jnp.where(mask > 0.5, 0.0, out[c][:HALF, :])
-        back_kept[c, HALF:, :] = out[c][HALF:, :]
 
 
 def end_kernel(
@@ -790,7 +841,7 @@
         blade_acc[...] += spread_terms(rows, cols, [lanes_of(hole_mu, n, c) for c in range(5)])
         return carry
 
-    lax.fori_loop(0, 2 * HOLES // CHUNK, blade_step, 0, unroll=2)
+    lax.fori_loop(0, 2 * HOLES // CHUNK, blade_step, 0, unroll=4)
 
     def back_step(n, carry):
         lanes = chunk_lanes(n)
@@ -850,16 +901,14 @@
     blade_donor_weight,
 ):
     shape = jax.ShapeDtypeStruct
-    place = jnp.stack([lax.axis_index("gy"), lax.axis_index("gx")]).astype(jnp.int32)
     blade = blade_state.reshape(5, WRAP * WALL, CHORD)
     cot = blade_cotangent.reshape(5, WRAP * WALL, CHORD)
-    matrices = (blade_flux.reshape(3, 25), back_flux.reshape(3, 25))
-    scaled = tuple(0.5 * time_step * m for m in matrices)
+    matrices = jnp.concatenate([blade_flux, back_flux]).reshape(6, 25)
     owners = (blade_owner.reshape(2, 1, RIMS), hole_owner.reshape(2, 1, HOLES))
     tables = (back_donor_cell, back_donor_weight, blade_donor_cell, blade_donor_weight)
 
     cot_planes, *edges = run(
-        edge_kernel, (place, cot, back_cotangent), [PLANES] + EDGE_SHAPES, scalars=1
+        edge_kernel, (blade, cot, back_cotangent), [PLANES] + edge_shapes(2 * WALL)
     )
     cot_halo = exchange(edges)
     send, back_planes = run(
@@ -872,7 +921,7 @@
     recv = swap(send)
     lin_send, blade_fields, back_fields, rim_rank, hole_rank = run(
         cot_kernel,
-        (place, *matrices, cot, cot_planes, *cot_halo, *owners, hole_cell),
+        (matrices, cot, cot_planes, *cot_halo, *owners, hole_cell),
         [
             shape((DEVS, 8, DEVS), F32),
             shape((FIELDS, WRAP * WALL, CHORD), F32),
@@ -880,40 +929,48 @@
             shape((2, 1, RIMS), jnp.int32),
             shape((2, 1, HOLES), jnp.int32),
         ],
-        scalars=3,
+        scalars=1,
         flops=2 * 10**9,
     )
     lin_recv = swap(lin_send)
     slots = (*owners, rim_rank, hole_rank, hole_cell)
     blade_first, back_first, *edges = run(
         fill_kernel,
-        (place, blade, back_planes, recv) + slots,
-        [BLADE, PLANES] + EDGE_SHAPES,
-        scalars=1,
+        (blade, back_planes, recv) + slots,
+        [BLADE, PLANES] + edge_shapes(16),
         flops=10**9,
     )
     first_halo = exchange(edges)
     blade_mid, back_mid, *edges = run(
         middle_kernel,
-        (place, *scaled, blade_first, back_first, *first_halo, blade_fields, back_fields)
+        (matrices, blade_first, back_first, *cot_halo[:2], *first_halo, blade_fields, back_fields)
         + (lin_recv,)
         + tables
         + (hole_cell,),
-        [BLADE, PLANES] + EDGE_SHAPES,
+        [BLADE, PLANES] + edge_shapes(WALL + 8),
         [pltpu.VMEM(BLADE.shape, F32), pltpu.VMEM(PLANES.shape, F32)]
         + DONOR_PARTS
         + [pltpu.VMEM((FIELDS, QH, DEVS), F32), pltpu.VMEM((FIELDS, QR, DEVS), F32)]
         + SUMS,
-        scalars=3,
+        scalars=1,
         flops=10**10,
     )
     mid_halo = exchange(edges)
-    both = (place, *matrices, blade_first, back_first, blade_mid, back_mid, *mid_halo)
-    (send,) = run(give_kernel, both + slots, [shape((DEVS, 2, DEVS), F32)], scalars=3, flops=10**9)
+    parts = run(
+        inner_kernel,
+        (matrices, blade_first, back_first, blade_mid, back_mid, hole_cell),
+        [BLADE, PLANES, shape((HALF, DEVS), F32)],
+        scalars=1,
+        flops=10**9,
+    )
+    send, blade_kept, back_kept = run(
+        last_kernel,
+        (matrices, blade_first, back_first, *parts, *mid_halo) + slots,
+        [shape((DEVS, 2, DEVS), F32), BLADE, PLANES],
+        scalars=1,
+        flops=10**9,
+    )
     recv = swap(send)
-    blade_kept, back_kept = run(
-        keep_kernel, both + (hole_cell,), [BLADE, PLANES], scalars=3, flops=10**9
-    )
     blade_last, back_last = run(
         end_kernel,
         (blade_kept, back_kept, recv) + tables,

time: 136 us -> 129 us (0.949)
  blocking collectives: 0 us -> 16.9 us
  starting transfers between devices: 54.3 us -> 41.9 us
  waiting for transfers between devices: 10.7 us -> 4.39 us
  Pallas kernels: 63.9 us -> 61.8 us
    all_to_all x0 -> x1, blocking collectives: none -> 16.9 us  [swap(): lax.all_to_all(rows, ('gx', 'gy'), split_axis=0, concat_axis=0, tiled=True)]
    all_to_all x3 -> x2, starting transfers between devices: 23.2 us -> 15.1 us  [swap(): lax.all_to_all(rows, ('gx', 'gy'), split_axis=0, concat_axis=0, tiled=True)]
    all_to_all x3 -> x2, waiting for transfers between devices: 5.78 us -> 0.01 us  [swap(): lax.all_to_all(rows, ('gx', 'gy'), split_axis=0, concat_axis=0, tiled=True)]
    ppermute x3, starting transfers between devices: 14.6 us -> 10.8 us  [exchange(): got_y2 = lax.ppermute(second_y, 'gy', pairs(1, gy, gy))]
    ppermute x3, waiting for transfers between devices: 3.26 us -> 0.01 us  [exchange(): got_y2 = lax.ppermute(second_y, 'gy', pairs(1, gy, gy))]
    ppermute x3, waiting for transfers between devices: 1.65 us -> 4.36 us  [exchange(): got_x2 = lax.ppermute(second_x, 'gx', pairs(1, gx - 1, gx))]
    ppermute x3, starting transfers between devices: 11.2 us -> 8.55 us  [exchange(): got_x2 = lax.ppermute(second_x, 'gx', pairs(1, gx - 1, gx))]
    pallas_call x8, Pallas kernels: 63.9 us -> 61.8 us  [run(): pl.pallas_call(kernel, out_shape=list(out_shape), in_specs=[SMEM] * scala...]
  transfers between devices with their start and end apart: 15 -> 14, of which waited for: 3 -> 2; matrix products, arithmetic and copies ran while one was open for 1% -> 1% of each run, Pallas kernels for 19% -> 19%
where the time goes in v3:
time: 129 us
  Pallas kernels  61.8 us (48%)
  starting transfers between devices  41.9 us (32%)
  blocking collectives  16.9 us (13%)
  waiting for transfers between devices  4.39 us (3%)
  local copies, waits for them, and re-layouts  3.06 us (2%)
    pallas_call x8, Pallas kernels, run(): pl.pallas_call(kernel, out_shape=list(out_shape), in_specs=[SMEM] * scala...  61.8 us
    all_to_all x1, blocking collectives, swap(): lax.all_to_all(rows, ('gx', 'gy'), split_axis=0, concat_axis=0, tiled=True)  16.9 us
    all_to_all x2, starting transfers between devices, swap(): lax.all_to_all(rows, ('gx', 'gy'), split_axis=0, concat_axis=0, tiled=True)  15.1 us
    ppermute x3, starting transfers between devices, exchange(): got_y2 = lax.ppermute(second_y, 'gy', pairs(1, gy, gy))  10.8 us
    ppermute x3, starting transfers between devices, exchange(): got_x2 = lax.ppermute(second_x, 'gx', pairs(1, gx - 1, gx))  8.55 us
    ppermute x3, waiting for transfers between devices, exchange(): got_x2 = lax.ppermute(second_x, 'gx', pairs(1, gx - 1, gx))  4.36 us
    ppermute x3, starting transfers between devices, exchange(): got_x = lax.ppermute(first_x, 'gx', pairs(0, gx, gx))  3.92 us
    ppermute x3, starting transfers between devices, exchange(): got_y = lax.ppermute(first_y, 'gy', pairs(0, gy, gy))  3.56 us
  transfers between devices with their start and end apart: 14, of which 2 were waited for; matrix products, arithmetic and copies ran while one was open for 1% of the time, Pallas kernels for 19%

profile of v3, /device:TPU:1, one launch (start us, length us, event | category | flops | bytes accessed | tf_op | source)
XLA Modules:
  0.0 129.0 jit_solution(17841731214500513157)
XLA Ops:
  0.6 2.6 %shard_map.141 = (f32[5,64,128]{2,1,0:T(8,128)}, f32[5,128,128]{2,1,0:T(8,128)}, f32[5,128,128]{2,1,0:T(8,128)}, f32[5,8,128]{2,1,0:T(8,128)}, f32[5,8,128]{2,1,0:T(8,128)}) custom-call(f32[5,256,128]{2,1,0:T(8,128)} %bitcast.7, f32[5,256,128]{2,1,0:T(8,128)} %bitcast.5, f32[5,16,512]{2,1,0:T(8,128)} %back_cot.1), custom_call_target="tpu_custom_call" | custom-call | bytes 2334720 | tf_op jit(solution)/shard_map/pallas_call | solution.py:874
  3.2 2.1 %collective-permute-start = (f32[5,128,128]{2,1,0:T(8,128)}, f32[5,128,128]{2,1,0:T(8,128)S(1)}, u32[]{:S(2)}, u32[]{:S(2)}) collective-permute-start(f32[5,128,128]{2,1,0:T(8,128)} %get-tuple-element.37), channel_id=1, source_target_pairs={{0,1},{2,3},{4,5},{6,7},{8,9},{10,11},{12,13},{14,15},{1,0},{3,2},... | collective-permute-start | bytes 983048 | tf_op jit(solution)/shard_map/ppermute | solution.py:376
  5.4 5.5 %collective-permute-start.1 = (f32[5,128,128]{2,1,0:T(8,128)}, f32[5,128,128]{2,1,0:T(8,128)S(1)}, u32[]{:S(2)}, u32[]{:S(2)}) collective-permute-start(f32[5,128,128]{2,1,0:T(8,128)} %get-tuple-element.38), channel_id=1, source_target_pairs={{1,2},{3,4},{5,6},{7,8},{9,10},{11,12},{13,14},{15,0},{2,1},{4,3},... | collective-permute-start | bytes 983048 | tf_op jit(solution)/shard_map/ppermute | solution.py:379
  10.8 8.5 %shard_map.140 = (f32[128,2,128]{2,1,0:T(2,128)}, f32[5,64,128]{2,1,0:T(8,128)}) custom-call(f32[5,256,128]{2,1,0:T(8,128)} %bitcast.8, f32[5,16,512]{2,1,0:T(8,128)} %back.1, s32[2,2048]{1,0:T(2,128)} %back_base.5, f32[2,8,2048]{2,1,0:T(8,128)} %back_weight.5, s32[2,4096]{1,0:T(2,128)} %blade_base.5, f32[2,8,4096]{2,1,0:T(8,128)} %blade_weight.5), custom_call_target="tpu_custom_call" | custom-call | flops 5000000000 | bytes 1556480 | tf_op jit(solution)/shard_map/pallas_call | solution.py:874
  19.3 6.5 %all-to-all-start = ((f32[128,2,128]{2,1,0:T(2,128)}), f32[128,2,128]{2,1,0:T(2,128)S(1)}, u32[]{:S(2)}, u32[]{:S(2)}) async-start(f32[128,2,128]{2,1,0:T(2,128)} %get-tuple-element.35), calls=%async_computation | async-start | bytes 262144 | tf_op jit(solution)/shard_map/all_to_all | solution.py:885
  25.8 1.1 collective-permute-start.2
  27.0 2.6 %collective-permute-start.3 = (f32[5,8,128]{2,1,0:T(8,128)S(1)}, f32[5,8,128]{2,1,0:T(8,128)S(1)}, u32[]{:S(2)}, u32[]{:S(2)}) collective-permute-start(f32[5,8,128]{2,1,0:T(8,128)S(1)} %copy-done.13), channel_id=1, source_target_pairs={{16,32},{48,64},{80,96},{32,16},{64,48},{96,80},{17,33},{49,65},{8... | collective-permute-start | bytes 61448 | tf_op jit(solution)/shard_map/ppermute | solution.py:378
  29.6 0.7 reshape.22.matrices
  30.3 0.0 collective-permute-done.2.got_x
  30.3 2.1 %collective-permute-done.3.got_x2 = f32[5,8,128]{2,1,0:T(8,128)S(1)} collective-permute-done((f32[5,8,128]{2,1,0:T(8,128)S(1)}, f32[5,8,128]{2,1,0:T(8,128)S(1)}, u32[]{:S(2)}, u32[]{:S(2)}) %collective-permute-start.3) | collective-permute-done | bytes 20512 | tf_op jit(solution)/shard_map/ppermute | solution.py:378
  32.4 0.0 collective-permute-done.got_y.old_y
  32.4 0.0 collective-permute-done.1.got_y2.old_y2
  32.4 0.6 copy-done.17
  33.0 0.1 copy-done.4
  33.1 0.1 copy-done.5
  33.2 8.2 %shard_map.142 = (f32[128,8,128]{2,1,0:T(8,128)}, f32[17,256,128]{2,1,0:T(8,128)}, f32[17,64,128]{2,1,0:T(8,128)}, s32[2,1,1024]{2,1,0:T(1,128)}, s32[2,1,2048]{2,1,0:T(1,128)}) custom-call(f32[6,25]{1,0:T(8,128)} %reshape.22.matrices, f32[5,256,128]{2,1,0:T(8,128)} %bitcast.6, f32[5,64,128]{2,1,0:T(8,128)} %get-tuple-element.36.cot_planes, ...), custom_call_target="tpu_custom_call" | custom-call | flops 2000000000 | bytes 4891224 | tf_op jit(solution)/shard_map/pallas_call | solution.py:874
  41.4 0.0 all-to-all-done.recv
  41.4 8.5 %all-to-all-start.1 = ((f32[128,8,128]{2,1,0:T(8,128)}), f32[128,8,128]{2,1,0:T(8,128)S(1)}, u32[]{:S(2)}, u32[]{:S(2)}) async-start(f32[128,8,128]{2,1,0:T(8,128)} %get-tuple-element.51), calls=%async_computation.1 | async-start | bytes 1048576 | tf_op jit(solution)/shard_map/all_to_all | solution.py:885
  50.0 3.7 %shard_map.143 = (f32[5,256,128]{2,1,0:T(8,128)}, f32[5,64,128]{2,1,0:T(8,128)}, f32[5,16,128]{2,1,0:T(8,128)}, f32[5,16,128]{2,1,0:T(8,128)}, f32[5,8,128]{2,1,0:T(8,128)}, /*index=5*/f32[5,8,128]{2,1,0:T(8,128)}) custom-call(f32[5,256,128]{2,1,0:T(8,128)} %bitcast.9, f32[5,64,128]{2,1,0:T(8,128)} %get-tuple-element.34.back_planes, ...), custom_call_target="tpu_custom_call" | custom-call | flops 1000000000 | bytes 1957888 | tf_op jit(solution)/shard_map/pallas_call | solution.py:874
  53.7 1.4 %collective-permute-start.4 = (f32[5,16,128]{2,1,0:T(8,128)}, f32[5,16,128]{2,1,0:T(8,128)S(1)}, u32[]{:S(2)}, u32[]{:S(2)}) collective-permute-start(f32[5,16,128]{2,1,0:T(8,128)} %get-tuple-element.45), channel_id=1, source_target_pairs={{0,1},{2,3},{4,5},{6,7},{8,9},{10,11},{12,13},{14,15},{1,0},{3,2},... | collective-permute-start | bytes 122888 | tf_op jit(solution)/shard_map/ppermute | solution.py:376
  55.0 4.7 %collective-permute-start.5 = (f32[5,16,128]{2,1,0:T(8,128)}, f32[5,16,128]{2,1,0:T(8,128)S(1)}, u32[]{:S(2)}, u32[]{:S(2)}) collective-permute-start(f32[5,16,128]{2,1,0:T(8,128)} %get-tuple-element.46), channel_id=1, source_target_pairs={{1,2},{3,4},{5,6},{7,8},{9,10},{11,12},{13,14},{15,0},{2,1},{4,3},... | collective-permute-start | bytes 122888 | tf_op jit(solution)/shard_map/ppermute | solution.py:379
  59.7 0.9 collective-permute-start.6
  60.7 3.0 %collective-permute-start.7 = (f32[5,8,128]{2,1,0:T(8,128)}, f32[5,8,128]{2,1,0:T(8,128)S(1)}, u32[]{:S(2)}, u32[]{:S(2)}) collective-permute-start(f32[5,8,128]{2,1,0:T(8,128)} %get-tuple-element.48), channel_id=1, source_target_pairs={{16,32},{48,64},{80,96},{32,16},{64,48},{96,80},{17,33},{49,65},{8... | collective-permute-start | bytes 61448 | tf_op jit(solution)/shard_map/ppermute | solution.py:378
  63.7 0.0 collective-permute-done.6.got_x
  63.7 2.3 %collective-permute-done.7.got_x2 = f32[5,8,128]{2,1,0:T(8,128)S(1)} collective-permute-done((f32[5,8,128]{2,1,0:T(8,128)}, f32[5,8,128]{2,1,0:T(8,128)S(1)}, u32[]{:S(2)}, u32[]{:S(2)}) %collective-permute-start.7) | collective-permute-done | bytes 20512 | tf_op jit(solution)/shard_map/ppermute | solution.py:378
  66.0 0.0 collective-permute-done.4.got_y
  66.0 0.0 collective-permute-done.5.got_y2
  66.0 0.0 all-to-all-done.1.recv
  66.0 0.5 copy-done.12
  66.6 0.0 copy-done.8
  66.6 0.0 copy-done.9
  66.6 0.2 copy-done
  66.8 21.0 %shard_map.144 = (f32[5,256,128]{2,1,0:T(8,128)}, f32[5,64,128]{2,1,0:T(8,128)}, f32[5,72,128]{2,1,0:T(8,128)}, f32[5,72,128]{2,1,0:T(8,128)}, f32[5,8,128]{2,1,0:T(8,128)}, /*index=5*/f32[5,8,128]{2,1,0:T(8,128)}) custom-call(f32[6,25]{1,0:T(8,128)} %reshape.22.matrices, f32[5,256,128]{2,1,0:T(8,128)} %get-tuple-element.43.blade_first, ...), custom_call_target="tpu_custom_call" | custom-call | flops 10000000000 | bytes 6595160 | tf_op jit(solution)/shard_map/pallas_call | solution.py:874
  87.8 0.1 collective-permute-start.8
  87.9 0.7 collective-permute-start.9
  88.6 1.8 %collective-permute-start.10 = (f32[5,8,128]{2,1,0:T(8,128)}, f32[5,8,128]{2,1,0:T(8,128)S(1)}, u32[]{:S(2)}, u32[]{:S(2)}) collective-permute-start(f32[5,8,128]{2,1,0:T(8,128)} %get-tuple-element.59), channel_id=1, source_target_pairs={{0,16},{32,48},{64,80},{96,112},{16,0},{48,32},{80,64},{112,96},{1... | collective-permute-start | bytes 61448 | tf_op jit(solution)/shard_map/ppermute | solution.py:377
  90.4 3.0 %collective-permute-start.11 = (f32[5,8,128]{2,1,0:T(8,128)}, f32[5,8,128]{2,1,0:T(8,128)S(1)}, u32[]{:S(2)}, u32[]{:S(2)}) collective-permute-start(f32[5,8,128]{2,1,0:T(8,128)} %get-tuple-element.60), channel_id=1, source_target_pairs={{16,32},{48,64},{80,96},{32,16},{64,48},{96,80},{17,33},{49,65},{8... | collective-permute-start | bytes 61448 | tf_op jit(solution)/shard_map/ppermute | solution.py:378
  93.4 4.2 %shard_map.145 = (f32[5,256,128]{2,1,0:T(8,128)}, f32[5,64,128]{2,1,0:T(8,128)}, f32[32,128]{1,0:T(8,128)}) custom-call(f32[6,25]{1,0:T(8,128)} %reshape.22.matrices, f32[5,256,128]{2,1,0:T(8,128)} %get-tuple-element.43.blade_first, f32[5,64,128]{2,1,0:T(8,128)} %get-tuple-element.44.back_first, f32[5,256,128]{2,1,0:T(8,128)} %get-tuple-element.52.blade_mid, ...), custom_call_target="tpu_custom_call" | custom-call | flops 1000000000 | bytes 2490968 | tf_op jit(solution)/shard_map/pallas_call | solution.py:874
  97.6 0.0 collective-permute-done.10.got_x
  97.6 0.0 collective-permute-done.11.got_x2
  97.6 0.0 collective-permute-done.9.got_y2
  97.6 0.5 copy-done.11
  98.2 0.0 copy-done.14
  98.2 0.1 copy-done.6
  98.3 0.1 copy-done.7
  98.4 4.4 %shard_map.146 = (f32[128,2,128]{2,1,0:T(2,128)}, f32[5,256,128]{2,1,0:T(8,128)}, f32[5,64,128]{2,1,0:T(8,128)}) custom-call(f32[6,25]{1,0:T(8,128)} %reshape.22.matrices, f32[5,256,128]{2,1,0:T(8,128)} %get-tuple-element.43.blade_first, f32[5,64,128]{2,1,0:T(8,128)} %get-tuple-element.44.back_first, f32[5,256,128]{2,1,0:T(8,128)} %get-tuple-element.54.blade_part, ...), custom_call_target="tpu_custom_call" | custom-call | flops 1000000000 | bytes 3080792 | tf_op jit(solution)/shard_map/pallas_call | solution.py:874
  102.8 16.9 %all_to_all.15.recv = f32[128,2,128]{2,1,0:T(2,128)} all-to-all(f32[128,2,128]{2,1,0:T(2,128)} %get-tuple-element.63), channel_id=1, replica_groups=mesh['gx'=8,'gy'=16] {'gx','gy'}, dimensions={0} | all-to-all | bytes 262144 | tf_op jit(solution)/shard_map/all_to_all | solution.py:885
  119.7 9.3 %shard_map.147 = (f32[5,256,128]{2,1,0:T(8,128)}, f32[5,16,512]{2,1,0:T(8,128)}) custom-call(f32[5,256,128]{2,1,0:T(8,128)} %get-tuple-element.61.blade_kept, f32[5,64,128]{2,1,0:T(8,128)} %get-tuple-element.62.back_kept, f32[128,2,128]{2,1,0:T(2,128)} %all_to_all.15.recv, s32[2,2048]{1,0:T(2,128)} %back_base.5, f32[2,8,2048]{2,1,0:T(8,128)} %back_weight.5, ...), custom_call_target="tpu_custom_call" | custom-call | flops 5000000000 | bytes 2211840 | tf_op jit(solution)/shard_map/pallas_call | solution.py:874
  (28 shorter events, 0.1 us)
Async XLA Ops:
  3.2 29.1 %collective-permute-start = (f32[5,128,128]{2,1,0:T(8,128)}, f32[5,128,128]{2,1,0:T(8,128)S(1)}, u32[]{:S(2)}, u32[]{:S(2)}) collective-permute-start(f32[5,128,128]{2,1,0:T(8,128)} %get-tuple-element.37), channel_id=1, source_target_pairs={{0,1},{2,3},{4,5},{6,7},{8,9},{10,11},{12,13},{14,15},{1,0},{3,2},... | collective-permute-start | bytes 983048 | tf_op jit(solution)/shard_map/ppermute | solution.py:376
  5.3 20.5 %copy-start.15 = (f32[5,8,128]{2,1,0:T(8,128)S(1)}, f32[5,8,128]{2,1,0:T(8,128)}, u32[]{:S(2)}) copy-start(f32[5,8,128]{2,1,0:T(8,128)} %get-tuple-element.39) | copy-start | bytes 61444
  5.3 21.6 %copy-start.13 = (f32[5,8,128]{2,1,0:T(8,128)S(1)}, f32[5,8,128]{2,1,0:T(8,128)}, u32[]{:S(2)}) copy-start(f32[5,8,128]{2,1,0:T(8,128)} %get-tuple-element.40) | copy-start | bytes 61444
  5.3 24.2 %copy-start.2 = (f32[3,5,5]{2,0,1:T(4,128)S(1)}, f32[3,5,5]{2,0,1:T(4,128)}, u32[]{:S(2)}) copy-start(f32[3,5,5]{2,0,1:T(4,128)} %param.18) | copy-start | bytes 904
  5.3 24.2 %copy-start.3 = (f32[3,5,5]{2,0,1:T(4,128)S(1)}, f32[3,5,5]{2,0,1:T(4,128)}, u32[]{:S(2)}) copy-start(f32[3,5,5]{2,0,1:T(4,128)} %param.17) | copy-start | bytes 904
  5.4 27.0 %collective-permute-start.1 = (f32[5,128,128]{2,1,0:T(8,128)}, f32[5,128,128]{2,1,0:T(8,128)S(1)}, u32[]{:S(2)}, u32[]{:S(2)}) collective-permute-start(f32[5,128,128]{2,1,0:T(8,128)} %get-tuple-element.38), channel_id=1, source_target_pairs={{1,2},{3,4},{5,6},{7,8},{9,10},{11,12},{13,14},{15,0},{2,1},{4,3},... | collective-permute-start | bytes 983048 | tf_op jit(solution)/shard_map/ppermute | solution.py:379
  19.3 22.1 %all-to-all-start = ((f32[128,2,128]{2,1,0:T(2,128)}), f32[128,2,128]{2,1,0:T(2,128)S(1)}, u32[]{:S(2)}, u32[]{:S(2)}) async-start(f32[128,2,128]{2,1,0:T(2,128)} %get-tuple-element.35), calls=%async_computation | async-start | bytes 262144 | tf_op jit(solution)/shard_map/all_to_all | solution.py:885
  25.8 4.5 %collective-permute-start.2 = (f32[5,8,128]{2,1,0:T(8,128)S(1)}, f32[5,8,128]{2,1,0:T(8,128)S(1)}, u32[]{:S(2)}, u32[]{:S(2)}) collective-permute-start(f32[5,8,128]{2,1,0:T(8,128)S(1)} %copy-done.15), channel_id=1, source_target_pairs={{0,16},{32,48},{64,80},{96,112},{16,0},{48,32},{80,64},{112,96},{1... | collective-permute-start | bytes 61448 | tf_op jit(solution)/shard_map/ppermute | solution.py:377
  27.0 5.4 %collective-permute-start.3 = (f32[5,8,128]{2,1,0:T(8,128)S(1)}, f32[5,8,128]{2,1,0:T(8,128)S(1)}, u32[]{:S(2)}, u32[]{:S(2)}) collective-permute-start(f32[5,8,128]{2,1,0:T(8,128)S(1)} %copy-done.13), channel_id=1, source_target_pairs={{16,32},{48,64},{80,96},{32,16},{64,48},{96,80},{17,33},{49,65},{8... | collective-permute-start | bytes 61448 | tf_op jit(solution)/shard_map/ppermute | solution.py:378
  30.3 2.1 %copy-start.16 = (f32[5,8,128]{2,1,0:T(8,128)}, f32[5,8,128]{2,1,0:T(8,128)S(1)}, u32[]{:S(2)}) copy-start(f32[5,8,128]{2,1,0:T(8,128)S(1)} %collective-permute-done.2.got_x) | copy-start | bytes 61444
  32.4 0.6 copy-start.17
  32.4 0.7 copy-start.4
  32.4 0.8 copy-start.5
  41.4 8.6 %copy-start.1 = (f32[128,2,128]{2,1,0:T(2,128)}, f32[128,2,128]{2,1,0:T(2,128)S(1)}, u32[]{:S(2)}) copy-start(f32[128,2,128]{2,1,0:T(2,128)S(1)} %all-to-all-done.recv) | copy-start | bytes 393220
  41.4 24.6 %all-to-all-start.1 = ((f32[128,8,128]{2,1,0:T(8,128)}), f32[128,8,128]{2,1,0:T(8,128)S(1)}, u32[]{:S(2)}, u32[]{:S(2)}) async-start(f32[128,8,128]{2,1,0:T(8,128)} %get-tuple-element.51), calls=%async_computation.1 | async-start | bytes 1048576 | tf_op jit(solution)/shard_map/all_to_all | solution.py:885
  53.7 12.3 %collective-permute-start.4 = (f32[5,16,128]{2,1,0:T(8,128)}, f32[5,16,128]{2,1,0:T(8,128)S(1)}, u32[]{:S(2)}, u32[]{:S(2)}) collective-permute-start(f32[5,16,128]{2,1,0:T(8,128)} %get-tuple-element.45), channel_id=1, source_target_pairs={{0,1},{2,3},{4,5},{6,7},{8,9},{10,11},{12,13},{14,15},{1,0},{3,2},... | collective-permute-start | bytes 122888 | tf_op jit(solution)/shard_map/ppermute | solution.py:376
  55.0 10.9 %collective-permute-start.5 = (f32[5,16,128]{2,1,0:T(8,128)}, f32[5,16,128]{2,1,0:T(8,128)S(1)}, u32[]{:S(2)}, u32[]{:S(2)}) collective-permute-start(f32[5,16,128]{2,1,0:T(8,128)} %get-tuple-element.46), channel_id=1, source_target_pairs={{1,2},{3,4},{5,6},{7,8},{9,10},{11,12},{13,14},{15,0},{2,1},{4,3},... | collective-permute-start | bytes 122888 | tf_op jit(solution)/shard_map/ppermute | solution.py:379
  59.7 3.9 %collective-permute-start.6 = (f32[5,8,128]{2,1,0:T(8,128)}, f32[5,8,128]{2,1,0:T(8,128)S(1)}, u32[]{:S(2)}, u32[]{:S(2)}) collective-permute-start(f32[5,8,128]{2,1,0:T(8,128)} %get-tuple-element.47), channel_id=1, source_target_pairs={{0,16},{32,48},{64,80},{96,112},{16,0},{48,32},{80,64},{112,96},{1... | collective-permute-start | bytes 61448 | tf_op jit(solution)/shard_map/ppermute | solution.py:377
  60.7 5.3 %collective-permute-start.7 = (f32[5,8,128]{2,1,0:T(8,128)}, f32[5,8,128]{2,1,0:T(8,128)S(1)}, u32[]{:S(2)}, u32[]{:S(2)}) collective-permute-start(f32[5,8,128]{2,1,0:T(8,128)} %get-tuple-element.48), channel_id=1, source_target_pairs={{16,32},{48,64},{80,96},{32,16},{64,48},{96,80},{17,33},{49,65},{8... | collective-permute-start | bytes 61448 | tf_op jit(solution)/shard_map/ppermute | solution.py:378
  63.7 2.3 %copy-start.10 = (f32[5,8,128]{2,1,0:T(8,128)}, f32[5,8,128]{2,1,0:T(8,128)S(1)}, u32[]{:S(2)}) copy-start(f32[5,8,128]{2,1,0:T(8,128)S(1)} %collective-permute-done.6.got_x) | copy-start | bytes 61444
  66.0 0.6 copy-start.12
  66.0 0.6 copy-start.8
  66.0 0.6 copy-start.9
  66.0 0.8 copy-start
  87.8 9.8 %collective-permute-start.8 = (f32[5,72,128]{2,1,0:T(8,128)}, f32[5,72,128]{2,1,0:T(8,128)S(1)}, u32[]{:S(2)}, u32[]{:S(2)}) collective-permute-start(f32[5,72,128]{2,1,0:T(8,128)} %get-tuple-element.57), channel_id=1, source_target_pairs={{0,1},{2,3},{4,5},{6,7},{8,9},{10,11},{12,13},{14,15},{1,0},{3,2},... | collective-permute-start | bytes 552968 | tf_op jit(solution)/shard_map/ppermute | solution.py:376
  87.9 9.7 %collective-permute-start.9 = (f32[5,72,128]{2,1,0:T(8,128)}, f32[5,72,128]{2,1,0:T(8,128)S(1)}, u32[]{:S(2)}, u32[]{:S(2)}) collective-permute-start(f32[5,72,128]{2,1,0:T(8,128)} %get-tuple-element.58), channel_id=1, source_target_pairs={{1,2},{3,4},{5,6},{7,8},{9,10},{11,12},{13,14},{15,0},{2,1},{4,3},... | collective-permute-start | bytes 552968 | tf_op jit(solution)/shard_map/ppermute | solution.py:379
  88.6 9.0 %collective-permute-start.10 = (f32[5,8,128]{2,1,0:T(8,128)}, f32[5,8,128]{2,1,0:T(8,128)S(1)}, u32[]{:S(2)}, u32[]{:S(2)}) collective-permute-start(f32[5,8,128]{2,1,0:T(8,128)} %get-tuple-element.59), channel_id=1, source_target_pairs={{0,16},{32,48},{64,80},{96,112},{16,0},{48,32},{80,64},{112,96},{1... | collective-permute-start | bytes 61448 | tf_op jit(solution)/shard_map/ppermute | solution.py:377
  90.4 7.2 %collective-permute-start.11 = (f32[5,8,128]{2,1,0:T(8,128)}, f32[5,8,128]{2,1,0:T(8,128)S(1)}, u32[]{:S(2)}, u32[]{:S(2)}) collective-permute-start(f32[5,8,128]{2,1,0:T(8,128)} %get-tuple-element.60), channel_id=1, source_target_pairs={{16,32},{48,64},{80,96},{32,16},{64,48},{96,80},{17,33},{49,65},{8... | collective-permute-start | bytes 61448 | tf_op jit(solution)/shard_map/ppermute | solution.py:378
  97.6 0.6 copy-start.11
  97.6 0.6 copy-start.14
  97.6 0.7 copy-start.6
  97.6 0.8 copy-start.7
